TPU v7x, 128 devices: a whole 4x4x4 slice. The times are simulated.
128 devices in a mesh: ctx: 16 (over x, y), head: 8 (over z, core).
Axes of the slice: x: 4, y: 4, z: 4, core: 2. Of those that a mesh axis runs over, the one named last changes fastest.
Arguments:
- inputs: bfloat16 [8192, 2048], P('ctx'), may hold values from -6 to 6
- query_key_weight: bfloat16 [2, 2048, 2048], P(None, None, 'head'), may hold values from -0.125 to 0.125
- value_gate_weight: bfloat16 [2, 2048, 4096], P(None, None, 'head'), may hold values from -0.125 to 0.125
- decay_beta_weight: bfloat16 [2, 2048, 32], P(None, None, 'head'), may hold values from -0.125 to 0.125
- beta_bias: float32 [32], P('head'), may hold values from -5 to -3
- decay_scale: float32 [32], P('head'), may hold values from 0.0001 to 0.1
- norm_gain: float32 [128], replicated, may hold values from 0.1 to 1.9
- out_weight: bfloat16 [4096, 2048], P('head'), may hold values from -0.09375 to 0.09375
- boundaries: int32 [8192], P('ctx'), may hold values 0 or 1
- grad_mixed: bfloat16 [8192, 2048], P('ctx'), may hold values from -6 to 6
Outputs:
- mixed: bfloat16 [8192, 2048], P('ctx', 'head')
- grad_inputs: bfloat16 [8192, 2048], P('ctx', 'head')
- grad_query_key: float32 [2, 2048, 2048], P(None, 'ctx', 'head')
- grad_value_gate: float32 [2, 2048, 4096], P(None, 'ctx', 'head')
- grad_decay_beta: float32 [2, 2048, 32], P(None, 'ctx', 'head')
- grad_out_weight: float32 [4096, 2048], P('head', 'ctx')
All inputs are finite; a program needn't handle non-finite values. No bound on the sum of `boundaries` on one device may be relied on, other than what follows from the above.
Results may differ from a plain program's by a relative error of at most 0.02.
Values may be sent and summed in bfloat16 or wider, within the bound.
A program may use at most 192 MiB of HBM per device.

v0:
```python
import jax
import jax.numpy as jnp
from jax import lax
from jax.sharding import PartitionSpec as P

DK = 128
DV = 128
SPAN = 64


EPS = 1e-06
PRECISE_MODE = lax.Precision.HIGHEST


def shifted(block, axis, distance):
    devices = range(lax.axis_size(axis))
    route = [(i - distance, i) for i in devices if i - distance in devices]
    return lax.ppermute(block, axis, route)


def head_inputs(proj_query_key, proj_value_gate, proj_decay_beta, beta_bias, decay_scale):
    tok_count = proj_query_key.shape[1]
    key_heads = proj_query_key.shape[2] // DK
    value_heads = proj_value_gate.shape[2] // DV
    repeat_count = value_heads // key_heads
    query_rows = proj_query_key[0].reshape(tok_count, key_heads, DK)
    key_rows = proj_query_key[1].reshape(tok_count, key_heads, DK)
    query_rows = query_rows * lax.rsqrt(
        jnp.sum(query_rows * query_rows, axis=-1, keepdims=True) + EPS
    )
    key_rows = key_rows * lax.rsqrt(jnp.sum(key_rows * key_rows, axis=-1, keepdims=True) + EPS)
    query_rows = jnp.repeat(query_rows, repeat_count, axis=1) * DK ** (-0.5)
    key_rows = jnp.repeat(key_rows, repeat_count, axis=1)
    value_rows = proj_value_gate[0].reshape(tok_count, value_heads, DV)
    gate_rows = proj_value_gate[1].reshape(tok_count, value_heads, DV)
    beta_rows = jax.nn.sigmoid(proj_decay_beta[1] + beta_bias)
    log_decay = -decay_scale * jax.nn.softplus(proj_decay_beta[0])
    return (query_rows, key_rows, value_rows, gate_rows, beta_rows, log_decay)


def to_spans(array_in, spans):
    head_count = array_in.shape[1]
    shaped = array_in.reshape(spans, SPAN, head_count, -1)
    return jnp.transpose(shaped, (2, 0, 1, 3))


def span_terms(query_rows, key_rows, value_rows, beta_rows, log_decay, resets):
    spans = beta_rows.shape[0] // SPAN
    query_blocks = to_spans(query_rows, spans)
    key_blocks = to_spans(key_rows, spans)
    value_blocks = to_spans(value_rows, spans)
    beta_blocks = to_spans(beta_rows[:, :, None], spans)[..., 0]
    cumulative = jnp.cumsum(to_spans(log_decay[:, :, None], spans)[..., 0], axis=-1)
    doc_index = jnp.cumsum(resets.reshape(spans, SPAN), axis=-1)[None]
    positions = jnp.arange(SPAN)
    lower_incl = positions[:, None] >= positions[None, :]
    lower_strict = (positions[:, None] > positions[None, :]).astype(jnp.float32)
    same_doc = (doc_index[..., :, None] == doc_index[..., None, :]) & lower_incl
    log_gap = jnp.minimum(cumulative[..., :, None] - cumulative[..., None, :], 0.0)
    pair_decay = jnp.where(same_doc, jnp.exp(log_gap), 0.0)
    start_keep = jnp.where(doc_index == 0, jnp.exp(cumulative), 0.0)
    end_keep = jnp.where(
        doc_index == doc_index[..., -1:],
        jnp.exp(jnp.minimum(cumulative[..., -1:] - cumulative, 0.0)),
        0.0,
    )
    total_keep = start_keep[..., -1]
    key_gram = jnp.einsum("hnck,hnjk->hncj", key_blocks, key_blocks, precision=PRECISE_MODE)
    system = (
        jnp.eye(SPAN, dtype=jnp.float32)
        + beta_blocks[..., :, None] * pair_decay * lower_strict * key_gram
    )
    right_side = jnp.concatenate(
        [beta_blocks[..., None] * value_blocks, (beta_blocks * start_keep)[..., None] * key_blocks],
        axis=-1,
    )
    solved = jax.scipy.linalg.solve_triangular(system, right_side, lower=True, unit_diagonal=True)
    pseudo_base = solved[..., :DV]
    key_weights = solved[..., DV:]
    end_keys = end_keep[..., None] * key_blocks
    scores = pair_decay * jnp.einsum(
        "hnck,hnjk->hncj", query_blocks, key_blocks, precision=PRECISE_MODE
    )
    start_queries = start_keep[..., None] * query_blocks
    return (start_queries, scores, pseudo_base, key_weights, end_keys, total_keep)


def run_spans(terms, state_in):

    def advance(carried_state, block_terms):
        (
            block_query_rows,
            block_score_matrix,
            block_starting_offset,
            block_weight_matrix,
            block_final_keys,
            block_retained_decay,
        ) = block_terms
        surrogate_values = block_starting_offset - jnp.einsum(
            "xuy,xyf->xuf", block_weight_matrix, carried_state, precision=PRECISE_MODE
        )
        produced_output = jnp.einsum(
            "xuy,xyf->xuf", block_query_rows, carried_state, precision=PRECISE_MODE
        ) + jnp.einsum("adx,axo->ado", block_score_matrix, surrogate_values, precision=PRECISE_MODE)
        updated_state = block_retained_decay[:, None, None] * carried_state + jnp.einsum(
            "gzy,gzq->gyq", block_final_keys, surrogate_values, precision=PRECISE_MODE
        )
        return (updated_state, produced_output)

    moved = tuple([jnp.moveaxis(member, 1, 0) for member in terms])
    final, produced_output = lax.scan(advance, state_in, moved)
    spans, head_count = (produced_output.shape[0], produced_output.shape[1])
    produced_output = jnp.transpose(produced_output, (0, 2, 1, 3)).reshape(
        spans * SPAN, head_count, DV
    )
    return (produced_output, final)


def transition_totals(terms):
    start_queries, scores, pseudo_base, key_weights, end_keys, total_keep = terms
    head_count = total_keep.shape[0]
    identity = jnp.eye(DK, dtype=jnp.float32)
    maps_a = total_keep[..., None, None] * identity - jnp.einsum(
        "hnck,hncj->hnkj", end_keys, key_weights, precision=PRECISE_MODE
    )
    maps_b = jnp.einsum("hnck,hncv->hnkv", end_keys, pseudo_base, precision=PRECISE_MODE)

    def compose(carried_state, block_maps):
        first_span, second_span = block_maps
        return (
            (
                jnp.einsum("hkj,hjm->hkm", first_span, carried_state[0], precision=PRECISE_MODE),
                jnp.einsum("azf,afg->azg", first_span, carried_state[1], precision=PRECISE_MODE)
                + second_span,
            ),
            None,
        )

    start = (
        jnp.broadcast_to(identity, (head_count, DK, DK)),
        jnp.zeros((head_count, DK, DV), jnp.float32),
    )
    totals, unused = lax.scan(
        compose, start, (jnp.moveaxis(maps_a, 1, 0), jnp.moveaxis(maps_b, 1, 0))
    )
    return totals


def mixer(
    proj_query_key,
    proj_value_gate,
    proj_decay_beta,
    beta_bias,
    decay_scale,
    norm_gain,
    resets,
    state_in,
):
    query_rows, key_rows, value_rows, gate_rows, beta_rows, log_decay = head_inputs(
        proj_query_key, proj_value_gate, proj_decay_beta, beta_bias, decay_scale
    )
    terms = span_terms(query_rows, key_rows, value_rows, beta_rows, log_decay, resets)
    produced_output, final = run_spans(terms, state_in)
    scale_rows = lax.rsqrt(
        jnp.mean(produced_output * produced_output, axis=-1, keepdims=True) + EPS
    )
    normed = produced_output * scale_rows * norm_gain * jax.nn.silu(gate_rows)
    return (normed.reshape(normed.shape[0], -1), final)


def mixer_totals(proj_query_key, proj_value_gate, proj_decay_beta, beta_bias, decay_scale, resets):
    query_rows, key_rows, value_rows, gate_rows, beta_rows, log_decay = head_inputs(
        proj_query_key, proj_value_gate, proj_decay_beta, beta_bias, decay_scale
    )
    return transition_totals(
        span_terms(query_rows, key_rows, value_rows, beta_rows, log_decay, resets)
    )


def body(
    inputs,
    query_key_weight,
    value_gate_weight,
    decay_beta_weight,
    beta_bias,
    decay_scale,
    norm_gain,
    out_weight,
    boundaries,
    grad_mixed,
):
    proj_query_key = jnp.einsum(
        "td,sdf->stf", inputs, query_key_weight, preferred_element_type=jnp.float32
    )
    proj_value_gate = jnp.einsum(
        "td,sdf->stf", inputs, value_gate_weight, preferred_element_type=jnp.float32
    )
    proj_decay_beta = jnp.einsum(
        "td,sdf->stf", inputs, decay_beta_weight, preferred_element_type=jnp.float32
    )
    head_count = beta_bias.shape[0]
    first_total, second_total = mixer_totals(
        proj_query_key, proj_value_gate, proj_decay_beta, beta_bias, decay_scale, boundaries
    )
    zero_state = jnp.zeros((head_count, DK, DV), jnp.float32)

    def hand_forward(position, incoming_state):
        outgoing_state = (
            jnp.einsum("azf,afg->azg", first_total, incoming_state, precision=PRECISE_MODE)
            + second_total
        )
        return shifted(outgoing_state.astype(jnp.bfloat16), "ctx", 1).astype(outgoing_state.dtype)

    state_in = lax.fori_loop(0, lax.axis_size("ctx") - 1, hand_forward, zero_state)

    def local_mixer(part_query_key, part_value_gate, part_decay_beta, carried_in):
        return mixer(
            part_query_key,
            part_value_gate,
            part_decay_beta,
            beta_bias,
            decay_scale,
            norm_gain,
            boundaries,
            carried_in,
        )

    (normed, state_out), pullback = jax.vjp(
        local_mixer, proj_query_key, proj_value_gate, proj_decay_beta, state_in
    )
    hidden = normed.astype(jnp.bfloat16)
    partial_out = jnp.dot(hidden, out_weight, preferred_element_type=jnp.float32)
    mixed = lax.psum_scatter(
        partial_out.astype(jnp.bfloat16), "head", scatter_dimension=1, tiled=True
    )
    delta_hidden = jnp.einsum(
        "td,fd->tf", grad_mixed, out_weight, preferred_element_type=jnp.float32
    )
    own_pull = pullback((delta_hidden, jnp.zeros_like(state_out)))
    local_state = own_pull[3]

    def hand_backward(position, incoming_state):
        outgoing_state = (
            jnp.einsum("lfg,lfb->lgb", first_total, incoming_state, precision=PRECISE_MODE)
            + local_state
        )
        return shifted(outgoing_state.astype(jnp.bfloat16), "ctx", -1).astype(outgoing_state.dtype)

    grad_state_out = lax.fori_loop(0, lax.axis_size("ctx") - 1, hand_backward, zero_state)
    far_pull = pullback((jnp.zeros_like(delta_hidden), grad_state_out))
    delta_query_key = (own_pull[0] + far_pull[0]).astype(jnp.bfloat16)
    delta_value_gate = (own_pull[1] + far_pull[1]).astype(jnp.bfloat16)
    delta_decay_beta = (own_pull[2] + far_pull[2]).astype(jnp.bfloat16)
    grad_rows = jnp.einsum(
        "stf,sdf->td", delta_query_key, query_key_weight, preferred_element_type=jnp.float32
    )
    grad_rows = grad_rows + jnp.einsum(
        "stf,sdf->td", delta_value_gate, value_gate_weight, preferred_element_type=jnp.float32
    )
    grad_rows = grad_rows + jnp.einsum(
        "stf,sdf->td", delta_decay_beta, decay_beta_weight, preferred_element_type=jnp.float32
    )
    grad_inputs = lax.psum_scatter(
        grad_rows.astype(jnp.bfloat16), "head", scatter_dimension=1, tiled=True
    )
    term_query_key = jnp.einsum(
        "td,stf->sdf", inputs, delta_query_key, preferred_element_type=jnp.float32
    )
    term_value_gate = jnp.einsum(
        "td,stf->sdf", inputs, delta_value_gate, preferred_element_type=jnp.float32
    )
    term_decay_beta = jnp.einsum(
        "td,stf->sdf", inputs, delta_decay_beta, preferred_element_type=jnp.float32
    )
    term_out = jnp.einsum("tf,td->fd", hidden, grad_mixed, preferred_element_type=jnp.float32)
    grad_query_key, grad_value_gate, grad_decay_beta, grad_out_weight = (
        lax.psum_scatter(
            term_query_key.astype(jnp.bfloat16), "ctx", scatter_dimension=1, tiled=True
        ).astype(jnp.float32),
        lax.psum_scatter(
            term_value_gate.astype(jnp.bfloat16), "ctx", scatter_dimension=1, tiled=True
        ).astype(jnp.float32),
        lax.psum_scatter(
            term_decay_beta.astype(jnp.bfloat16), "ctx", scatter_dimension=1, tiled=True
        ).astype(jnp.float32),
        lax.psum_scatter(
            term_out.astype(jnp.bfloat16), "ctx", scatter_dimension=1, tiled=True
        ).astype(jnp.float32),
    )
    return (mixed, grad_inputs, grad_query_key, grad_value_gate, grad_decay_beta, grad_out_weight)


def solution(mesh):
    in_specs = (
        P("ctx", None),
        P(None, None, "head"),
        P(None, None, "head"),
        P(None, None, "head"),
        P("head"),
        P("head"),
        P(),
        P("head", None),
        P("ctx"),
        P("ctx", None),
    )
    out_specs = (
        P("ctx", "head"),
        P("ctx", "head"),
        P(None, "ctx", "head"),
        P(None, "ctx", "head"),
        P(None, "ctx", "head"),
        P("head", "ctx"),
    )
    return jax.shard_map(body, mesh=mesh, in_specs=in_specs, out_specs=out_specs, check_vma=False)
```

profile of v0, /device:TPU:0, one launch (start us, length us, event | category | flops | bytes accessed | tf_op | source)
XLA Modules:
  0.0 1513.5 jit_solution(16937335305665924239)
XLA Ops:
  29.1 158.7 %custom-call.13 = f32[4,8,1,64,64]{3,4,2,1,0:T(8,128)} custom-call(f32[4,8,1,64,64]{4,3,2,1,0:T(8,128)} %fusion.169), custom_call_target="InvertDiagBlocksLowerTriangular" | custom-call | tf_op jit(solution)/shard_map/jit(_solve_triangular)/vmap(vmap())/triangular_solve/custom-call.1 | solution.py:77
  224.5 49.0 %while.108 = (s32[]{:T(128)}, f32[4,128,128]{2,1,0:T(8,128)}, f32[4,128,128]{2,1,0:T(8,128)}, f32[8,4,128,128]{3,2,0,1:T(8,128)}, f32[8,4,128,128]{3,2,0,1:T(8,128)}, /*index=5*/s32[]{:T(128)}, s32[]{:T(128)}) while((s32[]{:T(128)}, f32[4,128,128]{2,1,0:T(8,128)}, f32[4,128,128]{2,1,0:T(8,128)}, f32[8,4,128,128]{3,2,0,1:T(8,128)}, ...), condition=%wide.region_4.6_spmd.clone, body=%wide.region_3.5_spmd.clone.sunk | while | flops 201457664 | bytes 2885207 | solution.py:143
  286.7 172.4 %while.109 = (s32[]{:T(128)}, f32[4,128,128]{2,1,0:T(8,128)}, f32[4,128,128]{2,1,0:T(8,128)}, f32[4,128,128]{2,1,0:T(8,128)}, s32[]{:T(128)}, /*index=5*/s32[]{:T(128)}) while((s32[]{:T(128)}, f32[4,128,128]{2,1,0:T(8,128)}, f32[4,128,128]{2,1,0:T(8,128)}, f32[4,128,128]{2,1,0:T(8,128)}, s32[]{:T(128)}, /*index=5*/s32[]{:T(128)}) %tuple.240), condition=%wide.region_6.8_spmd.clone, body=%wide.region_5.7_spmd.clone.sunk | while | flops 100925440 | bytes 1835127 | solution.py:214
  398.2 7.5 collective-permute-start
  411.6 7.7 collective-permute-start
  436.1 7.3 collective-permute-start
  448.4 7.3 collective-permute-start
  460.2 90.2 %while.106 = (s32[]{:T(128)}, f32[4,128,128]{2,1,0:T(8,128)}, f32[8,4,64,128]{3,1,2,0:T(4,128)}, f32[8,4,128,128]{3,2,1,0:T(8,128)}, f32[8,4,64,128]{3,2,1,0:T(8...) while((s32[]{:T(128)}, f32[4,128,128]{2,1,0:T(8,128)}, ...), condition=%wide.region_9.11_spmd, body=%wide.region_8.10_spmd.sunk | while | flops 176357376 | bytes 3413169 | solution.py:111
  584.3 165.7 %while.110 = (s32[]{:T(128)}, f32[4,128,128]{2,1,0:T(8,128)}, f32[8,4,64,128]{3,2,0,1:T(8,128)}, f32[8,4,64,64]{3,2,0,1:T(8,128)}, f32[8,4,64,128]{3,2,1,0:T(8,1...) while((s32[]{:T(128)}, f32[4,128,128]{2,1,0:T(8,128)}, ...), condition=%wide.region_15.17_spmd.clone, body=%wide.region_13.16_spmd.clone.sunk | while | flops 353009664 | bytes 6560092 | solution.py:111
  758.7 176.0 %while.111 = (s32[]{:T(128)}, f32[4,128,128]{2,1,0:T(8,128)S(1)}, f32[4,128,128]{1,2,0:T(8,128)}, f32[4,128,128]{2,1,0:T(8,128)}, s32[]{:T(128)}, /*index=5*/s32[]{:T(128)}) while((s32[]{:T(128)}, f32[4,128,128]{2,1,0:T(8,128)S(1)}, f32[4,128,128]{1,2,0:T(8,128)}, f32[4,128,128]{2,1,0:T(8,128)}, s32[]{:T(128)}, ...), condition=%wide.region_21.24_spmd.clone, body=%wide.region_20.23_spmd.clone.sunk | while | flops 100925440 | bytes 1835127 | solution.py:249
  761.4 8.3 collective-permute-done.1
  773.4 8.3 collective-permute-done.1
  785.4 8.3 collective-permute-done.1
  797.4 9.0 collective-permute-done.1
  810.0 9.1 collective-permute-done.1
  822.8 8.5 collective-permute-done.1
  834.9 7.8 collective-permute-done.1
  846.4 7.2 collective-permute-done.1
  857.3 7.8 collective-permute-done.1
  868.8 7.8 collective-permute-done.1
  880.2 7.8 collective-permute-done.1
  891.7 7.8 collective-permute-done.1
  903.1 7.8 collective-permute-done.1
  914.6 7.8 collective-permute-done.1
  926.0 7.8 collective-permute-done.1
  940.4 138.3 %while.107 = (s32[]{:T(128)}, f32[4,128,128]{2,1,0:T(8,128)S(1)}, f32[8,4,64,128]{3,2,0,1:T(8,128)}, f32[8,4,64,64]{3,2,0,1:T(8,128)}, f32[8,4,64,128]{3,2,1,0:T...) while((s32[]{:T(128)}, f32[4,128,128]{2,1,0:T(8,128)S(1)}, ...), condition=%wide.region_25.28_spmd, body=%wide.region_23.27_spmd.sunk | while | flops 352747520 | bytes 5510453 | solution.py:111
  1215.0 11.2 copy.363
  1247.1 30.3 %reduce-scatter.19.cloned.1.call-done = bf16[128,512]{1,0:T(8,128)(2,1)} async-done(((bf16[2048,512]{1,0:T(8,128)(2,1)}), bf16[128,512]{1,0:T(8,128)(2,1)}) %reduce-scatter.19.cloned.1.call-update) | async-done | bytes 131088
  1279.3 74.9 %reduce-scatter.25.cloned.1.call-done = bf16[128,512]{1,0:T(8,128)(2,1)} async-done(((bf16[2048,512]{1,0:T(8,128)(2,1)}), bf16[128,512]{1,0:T(8,128)(2,1)}) %reduce-scatter.25.cloned.1.call-update) | async-done | bytes 131088
  1356.0 78.7 %reduce-scatter.21.cloned.1.call-done = bf16[128,1024]{1,0:T(8,128)(2,1)} async-done(((bf16[2048,1024]{1,0:T(8,128)(2,1)}), bf16[128,1024]{1,0:T(8,128)(2,1)}) %reduce-scatter.21.cloned.1.call-update) | async-done | bytes 262160
  1437.0 33.8 %reduce-scatter.17.cloned.1.call-done = bf16[512,256]{1,0:T(8,128)(2,1)} async-done(((bf16[512,2048]{1,0:T(8,128)(2,1)}), bf16[512,256]{1,0:T(8,128)(2,1)}) %reduce-scatter.17.cloned.1.call-update) | async-done | bytes 262160 | tf_op jit(solution)/shard_map/reduce_scatter | solution.py:263
  1470.8 35.4 %reduce-scatter.15.cloned.1.call-done = bf16[512,256]{1,0:T(8,128)(2,1)} async-done(((bf16[512,2048]{1,0:T(8,128)(2,1)}), bf16[512,256]{1,0:T(8,128)(2,1)}) %reduce-scatter.15.cloned.1.call-update) | async-done | bytes 262160 | tf_op jit(solution)/shard_map/reduce_scatter | solution.py:233
  (814 shorter events, 922.0 us)
Async XLA Ops:
  7.2 1238.4 %reduce-scatter.23.cloned.1.call-start = ((), (), s32[]{:S(2)}) async-start(), calls=%async_computation.10 | async-start | bytes 557056
  297.6 7.0 collective-permute-start
  338.0 7.5 collective-permute-start
  348.7 9.1 collective-permute-start
  360.9 9.1 collective-permute-start
  373.1 9.1 collective-permute-start
  385.3 9.7 collective-permute-start
  398.2 10.3 collective-permute-start
  411.6 9.5 collective-permute-start
  424.2 8.8 collective-permute-start
  436.1 9.1 collective-permute-start
  448.4 9.1 collective-permute-start
  760.1 9.6 collective-permute-start.1
  772.1 9.6 collective-permute-start.1
  784.1 9.6 collective-permute-start.1
  796.1 10.3 collective-permute-start.1
  808.7 10.4 collective-permute-start.1
  821.5 9.8 collective-permute-start.1
  833.6 9.1 collective-permute-start.1
  845.1 8.5 collective-permute-start.1
  856.0 9.1 collective-permute-start.1
  867.5 9.1 collective-permute-start.1
  878.9 9.1 collective-permute-start.1
  890.4 9.1 collective-permute-start.1
  901.8 9.1 collective-permute-start.1
  913.3 9.1 collective-permute-start.1
  924.7 9.1 collective-permute-start.1
  1118.1 159.4 %reduce-scatter.19.cloned.1.call-start = ((), (), s32[]{:S(2)}) async-start(), calls=%async_computation.8 | async-start | bytes 2228224
  1176.8 177.5 %reduce-scatter.25.cloned.1.call-start = ((), (), s32[]{:S(2)}) async-start(), calls=%async_computation.11 | async-start | bytes 2228224
  1191.0 243.7 %reduce-scatter.21.cloned.1.call-start = ((), (), s32[]{:S(2)}) async-start(), calls=%async_computation.9 | async-start | bytes 4456448
  1231.5 239.3 %reduce-scatter.17.cloned.1.call-start = ((), (), s32[]{:S(2)}) async-start(), calls=%async_computation.7 | async-start | bytes 2359296 | tf_op jit(solution)/shard_map/reduce_scatter | solution.py:263
  1240.3 265.9 %reduce-scatter.15.cloned.1.call-start = ((), (), s32[]{:S(2)}) async-start(), calls=%async_computation.6 | async-start | bytes 2359296 | tf_op jit(solution)/shard_map/reduce_scatter | solution.py:233
  (118 other events, 1071.4 us)
Sparse Core Ops, SparseCore 0:
  1118.2 81.9 reduce-scatter.22
  1203.8 73.5 reduce-scatter.18
  1280.7 73.5 reduce-scatter.24
  1357.8 76.8 reduce-scatter.20
  1437.5 33.2 reduce-scatter.16
  1473.6 32.5 reduce-scatter.14
where the time goes:
time: 1530 us; the launch traced here: 1510 us
  matrix products  477 us (31%)
  waiting for transfers between devices  404 us (26%)
  other arithmetic  276 us (18%)
  local copies, waits for them, and re-layouts  223 us (15%)
  starting transfers between devices  115 us (8%)
  between operations  15.9 us (1%)
    unnamed x10, waiting for transfers between devices  184 us
    another operation x5, other arithmetic, span_terms(): jax.scipy.linalg.solve_triangular(system, right_side, lower=True, unit_di...  163 us
    ppermute x30, waiting for transfers between devices, shifted(): return lax.ppermute(block, axis, route)  151 us
    ppermute x30, starting transfers between devices, shifted(): return lax.ppermute(block, axis, route)  115 us
    dot_general x40, matrix products, advance(): jnp.einsum('gzy,gzq->gyq', block_final_keys, surrogate_values, precision=...  85.2 us
    dot_general x40, matrix products, advance(): jnp.einsum('xuy,xyf->xuf', block_weight_matrix, carried_state, precision=...  81.6 us
    dot_general x40, matrix products, advance(): jnp.einsum('xuy,xyf->xuf', block_query_rows, carried_state, precision=PRE...  71.2 us
    dot_general x40, matrix products, advance(): jnp.einsum('adx,axo->ado', block_score_matrix, surrogate_values, precisio...  63.4 us
  transfers between devices with their start and end apart: 36, of which 35 were waited for; matrix products, arithmetic and copies ran while one was open for 9% of the time, Pallas kernels for 0%

commit v1 on v0

v1 whole, which is shorter than its diff:
```python
import functools

import jax
import jax.numpy as jnp
from jax import lax
from jax.experimental import pallas as pl
from jax.experimental.pallas import tpu as pltpu
from jax.sharding import PartitionSpec as P

DK = 128
DV = 128
BLOCK = 128
EPS = 1e-06
LANES = 128
SIDE = 4
F32 = jnp.float32
BF16 = jnp.bfloat16
MESH = pl.DeviceIdType.MESH

NN = ((1,), (0,))
NT = ((1,), (1,))
TN = ((0,), (0,))


def dot(a, b, dims):
    return lax.dot_general(a, b, (dims, ((), ())), preferred_element_type=F32)


def split(a):
    high = a.astype(BF16)
    return high, (a - high.astype(F32)).astype(BF16)


def mm3(a, b, dims=NN):
    a_high, a_low = split(a)
    b_high, b_low = split(b)
    return dot(a_high, b_high, dims) + (dot(a_high, b_low, dims) + dot(a_low, b_high, dims))


def mm1(a, b, dims=NN):
    return dot(a.astype(BF16), b.astype(BF16), dims)


def exact(a, b, dims=NN):
    return lax.dot_general(
        a, b, (dims, ((), ())), precision=lax.Precision.HIGHEST, preferred_element_type=F32
    )


def rows_cols():
    rows = lax.broadcasted_iota(jnp.int32, (BLOCK, BLOCK), 0)
    cols = lax.broadcasted_iota(jnp.int32, (BLOCK, BLOCK), 1)
    return rows, cols


def softplus(x):
    return jnp.maximum(x, 0.0) + jnp.log1p(jnp.exp(-jnp.abs(x)))


def unit(raw):
    scale = lax.rsqrt(jnp.sum(raw * raw, axis=-1, keepdims=True) + EPS)
    return raw * scale, scale


def invert(systems):
    rows, cols = rows_cols()
    eye = (rows == cols).astype(F32)
    first = ((rows >> 1) == (cols >> 1)) & (rows > cols)
    inverses = [eye - jnp.where(first, n, 0.0) for n in systems]
    for level in range(1, 7):
        pick = ((rows >> (level + 1)) == (cols >> (level + 1))) & (
            (rows >> level) > (cols >> level)
        )
        halves = [mm3(jnp.where(pick, n, 0.0), x) for n, x in zip(systems, inverses)]
        inverses = [x - mm3(x, h) for x, h in zip(inverses, halves)]
    return inverses


def gates(side, reset, scale_row, bias_row, heads):
    rows, cols = rows_cols()
    beta = jax.nn.sigmoid(side + bias_row)
    decay = -scale_row * softplus(side)
    lower = (rows >= cols).astype(F32)
    summed = exact(lower, jnp.where(cols == 2 * heads, reset, decay))
    flipped = summed.T
    doc = summed[:, 2 * heads : 2 * heads + 1]
    doc_row = flipped[2 * heads : 2 * heads + 1, :]
    same = (doc == doc_row) & (rows >= cols)
    start = jnp.where(doc == 0.0, jnp.exp(summed), 0.0)
    last = summed[BLOCK - 1 : BLOCK, :]
    end = jnp.where(
        doc == doc[BLOCK - 1 : BLOCK, :], jnp.exp(jnp.minimum(last - summed, 0.0)), 0.0
    )
    return beta, summed, flipped, same, start, end


def pair_decay(summed, flipped, same, head):
    gap = jnp.minimum(summed[:, head : head + 1] - flipped[head : head + 1, :], 0.0)
    return jnp.where(same, jnp.exp(gap), 0.0)


def terms_kernel(
    key_heads,
    repeat,
    proj_ref,
    reset_ref,
    scale_ref,
    bias_ref,
    x_ref,
    u_ref,
    w_ref,
    p_ref,
    e_ref,
    o_ref,
    a_ref,
    b_ref,
    prefix_ref,
    a_total,
    b_total,
):
    step = pl.program_id(0)
    heads = key_heads * repeat
    rows, cols = rows_cols()
    eye = (rows == cols).astype(F32)

    @pl.when(step == 0)
    def _():
        for h in range(heads):
            a_total[h] = eye
            b_total[h] = jnp.zeros_like(eye)

    value_at = 2 * key_heads * DK
    side_at = value_at + 2 * heads * DV
    side = proj_ref[:, side_at : side_at + LANES]
    beta, summed, flipped, same, start, end = gates(
        side, reset_ref[...], scale_ref[...], bias_ref[...], heads
    )
    systems, scores, queries, keys = [], [], [], []
    for kh in range(key_heads):
        q, _ = unit(proj_ref[:, kh * DK : (kh + 1) * DK])
        q = q * DK ** (-0.5)
        k, _ = unit(proj_ref[:, (key_heads + kh) * DK : (key_heads + kh + 1) * DK])
        gram = mm3(k, k, NT)
        cross = mm3(q, k, NT)
        for h in range(kh * repeat, (kh + 1) * repeat):
            decay = pair_decay(summed, flipped, same, h)
            strength = beta[:, heads + h : heads + h + 1]
            systems.append(jnp.where(rows > cols, strength * decay * gram, 0.0))
            scores.append(decay * cross)
            queries.append(q)
            keys.append(k)
    inverses = invert(systems)
    for h in range(heads):
        strength = beta[:, heads + h : heads + h + 1]
        begin = start[:, h : h + 1]
        v = proj_ref[:, value_at + h * DV : value_at + (h + 1) * DV]
        right = jnp.concatenate([strength * v, (strength * begin) * keys[h]], axis=1)
        solved = mm3(inverses[h], right)
        end_keys = end[:, h : h + 1] * keys[h]
        state_map = mm3(end_keys, solved, TN)
        local = mm3(scores[h], solved)
        total = begin[BLOCK - 1 : BLOCK, :]
        a = total * eye - state_map[:, DV:]
        b = state_map[:, :DV]
        x_ref[0, h] = inverses[h]
        u_ref[0, h] = solved[:, :DV]
        w_ref[0, h] = solved[:, DV:]
        p_ref[0, h] = scores[h]
        e_ref[0, h] = begin * queries[h] - local[:, DV:]
        o_ref[0, h] = local[:, :DV]
        a_ref[0, h] = a
        b_ref[0, h] = b
        prefix_ref[0, h] = a_total[h]
        both = mm3(a, jnp.concatenate([a_total[h], b_total[h]], axis=1))
        a_total[h] = both[:, :DK]
        b_total[h] = both[:, DK:] + b


def forward_kernel(
    heads,
    gate_ref,
    up_ref,
    gain_ref,
    state_ref,
    u_ref,
    w_ref,
    e_ref,
    o_ref,
    a_ref,
    b_ref,
    prefix_ref,
    hidden_ref,
    gate_grad_ref,
    grad_ref,
    value_ref,
    before_ref,
    total_ref,
    state,
):
    step = pl.program_id(0)

    @pl.when(step == 0)
    def _():
        state[...] = state_ref[...]
        total_ref[...] = jnp.zeros_like(total_ref)

    gain = gain_ref[...]
    for h in range(heads):
        s = state[h]
        before_ref[0, h] = s
        stacked = mm3(jnp.concatenate([a_ref[0, h], e_ref[0, h], w_ref[0, h]], axis=0), s)
        state[h] = stacked[:DK] + b_ref[0, h]
        out = stacked[DK : DK + BLOCK] + o_ref[0, h]
        value_ref[0, h] = u_ref[0, h] - stacked[DK + BLOCK :]
        scale = lax.rsqrt(jnp.mean(out * out, axis=-1, keepdims=True) + EPS)
        normed = out * scale
        g = gate_ref[:, h * DV : (h + 1) * DV]
        up = up_ref[:, h * DV : (h + 1) * DV]
        opened = jax.nn.sigmoid(g)
        swish = g * opened
        hidden_ref[:, h * DV : (h + 1) * DV] = (normed * gain * swish).astype(BF16)
        gate_grad_ref[:, h * DV : (h + 1) * DV] = (
            up * normed * gain * (opened * (1.0 + g * (1.0 - opened)))
        ).astype(BF16)
        d_normed = up * gain * swish
        d_out = scale * (
            d_normed - normed * jnp.mean(d_normed * normed, axis=-1, keepdims=True)
        )
        grad_ref[0, h] = d_out
        local = mm3(e_ref[0, h], d_out, TN)
        total_ref[h] += mm3(prefix_ref[0, h], local, TN)


def backward_kernel(
    key_heads,
    repeat,
    proj_ref,
    reset_ref,
    scale_ref,
    bias_ref,
    grad_state_ref,
    x_ref,
    p_ref,
    value_ref,
    before_ref,
    grad_ref,
    gate_grad_ref,
    delta_ref,
    grad_state,
):
    step = pl.program_id(0)
    heads = key_heads * repeat
    rows, cols = rows_cols()

    @pl.when(step == 0)
    def _():
        grad_state[...] = grad_state_ref[...]

    value_at = 2 * key_heads * DK
    side_at = value_at + 2 * heads * DV
    side = proj_ref[:, side_at : side_at + LANES]
    beta, summed, flipped, same, start, end = gates(
        side, reset_ref[...], scale_ref[...], bias_ref[...], heads
    )
    d_summed = jnp.zeros((BLOCK, LANES), F32)
    d_strength = jnp.zeros((BLOCK, LANES), F32)
    at_last = rows[:, :1] == BLOCK - 1
    for kh in range(key_heads):
        q_unit, q_scale = unit(proj_ref[:, kh * DK : (kh + 1) * DK])
        q = q_unit * DK ** (-0.5)
        k, k_scale = unit(proj_ref[:, (key_heads + kh) * DK : (key_heads + kh + 1) * DK])
        dq_sum = jnp.zeros((BLOCK, DK), F32)
        dk_sum = jnp.zeros((BLOCK, DK), F32)
        for h in range(kh * repeat, (kh + 1) * repeat):
            decay = pair_decay(summed, flipped, same, h)
            strength = beta[:, heads + h : heads + h + 1]
            begin = start[:, h : h + 1]
            finish = end[:, h : h + 1]
            v = proj_ref[:, value_at + h * DV : value_at + (h + 1) * DV]
            d_out = grad_ref[0, h]
            value = value_ref[0, h]
            s = before_ref[0, h]
            ds = grad_state[h]
            total = begin[BLOCK - 1 : BLOCK, :]
            d_value = mm3(p_ref[0, h], d_out, TN) + finish * mm3(k, ds)
            d_right = mm3(x_ref[0, h], d_value, TN)
            both = jnp.concatenate([d_out, -d_right], axis=0)
            pairs = mm3(both, value, NT)
            d_scores = pairs[:BLOCK] * decay
            d_system = jnp.where(rows > cols, pairs[BLOCK:] * decay, 0.0)
            starts = mm3(both, s, NT)
            d_end = mm3(value, ds, NT)
            right = mm3(jnp.concatenate([d_scores, d_system], axis=0), k)
            dq = right[:BLOCK] + begin * starts[:BLOCK]
            row_part = right[BLOCK:] + begin * starts[BLOCK:]
            ends = finish * d_end
            dk_col = (
                mm3(
                    jnp.concatenate([d_scores, strength * d_system], axis=0),
                    jnp.concatenate([q, k], axis=0),
                    TN,
                )
                + ends
            )
            dk_row = strength * row_part
            grad_state[h] = total * ds + mm3(
                jnp.concatenate([begin * q, (strength * begin) * k], axis=0), both, TN
            )
            dq_sum += dq
            dk_sum += dk_row + dk_col
            d_beta = jnp.sum(k * row_part + v * d_right, axis=-1, keepdims=True)
            d_cum = jnp.sum(q * dq + k * (dk_row - dk_col), axis=-1, keepdims=True)
            d_last = jnp.sum(k * ends) + jnp.sum(s * ds * total)
            d_cum = d_cum + jnp.where(at_last, d_last, 0.0)
            d_summed = d_summed + jnp.where(cols == h, d_cum, 0.0)
            d_strength = d_strength + jnp.where(cols == heads + h, d_beta, 0.0)
            delta_ref[:, value_at + h * DV : value_at + (h + 1) * DV] = (
                strength * d_right
            ).astype(BF16)
        dq_raw = (q_scale * DK ** (-0.5)) * (
            dq_sum - q_unit * jnp.sum(q_unit * dq_sum, axis=-1, keepdims=True)
        )
        dk_raw = k_scale * (dk_sum - k * jnp.sum(k * dk_sum, axis=-1, keepdims=True))
        delta_ref[:, kh * DK : (kh + 1) * DK] = dq_raw.astype(BF16)
        delta_ref[:, (key_heads + kh) * DK : (key_heads + kh + 1) * DK] = dk_raw.astype(BF16)
    gate_at = value_at + heads * DV
    delta_ref[:, gate_at : gate_at + heads * DV] = gate_grad_ref[...]
    lower = (rows >= cols).astype(F32)
    d_decay = exact(lower, d_summed, TN)
    d_side = d_decay * (-scale_ref[...]) * jax.nn.sigmoid(side) + d_strength * beta * (1.0 - beta)
    delta_ref[:, side_at : side_at + LANES] = d_side.astype(BF16)


def mm_wide(a, s, dims=NN):
    s_high, s_low = split(s)
    return dot(a, s_high, dims) + dot(a, s_low, dims)


def greet(peers):
    barrier = pltpu.get_barrier_semaphore()
    for peer in peers:
        pl.semaphore_signal(barrier, inc=1, device_id={"ctx": peer}, device_id_type=MESH)
    pl.semaphore_wait(barrier, len(peers))


def ring_peers():
    me = lax.axis_index("ctx")
    x, y = me // SIDE, lax.rem(me, SIDE)
    row = [x * SIDE + lax.rem(y + d, SIDE) for d in range(1, SIDE)]
    col = [lax.rem(x + d, SIDE) * SIDE + y for d in range(1, SIDE)]
    return x, y, row, col


def exchange(buffer, slot, peers, send_sem, recv_sem):
    copies = [
        pltpu.make_async_remote_copy(
            src_ref=buffer.at[slot],
            dst_ref=buffer.at[slot],
            send_sem=send_sem.at[d],
            recv_sem=recv_sem.at[d],
            device_id={"ctx": peer},
            device_id_type=MESH,
        )
        for d, peer in enumerate(peers)
    ]
    for copy in copies:
        copy.start()
    return copies


def chain_forward_kernel(
    heads, a_ref, b_ref, s_ref, rows_ref, cols_ref, row_buf, col_buf, sems
):
    x, y, row, col = ring_peers()
    greet(row + col)
    for h in range(heads):
        row_buf[y, 0, h] = a_ref[h].astype(BF16)
        row_buf[y, 1, h] = b_ref[h].astype(BF16)
    copies = exchange(row_buf, y, row, sems.at[0], sems.at[1])
    for copy in copies:
        copy.wait()
    for h in range(heads):
        a = row_buf[0, 0, h].astype(F32)
        b = row_buf[0, 1, h].astype(F32)
        for i in range(1, SIDE):
            both = mm_wide(row_buf[i, 0, h], jnp.concatenate([a, b], axis=1))
            a = both[:, :DK]
            b = both[:, DK:] + row_buf[i, 1, h].astype(F32)
        col_buf[x, 0, h] = a.astype(BF16)
        col_buf[x, 1, h] = b.astype(BF16)
    copies = exchange(col_buf, x, col, sems.at[2], sems.at[3])
    for copy in copies:
        copy.wait()
    for h in range(heads):
        s = jnp.zeros((DK, DV), F32)
        for i in range(SIDE - 1):
            new = mm_wide(col_buf[i, 0, h], s) + col_buf[i, 1, h].astype(F32)
            s = jnp.where(i < x, new, s)
        for i in range(SIDE - 1):
            new = mm_wide(row_buf[i, 0, h], s) + row_buf[i, 1, h].astype(F32)
            s = jnp.where(i < y, new, s)
        s_ref[h] = s
        for i in range(SIDE):
            rows_ref[i, h] = row_buf[i, 0, h]
            cols_ref[i, h] = col_buf[i, 0, h]


def chain_backward_kernel(heads, l_ref, rows_ref, cols_ref, g_ref, row_buf, col_buf, sems):
    x, y, row, col = ring_peers()
    greet(row + col)
    for h in range(heads):
        row_buf[y, h] = l_ref[h].astype(BF16)
    copies = exchange(row_buf, y, row, sems.at[0], sems.at[1])
    for copy in copies:
        copy.wait()
    for h in range(heads):
        g = row_buf[SIDE - 1, h].astype(F32)
        for i in range(SIDE - 2, -1, -1):
            g = mm_wide(rows_ref[i, h], g, TN) + row_buf[i, h].astype(F32)
        col_buf[x, h] = g.astype(BF16)
    copies = exchange(col_buf, x, col, sems.at[2], sems.at[3])
    for copy in copies:
        copy.wait()
    for h in range(heads):
        g = jnp.zeros((DK, DV), F32)
        for i in range(SIDE - 1, 0, -1):
            new = mm_wide(cols_ref[i, h], g, TN) + col_buf[i, h].astype(F32)
            g = jnp.where(i > x, new, g)
        for i in range(SIDE - 1, 0, -1):
            new = mm_wide(rows_ref[i, h], g, TN) + row_buf[i, h].astype(F32)
            g = jnp.where(i > y, new, g)
        g_ref[h] = g


VMEM_LIMIT = 48 * 2**20


def body(
    inputs,
    query_key_weight,
    value_gate_weight,
    decay_beta_weight,
    beta_bias,
    decay_scale,
    norm_gain,
    out_weight,
    boundaries,
    grad_mixed,
):
    tokens, width = inputs.shape
    heads = beta_bias.shape[0]
    key_heads = query_key_weight.shape[2] // DK
    repeat = heads // key_heads
    blocks = tokens // BLOCK
    weights = jnp.concatenate(
        [
            query_key_weight[0],
            query_key_weight[1],
            value_gate_weight[0],
            value_gate_weight[1],
            decay_beta_weight[0],
            decay_beta_weight[1],
            jnp.zeros((width, LANES - 2 * heads), BF16),
        ],
        axis=1,
    )
    columns = weights.shape[1]
    proj = jnp.dot(inputs, weights, preferred_element_type=F32)
    up = jnp.einsum("td,fd->tf", grad_mixed, out_weight, preferred_element_type=F32)
    resets = boundaries.astype(F32)[:, None]
    scale_row = jnp.pad(decay_scale, (0, LANES - heads))[None]
    bias_row = jnp.pad(beta_bias, (heads, LANES - 2 * heads))[None]
    gain_row = norm_gain[None]

    square = jax.ShapeDtypeStruct((blocks, heads, BLOCK, BLOCK), F32)
    state = jax.ShapeDtypeStruct((heads, DK, DV), F32)

    def whole(shape):
        return pl.BlockSpec(shape, lambda i: (0,) * len(shape))

    def at(index):
        def token(shape, column=0):
            return pl.BlockSpec(shape, lambda i: (index(i), column))

        per_block = pl.BlockSpec((1, heads, BLOCK, BLOCK), lambda i: (index(i), 0, 0, 0))
        return token, per_block

    params = pltpu.CompilerParams(
        dimension_semantics=("arbitrary",), vmem_limit_bytes=VMEM_LIMIT
    )
    token, per_block = at(lambda i: i)
    state_spec = whole((heads, DK, DV))
    terms = pl.pallas_call(
        functools.partial(terms_kernel, key_heads, repeat),
        grid=(blocks,),
        in_specs=[
            token((BLOCK, columns)),
            token((BLOCK, 1)),
            whole((1, LANES)),
            whole((1, LANES)),
        ],
        out_specs=[per_block] * 9 + [state_spec] * 2,
        out_shape=[square] * 9 + [state] * 2,
        compiler_params=params,
        name="terms",
    )(proj, resets, scale_row, bias_row)
    inverse, base, weight, score, start_map, local_out, step_map, step_add, prefix = terms[:9]
    map_total, add_total = terms[9:]

    state_in, row_maps, col_maps = chain_forward(map_total, add_total)

    gate_at = (2 * key_heads * DK + heads * DV) // (heads * DV)
    hidden, gate_grad, grad_out, value, before, grad_total = pl.pallas_call(
        functools.partial(forward_kernel, heads),
        grid=(blocks,),
        in_specs=[
            token((BLOCK, heads * DV), gate_at),
            token((BLOCK, heads * DV)),
            whole((1, LANES)),
            state_spec,
        ]
        + [per_block] * 7,
        out_specs=[token((BLOCK, heads * DV))] * 2 + [per_block] * 3 + [state_spec],
        out_shape=[jax.ShapeDtypeStruct((tokens, heads * DV), BF16)] * 2 + [square] * 3 + [state],
        scratch_shapes=[pltpu.VMEM((heads, DK, DV), F32)],
        compiler_params=params,
        name="forward",
    )(
        proj,
        up,
        gain_row,
        state_in,
        base,
        weight,
        start_map,
        local_out,
        step_map,
        step_add,
        prefix,
    )
    partial_out = jnp.dot(hidden, out_weight, preferred_element_type=F32)
    mixed = lax.psum_scatter(partial_out.astype(BF16), "head", scatter_dimension=1, tiled=True)
    term_out = jnp.einsum("tf,td->fd", hidden, grad_mixed, preferred_element_type=F32)
    grad_out_weight = lax.psum_scatter(
        term_out.astype(BF16), "ctx", scatter_dimension=1, tiled=True
    ).astype(F32)

    grad_state = chain_backward(grad_total, row_maps, col_maps)

    token, per_block = at(lambda i: blocks - 1 - i)
    delta = pl.pallas_call(
        functools.partial(backward_kernel, key_heads, repeat),
        grid=(blocks,),
        in_specs=[
            token((BLOCK, columns)),
            token((BLOCK, 1)),
            whole((1, LANES)),
            whole((1, LANES)),
            state_spec,
        ]
        + [per_block] * 5
        + [token((BLOCK, heads * DV))],
        out_specs=token((BLOCK, columns)),
        out_shape=jax.ShapeDtypeStruct((tokens, columns), BF16),
        scratch_shapes=[pltpu.VMEM((heads, DK, DV), F32)],
        compiler_params=params,
        name="backward",
    )(
        proj,
        resets,
        scale_row,
        bias_row,
        grad_state,
        inverse,
        score,
        value,
        before,
        grad_out,
        gate_grad,
    )
    term = jnp.einsum("td,tf->df", inputs, delta, preferred_element_type=F32)
    term = lax.psum_scatter(term.astype(BF16), "ctx", scatter_dimension=0, tiled=True).astype(F32)
    grad_rows = jnp.einsum("tf,df->td", delta, weights, preferred_element_type=F32)
    grad_inputs = lax.psum_scatter(grad_rows.astype(BF16), "head", scatter_dimension=1, tiled=True)
    key_width = key_heads * DK
    value_width = heads * DV

    def pair(start, size):
        return jnp.stack([term[:, start : start + size], term[:, start + size : start + 2 * size]])

    return (
        mixed,
        grad_inputs,
        pair(0, key_width),
        pair(2 * key_width, value_width),
        pair(2 * key_width + 2 * value_width, heads),
        grad_out_weight,
    )


def chain_forward(map_total, add_total):
    heads = map_total.shape[0]
    maps = jax.ShapeDtypeStruct((SIDE, heads, DK, DK), BF16)
    buffer = pltpu.VMEM((SIDE, 2, heads, DK, DV), BF16)
    return pl.pallas_call(
        functools.partial(chain_forward_kernel, heads),
        out_shape=[jax.ShapeDtypeStruct((heads, DK, DV), F32), maps, maps],
        in_specs=[pl.BlockSpec(memory_space=pltpu.VMEM)] * 2,
        out_specs=[pl.BlockSpec(memory_space=pltpu.VMEM)] * 3,
        scratch_shapes=[buffer, buffer, pltpu.SemaphoreType.DMA((4, SIDE - 1))],
        compiler_params=pltpu.CompilerParams(
            collective_id=0, has_side_effects=True, vmem_limit_bytes=VMEM_LIMIT
        ),
        name="chain_forward",
    )(map_total, add_total)


def chain_backward(grad_total, row_maps, col_maps):
    heads = grad_total.shape[0]
    buffer = pltpu.VMEM((SIDE, heads, DK, DV), BF16)
    return pl.pallas_call(
        functools.partial(chain_backward_kernel, heads),
        out_shape=jax.ShapeDtypeStruct((heads, DK, DV), F32),
        in_specs=[pl.BlockSpec(memory_space=pltpu.VMEM)] * 3,
        out_specs=pl.BlockSpec(memory_space=pltpu.VMEM),
        scratch_shapes=[buffer, buffer, pltpu.SemaphoreType.DMA((4, SIDE - 1))],
        compiler_params=pltpu.CompilerParams(
            collective_id=1, has_side_effects=True, vmem_limit_bytes=VMEM_LIMIT
        ),
        name="chain_backward",
    )(grad_total, row_maps, col_maps)


def solution(mesh):
    in_specs = (
        P("ctx", None),
        P(None, None, "head"),
        P(None, None, "head"),
        P(None, None, "head"),
        P("head"),
        P("head"),
        P(),
        P("head", None),
        P("ctx"),
        P("ctx", None),
    )
    out_specs = (
        P("ctx", "head"),
        P("ctx", "head"),
        P(None, "ctx", "head"),
        P(None, "ctx", "head"),
        P(None, "ctx", "head"),
        P("head", "ctx"),
    )
    return jax.shard_map(body, mesh=mesh, in_specs=in_specs, out_specs=out_specs, check_vma=False)
```

time: 1530 us -> 367 us (0.24)
  matrix products: 477 us -> 33.1 us
  other arithmetic: 276 us -> 2.26 us
  waiting for transfers between devices: 404 us -> 149 us
  local copies, waits for them, and re-layouts: 223 us -> 58.4 us
  starting transfers between devices: 115 us -> 0.34 us
  Pallas kernels: 0 us -> 109 us
    dot_general x232 -> x6, matrix products: 464 us -> 33.1 us  [the longest x1 8.72 us: body(): proj = jnp.dot(inputs, weights, preferred_element_type=F32)]
    another operation x12 -> x3, other arithmetic: 170 us -> 0.65 us  [pair(): jnp.stack([term[:, start:start + size], term[:, start + size:start + 2 *...]
    ppermute x30 -> x0, waiting for transfers between devices: 151 us -> none  [shifted(): return lax.ppermute(block, axis, route)]
    ppermute x30 -> x0, starting transfers between devices: 115 us -> none  [shifted(): return lax.ppermute(block, axis, route)]
    pallas_call x0 -> x5, Pallas kernels: none -> 109 us  [the longest x1 34.7 us: chain_forward(): pl.pallas_call(functools.partial(chain_forward_kernel, heads), out_shape=...]
    unnamed x10 -> x6, waiting for transfers between devices: 184 us -> 81.1 us
    reduce_sum x29 -> x0, other arithmetic: 45.4 us -> none  [the longest x16 21.5 us: advance(): block_retained_decay[:, None, None] * carried_state]
    convert_element_type x39 -> x3, other arithmetic: 43.7 us -> 1.61 us  [the longest x1 0.82 us: body(): resets = boundaries.astype(F32)[:, None]]
  transfers between devices with their start and end apart: 36 -> 4, of which waited for: 35 -> 3; matrix products, arithmetic and copies ran while one was open for 9% -> 10% of each run, Pallas kernels for 0% -> 11%
where the time goes in v1:
time: 367 us; the launch traced here: 365 us
  waiting for transfers between devices  149 us (41%)
  Pallas kernels  109 us (30%)
  local copies, waits for them, and re-layouts  58.4 us (16%)
  matrix products  33.1 us (9%)
  between operations  14 us (4%)
    unnamed x6, waiting for transfers between devices  81.1 us
    unnamed x68, local copies, waits for them, and re-layouts  38.1 us
    reduce_scatter x1, waiting for transfers between devices, body(): lax.psum_scatter(partial_out.astype(BF16), 'head', scatter_dimension=1, t...  35.4 us
    pallas_call x1, Pallas kernels, chain_forward(): pl.pallas_call(functools.partial(chain_forward_kernel, heads), out_shape=...  34.7 us
    reduce_scatter x1, waiting for transfers between devices, body(): lax.psum_scatter(grad_rows.astype(BF16), 'head', scatter_dimension=1, til...  32.3 us
    pallas_call x1, Pallas kernels, chain_backward(): pl.pallas_call(functools.partial(chain_backward_kernel, heads), out_shape...  22.9 us
    pallas_call x1, Pallas kernels, body(): pl.pallas_call(functools.partial(terms_kernel, key_heads, repeat), grid=(...  20.1 us
    pallas_call x1, Pallas kernels, body(): pl.pallas_call(functools.partial(backward_kernel, key_heads, repeat), gri...  18 us
  transfers between devices with their start and end apart: 4, of which 3 were waited for; matrix products, arithmetic and copies ran while one was open for 10% of the time, Pallas kernels for 11%

profile of v1, /device:TPU:0, one launch (start us, length us, event | category | flops | bytes accessed | tf_op | source)
XLA Modules:
  0.0 365.5 jit_solution(14972359592085859420)
XLA Ops:
  9.0 1.1 copy.29
  10.0 1.1 copy.28
  11.1 2.9 slice_bitcast_fusion.2
  14.0 2.4 slice_bitcast_fusion
  16.5 1.2 copy-done.30
  17.8 2.3 fusion.1.up_ref
  20.9 11.0 %concatenate.3 = bf16[2048,1664]{1,0:T(8,128)(2,1)} concatenate(bf16[2048,256]{1,0:T(8,128)(2,1)} %get-tuple-element.67, bf16[2048,256]{1,0:T(8,128)(2,1)S(1)} %get-tuple-element.66, bf16[2048,512]{1,0:T(8,128)(2,1)} %get-tuple-element.65, bf16[2048,512]{1,0:T(8,128)(2,1)} %get-tuple-element.64, bf16[2048,4]{1,0:T(8,128)(2,1)} %copy.28, bf16[2048,4]{1,0:T(8,128)(2,1)} %copy.29, ...), dimensions={1} | concatenate | bytes 13631488 | tf_op jit(solution)/shard_map/concatenate | solution.py:455
  31.9 8.7 %convolution_bitcast_fusion.proj_ref.gate_ref = f32[512,1664]{1,0:T(8,128)} fusion(bf16[512,2048]{1,0:T(8,128)(2,1)S(1)} %copy-done, bf16[2048,1664]{1,0:T(8,128)(2,1)} %concatenate.3), kind=kOutput, calls=%fused_computation.2 | convolution fusion | flops 3489660928 | bytes 12320768 | tf_op jit(solution)/shard_map/dot_general | solution.py:468
  40.6 20.1 %terms.1 = (f32[4,4,128,128]{3,2,1,0:T(8,128)S(1)}, f32[4,4,128,128]{3,2,1,0:T(8,128)S(1)}, f32[4,4,128,128]{3,2,1,0:T(8,128)S(1)}, f32[4,4,128,128]{3,2,1,0:T(8...) custom-call(f32[512,1664]{1,0:T(8,128)} %convolution_bitcast_fusion., ...), custom_call_target="tpu_custom_call" | custom-call | tf_op jit(solution)/shard_map/terms/pallas_call | solution.py:493
  60.8 1.0 copy-done.2
  64.7 34.7 %chain_forward.1 = (f32[4,128,128]{2,1,0:T(8,128)S(1)}, bf16[4,4,128,128]{3,2,1,0:T(8,128)(2,1)S(1)}, bf16[4,4,128,128]{3,2,1,0:T(8,128)(2,1)S(1)}) custom-call(f32[4,128,128]{2,1,0:T(8,128)S(1)} %get-tuple-element.26.a_ref, f32[4,128,128]{2,1,0:T(8,128)S(1)} %get-tuple-element.27.b_ref), custom_call_target="tpu_custom_call" | custom-call | tf_op jit(solution)/shard_map/chain_forward/pallas_call | solution.py:605
  100.3 12.9 %forward.1 = (bf16[512,512]{1,0:T(8,128)(2,1)S(1)}, bf16[512,512]{1,0:T(8,128)(2,1)S(1)}, f32[4,4,128,128]{3,2,1,0:T(8,128)S(1)}, f32[4,4,128,128]{3,2,1,0:T(8,1...) custom-call(f32[512,1664]{1,0:T(8,128)} %convolution_bitcast_fusion.proj_ref.gate_ref, ...), custom_call_target="tpu_custom_call" | custom-call | tf_op jit(solution)/shard_map/forward/pallas_call | solution.py:513
  114.2 1.0 copy-done.5
  118.5 2.6 convolution_convert_fusion.1
  121.1 3.9 %copy.38 = bf16[512,2048]{0,1:T(8,128)(2,1)} copy(bf16[512,2048]{1,0:T(8,128)(2,1)} %convolution_convert_fusion.1) | data formatting | bytes 4194304
  125.3 1.1 copy-done.16
  126.4 1.0 copy-done.18
  128.4 22.9 %chain_backward.1.grad_state_ref = f32[4,128,128]{2,1,0:T(8,128)S(1)} custom-call(f32[4,128,128]{2,1,0:T(8,128)S(1)} %copy-done.20, bf16[4,4,128,128]{3,2,1,0:T(8,128)(2,1)S(1)} %copy-done.16, bf16[4,4,128,128]{3,2,1,0:T(8,128)(2,1)S(1)} %copy-done.18), custom_call_target="tpu_custom_call" | custom-call | tf_op jit(solution)/shard_map/chain_backward/pallas_call | solution.py:621
  151.3 1.2 copy-done.6
  152.6 1.2 copy-done.8
  153.8 1.0 copy-done.14
  154.8 18.0 %backward.1 = bf16[512,1664]{1,0:T(8,128)(2,1)} custom-call(f32[512,1664]{1,0:T(8,128)} %convolution_bitcast_fusion.proj_ref.gate_ref, f32[512,1]{1,0:T(8,128)S(1)} %copy.31.reset_ref, f32[1,128]{1,0:T(1,128)S(1)} %get-tuple-element.77.scale_ref, f32[1,128]{1,0:T(1,128)S(1)} %get-tuple-element.76.bias_ref, f32[4,128,128]{2,1,0:T(8,128)S(1)} %chain_backward.1.grad_state_ref, ...), custom_call_target="tpu_custom_call" | custom-call | tf_op jit(solution)/shard_map/backward/pallas_call | solution.py:551
  172.8 7.2 %fusion = bf16[2048,1664]{0,1:T(8,128)(2,1)} fusion(bf16[512,1664]{1,0:T(8,128)(2,1)} %backward.1, bf16[512,2048]{1,0:T(8,128)(2,1)S(1)} %copy-done), kind=kOutput, calls=%fused_computation.1 | convolution fusion | flops 3493068800 | bytes 10616832 | tf_op jit(solution)/shard_map/td,tf->df/dot_general | solution.py:581
  180.0 9.7 %copy.36 = bf16[2048,1664]{1,0:T(8,128)(2,1)} copy(bf16[2048,1664]{0,1:T(8,128)(2,1)} %fusion) | data formatting | bytes 13631488
  189.8 1.4 copy-done.25
  191.1 8.1 %convolution_convert_fusion.2 = bf16[512,2048]{1,0:T(8,128)(2,1)} fusion(bf16[512,1664]{1,0:T(8,128)(2,1)S(1)} %copy-done.25, bf16[2048,1664]{1,0:T(8,128)(2,1)} %concatenate.3), kind=kOutput, calls=%fused_computation.4 | convolution fusion | flops 3490709504 | bytes 10616832 | tf_op jit(solution)/shard_map/tf,df->td/dot_general | solution.py:583
  200.3 4.2 %convolution_convert_fusion.3 = bf16[512,2048]{1,0:T(8,128)(2,1)} fusion(bf16[512,512]{1,0:T(8,128)(2,1)S(1)} %copy-done.23, bf16[512,2048]{1,0:T(8,128)(2,1)} %param.17), kind=kOutput, calls=%fused_computation.5 | convolution fusion | flops 1074790400 | bytes 4718592 | tf_op jit(solution)/shard_map/dot_general | solution.py:541
  204.5 1.0 copy.39
  206.3 81.0 %reduce-scatter.13.cloned.1.call-done = bf16[128,1664]{1,0:T(8,128)(2,1)} async-done(((bf16[2048,1664]{1,0:T(8,128)(2,1)}), bf16[128,1664]{1,0:T(8,128)(2,1)}) %reduce-scatter.13.cloned.1.call-update) | async-done | bytes 426000
  287.3 1.3 copy.37
  291.2 32.3 %reduce-scatter.11.cloned.1.call-done = bf16[512,256]{1,0:T(8,128)(2,1)} async-done(((bf16[512,2048]{1,0:T(8,128)(2,1)}), bf16[512,256]{1,0:T(8,128)(2,1)}) %reduce-scatter.11.cloned.1.call-update) | async-done | bytes 262160 | tf_op jit(solution)/shard_map/reduce_scatter | solution.py:584
  323.5 35.4 %reduce-scatter.9.cloned.1.call-done = bf16[512,256]{1,0:T(8,128)(2,1)} async-done(((bf16[512,2048]{1,0:T(8,128)(2,1)}), bf16[512,256]{1,0:T(8,128)(2,1)}) %reduce-scatter.9.cloned.1.call-update) | async-done | bytes 262160 | tf_op jit(solution)/shard_map/reduce_scatter | solution.py:542
  (77 shorter events, 16.5 us)
Async XLA Ops:
  7.2 24.7 %copy-start = (bf16[512,2048]{1,0:T(8,128)(2,1)S(1)}, bf16[512,2048]{1,0:T(8,128)(2,1)}, u32[]{:S(2)}) copy-start(bf16[512,2048]{1,0:T(8,128)(2,1)} %param.10) | copy-start | bytes 6291460
  7.2 197.3 %reduce-scatter.15.cloned.1.call-start = ((), (), s32[]{:S(2)}) async-start(), calls=%async_computation.7 | async-start | bytes 2228224
  11.1 2.9 copy-start.24
  14.0 2.4 copy-start.26
  14.0 2.4 copy-start.27
  14.0 2.5 copy-start.28
  14.0 3.8 %copy-start.30 = (bf16[512,2048]{1,0:T(8,128)(2,1)S(1)}, bf16[512,2048]{1,0:T(8,128)(2,1)}, u32[]{:S(2)}) copy-start(bf16[512,2048]{1,0:T(8,128)(2,1)} %param.17) | copy-start | bytes 6291460
  40.6 59.7 %copy-start.9 = (f32[512,512]{1,0:T(8,128)S(1)}, f32[512,512]{1,0:T(8,128)}, u32[]{:S(2)}) copy-start(f32[512,512]{1,0:T(8,128)} %fusion.1.up_ref) | copy-start | bytes 3145732
  40.6 59.7 %copy-start.21 = (f32[128]{0:T(128)S(1)}, f32[128]{0:T(128)}, u32[]{:S(2)}) copy-start(f32[128]{0:T(128)} %param.16) | copy-start | bytes 1540
  60.8 1.0 copy-start.2
  61.8 1.0 copy-start.10
  62.8 1.0 copy-start.11
  63.8 1.0 copy-start.12
  99.5 0.8 copy-start.17
  100.3 12.9 %copy-start.15 = (bf16[4,4,128,128]{3,2,1,0:T(8,128)(2,1)}, bf16[4,4,128,128]{3,2,1,0:T(8,128)(2,1)S(1)}, u32[]{:S(2)}) copy-start(bf16[4,4,128,128]{3,2,1,0:T(8,128)(2,1)S(1)} %get-tuple-element.38.rows_ref) | copy-start | bytes 1572868
  100.3 18.2 %copy-start.29 = (bf16[512,2048]{1,0:T(8,128)(2,1)S(1)}, bf16[512,2048]{1,0:T(8,128)(2,1)}, u32[]{:S(2)}) copy-start(bf16[512,2048]{1,0:T(8,128)(2,1)} %param.19) | copy-start | bytes 6291460
  113.2 1.0 copy-start.4
  114.2 1.0 copy-start.5
  115.2 1.0 copy-start.7
  125.0 162.3 %reduce-scatter.13.cloned.1.call-start = ((), (), s32[]{:S(2)}) async-start(), calls=%async_computation.6 | async-start | bytes 7241728
  125.3 26.0 %copy-start.3 = (f32[4,4,128,128]{3,2,1,0:T(8,128)S(1)}, f32[4,4,128,128]{3,2,1,0:T(8,128)}, u32[]{:S(2)}) copy-start(f32[4,4,128,128]{3,2,1,0:T(8,128)} %copy-done.2) | copy-start | bytes 3145732
  125.3 1.1 copy-start.16
  126.4 1.0 copy-start.18
  127.5 0.9 copy-start.20
  151.3 1.2 copy-start.6
  152.6 1.2 copy-start.8
  153.8 1.0 copy-start.14
  189.7 1.5 copy-start.25
  189.7 133.8 %reduce-scatter.11.cloned.1.call-start = ((), (), s32[]{:S(2)}) async-start(), calls=%async_computation.5 | async-start | bytes 2359296 | tf_op jit(solution)/shard_map/reduce_scatter | solution.py:584
  199.2 1.0 copy-start.23
  199.3 159.6 %reduce-scatter.9.cloned.1.call-start = ((), (), s32[]{:S(2)}) async-start(), calls=%async_computation.4 | async-start | bytes 2359296 | tf_op jit(solution)/shard_map/reduce_scatter | solution.py:542
  288.6 70.3 %copy-start.1 = (bf16[512,2048]{1,0:T(8,128)(2,1)S(1)}, bf16[512,2048]{1,0:T(8,128)(2,1)}, u32[]{:S(2)}) copy-start(bf16[512,2048]{1,0:T(8,128)(2,1)} %param.10) | copy-start | bytes 6291460
  (3 other events, 2.3 us)
Sparse Core Ops, SparseCore 0:
  125.2 76.7 reduce-scatter.14
  205.8 81.4 reduce-scatter.12
  290.3 33.1 reduce-scatter.10
  326.4 32.5 reduce-scatter.8

commit v2 on v1

--- a/solution.py
+++ b/solution.py
@@ -432,6 +432,290 @@
         g_ref[h] = g
 
 
+def add_into(target, index, *others):
+    total = target[index].astype(F32)
+    for ref, at in others:
+        total += ref[at].astype(F32)
+    target[index] = total.astype(BF16)
+
+
+def around(position):
+    return (
+        lax.rem(position + 1, SIDE),
+        lax.rem(position + SIDE - 1, SIDE),
+        lax.rem(position + 2, SIDE),
+    )
+
+
+def finish_kernel(
+    parts,
+    split_at,
+    x_ref,
+    delta_ref,
+    weight_ref,
+    hidden_ref,
+    out_weight_ref,
+    mixed_ref,
+    grad_ref,
+    qk_ref,
+    vg_ref,
+    db_ref,
+    one,
+    two,
+    one_first,
+    two_first,
+    one_second,
+    two_second,
+    one_third,
+    two_third,
+    one_fourth,
+    two_fourth,
+    away,
+    kept,
+    core_in,
+    z_first,
+    z_second,
+    send_sem,
+    recv_sem,
+):
+    me = lax.axis_index("ctx")
+    mine = lax.axis_index("head")
+    x, y = me // SIDE, lax.rem(me, SIDE)
+    z, core = mine // 2, lax.rem(mine, 2)
+    x_up, x_down, x_far = around(x)
+    y_up, y_down, y_far = around(y)
+    z_up, z_down, z_far = around(z)
+    peers = [
+        {"ctx": x * SIDE + y_up},
+        {"ctx": x * SIDE + y_down},
+        {"ctx": x_up * SIDE + y},
+        {"ctx": x_down * SIDE + y},
+        {"head": z * 2 + 1 - core},
+        {"head": z_up * 2 + core},
+        {"head": z_down * 2 + core},
+    ]
+    barrier = pltpu.get_barrier_semaphore()
+    for peer in peers:
+        pl.semaphore_signal(barrier, inc=1, device_id=peer, device_id_type=MESH)
+    pl.semaphore_wait(barrier, len(peers))
+    y_next, y_prev, x_next, x_prev, pair, z_next, z_prev = peers
+    used = []
+
+    def send(src, dst, peer):
+        slot = len(used)
+        copy = pltpu.make_async_remote_copy(
+            src_ref=src,
+            dst_ref=dst,
+            send_sem=send_sem.at[slot],
+            recv_sem=recv_sem.at[slot],
+            device_id=peer,
+            device_id_type=MESH,
+        )
+        copy.start()
+        used.append(copy)
+        return copy
+
+    width = grad_ref.shape[1]
+    rows = qk_ref.shape[1]
+
+    def mixed_block(z_to, core_to, target):
+        at = pl.multiple_of((z_to * 2 + core_to) * width, width)
+        target[0, z_to] = dot(
+            hidden_ref[...], out_weight_ref[:, pl.ds(at, width)], NN
+        ).astype(BF16)
+
+    def grad_block(z_to, core_to, target):
+        at = pl.multiple_of((z_to * 2 + core_to) * width, width)
+        target[1, z_to] = dot(delta_ref[...], weight_ref[pl.ds(at, width), :], NT).astype(BF16)
+
+    def term_block(x_to, y_to):
+        at = pl.multiple_of((x_to * SIDE + y_to) * rows, rows)
+        term = dot(x_ref[:, pl.ds(at, rows)], delta_ref[...], TN).astype(BF16)
+        one[y_to, x_to] = term[:, :split_at]
+        two[x_to, y_to] = term[:, split_at:]
+
+    def each(count, body):
+        def step(i, carry):
+            body(i)
+            return carry
+
+        lax.fori_loop(0, count, step, 0)
+
+    each(SIDE, lambda i: term_block(i, y_far))
+    one_a = send(one.at[y_far, pl.ds(0, 2)], one_first.at[0], y_next)
+    one_b = send(one.at[y_far, pl.ds(2, 2)], one_first.at[1], y_prev)
+    each(SIDE - 1, lambda i: term_block(x_far, lax.rem(y_far + 1 + i, SIDE)))
+    two_a = send(two.at[x_far, pl.ds(0, 2)], two_first.at[0], x_next)
+    two_b = send(two.at[x_far, pl.ds(2, 2)], two_first.at[1], x_prev)
+    each(SIDE, lambda i: mixed_block(i, 1 - core, away))
+    mixed_pair = send(away.at[0], core_in.at[0], pair)
+    each(
+        (SIDE - 1) * (SIDE - 1),
+        lambda i: term_block(
+            lax.rem(x_far + 1 + i // (SIDE - 1), SIDE),
+            lax.rem(y_far + 1 + lax.rem(i, SIDE - 1), SIDE),
+        ),
+    )
+    each(SIDE, lambda i: mixed_block(i, core, kept))
+
+    def second(store, first, second_in, ups, downs, up_peer, down_peer, a, b):
+        a.wait_recv()
+        each(2, lambda i: add_into(store, (ups, i), (first, (0, i))))
+        up = send(store.at[ups], second_in.at[0], up_peer)
+        b.wait_recv()
+        each(2, lambda i: add_into(store, (downs, 2 + i), (first, (1, i))))
+        down = send(store.at[downs], second_in.at[1], down_peer)
+        return up, down
+
+    one_c = second(one, one_first, one_second, y_up, y_down, y_next, y_prev, one_a, one_b)
+    two_c = second(two, two_first, two_second, x_up, x_down, x_next, x_prev, two_a, two_b)
+
+    half = grad_ref.shape[0] // 2
+
+    def z_start(k, arrived):
+        arrived.wait_recv()
+        add_into(kept, (k, z_far), (core_in, (k, z_far)))
+        a = send(kept.at[k, z_far, pl.ds(0, half)], z_first.at[k, 0], z_next)
+        b = send(kept.at[k, z_far, pl.ds(half, half)], z_first.at[k, 1], z_prev)
+        each(
+            SIDE - 1,
+            lambda i: add_into(
+                kept,
+                (k, lax.rem(z_far + 1 + i, SIDE)),
+                (core_in, (k, lax.rem(z_far + 1 + i, SIDE))),
+            ),
+        )
+        return a, b
+
+    def z_middle(k, pending):
+        a, b = pending
+        a.wait_recv()
+        add_into(kept, (k, z_up, pl.ds(0, half)), (z_first, (k, 0)))
+        up = send(kept.at[k, z_up], z_second.at[k, 0], z_next)
+        b.wait_recv()
+        add_into(kept, (k, z_down, pl.ds(half, half)), (z_first, (k, 1)))
+        down = send(kept.at[k, z_down], z_second.at[k, 1], z_prev)
+        return up, down
+
+    def z_end(k, pending, out_ref):
+        for copy in pending:
+            copy.wait_recv()
+        out_ref[...] = (
+            kept[k, z].astype(F32) + z_second[k, 0].astype(F32) + z_second[k, 1].astype(F32)
+        ).astype(BF16)
+
+    mixed_z = z_start(0, mixed_pair)
+    each(SIDE, lambda i: grad_block(i, 1 - core, away))
+    grad_pair = send(away.at[1], core_in.at[1], pair)
+    mixed_z = z_middle(0, mixed_z)
+    each(SIDE, lambda i: grad_block(i, core, kept))
+    grad_z = z_start(1, grad_pair)
+    z_end(0, mixed_z, mixed_ref)
+    grad_z = z_middle(1, grad_z)
+
+    def third(store, second_in, third_in, at, far, far_next, far_prev, pending):
+        for copy in pending:
+            copy.wait_recv()
+        add_into(store, (at, far), (second_in, (0, far)), (second_in, (1, far)))
+        n = rows // 2
+        a = send(store.at[at, far, pl.ds(0, n)], third_in.at[0], far_next)
+        b = send(store.at[at, far, pl.ds(n, n)], third_in.at[1], far_prev)
+        for i in range(1, SIDE):
+            other = lax.rem(far + i, SIDE)
+            add_into(store, (at, other), (second_in, (0, other)), (second_in, (1, other)))
+        return a, b
+
+    def fourth(store, third_in, fourth_in, at, ups, downs, up_peer, down_peer, pending):
+        a, b = pending
+        n = rows // 2
+        a.wait_recv()
+        add_into(store, (at, ups, pl.ds(0, n)), (third_in, 0))
+        up = send(store.at[at, ups], fourth_in.at[0], up_peer)
+        b.wait_recv()
+        add_into(store, (at, downs, pl.ds(n, n)), (third_in, 1))
+        down = send(store.at[at, downs], fourth_in.at[1], down_peer)
+        return up, down
+
+    two_d = third(two, two_second, two_third, x, y_far, y_next, y_prev, two_c)
+    one_d = third(one, one_second, one_third, y, x_far, x_next, x_prev, one_c)
+    two_e = fourth(two, two_third, two_fourth, x, y_up, y_down, y_next, y_prev, two_d)
+    one_e = fourth(one, one_third, one_fourth, y, x_up, x_down, x_next, x_prev, one_d)
+    z_end(1, grad_z, grad_ref)
+
+    def total(store, fourth_in, at, to, pending):
+        for copy in pending:
+            copy.wait_recv()
+        return (
+            store[at, to].astype(F32) + fourth_in[0].astype(F32) + fourth_in[1].astype(F32)
+        )
+
+    sums = (total(two, two_fourth, x, y, two_e), total(one, one_fourth, y, x, one_e))
+    for ref, s, start, size in parts:
+        if start < split_at:
+            ref_value = sums[1][:, start : start + size]
+        else:
+            ref_value = sums[0][:, start - split_at : start - split_at + size]
+        (qk_ref, vg_ref, db_ref)[ref][s] = ref_value
+    for copy in used:
+        copy.wait_send()
+
+
+def finish(inputs, delta, weights, hidden, out_weight, heads, key_heads):
+    tokens, width = inputs.shape
+    columns = delta.shape[1]
+    key_width, value_width = key_heads * DK, heads * DV
+    side_at = 2 * (key_width + value_width)
+    parts = [
+        (0, 0, 0, key_width),
+        (0, 1, key_width, key_width),
+        (1, 0, 2 * key_width, value_width),
+        (1, 1, 2 * key_width + value_width, value_width),
+        (2, 0, side_at, heads),
+        (2, 1, side_at + heads, heads),
+    ]
+    split_at = 2 * key_width + value_width
+    rows = width // (SIDE * SIDE)
+    block = width // (2 * SIDE)
+    sizes = (split_at, columns - split_at)
+    half = tokens // 2
+
+    def both(*shape):
+        return [pltpu.VMEM((*shape, n), BF16) for n in sizes]
+
+    vmem = pl.BlockSpec(memory_space=pltpu.VMEM)
+    return pl.pallas_call(
+        functools.partial(finish_kernel, parts, split_at),
+        out_shape=[
+            jax.ShapeDtypeStruct((tokens, block), BF16),
+            jax.ShapeDtypeStruct((tokens, block), BF16),
+            jax.ShapeDtypeStruct((2, rows, key_width), F32),
+            jax.ShapeDtypeStruct((2, rows, value_width), F32),
+            jax.ShapeDtypeStruct((2, rows, heads), F32),
+        ],
+        in_specs=[vmem] * 5,
+        out_specs=[vmem] * 5,
+        scratch_shapes=[
+            *both(SIDE, SIDE, rows),
+            *both(2, 2, rows),
+            *both(2, SIDE, rows),
+            *both(2, rows // 2),
+            *both(2, rows),
+            pltpu.VMEM((2, SIDE, tokens, block), BF16),
+            pltpu.VMEM((2, SIDE, tokens, block), BF16),
+            pltpu.VMEM((2, SIDE, tokens, block), BF16),
+            pltpu.VMEM((2, 2, half, block), BF16),
+            pltpu.VMEM((2, 2, tokens, block), BF16),
+            pltpu.SemaphoreType.DMA((26,)),
+            pltpu.SemaphoreType.DMA((26,)),
+        ],
+        compiler_params=pltpu.CompilerParams(
+            collective_id=2, has_side_effects=True, vmem_limit_bytes=FINISH_LIMIT
+        ),
+        name="finish",
+    )(inputs, delta, weights, hidden, out_weight)
+
+
+FINISH_LIMIT = 56 * 2**20
 VMEM_LIMIT = 48 * 2**20
 
 
@@ -538,8 +822,6 @@
         step_add,
         prefix,
     )
-    partial_out = jnp.dot(hidden, out_weight, preferred_element_type=F32)
-    mixed = lax.psum_scatter(partial_out.astype(BF16), "head", scatter_dimension=1, tiled=True)
     term_out = jnp.einsum("tf,td->fd", hidden, grad_mixed, preferred_element_type=F32)
     grad_out_weight = lax.psum_scatter(
         term_out.astype(BF16), "ctx", scatter_dimension=1, tiled=True
@@ -578,22 +860,15 @@
         grad_out,
         gate_grad,
     )
-    term = jnp.einsum("td,tf->df", inputs, delta, preferred_element_type=F32)
-    term = lax.psum_scatter(term.astype(BF16), "ctx", scatter_dimension=0, tiled=True).astype(F32)
-    grad_rows = jnp.einsum("tf,df->td", delta, weights, preferred_element_type=F32)
-    grad_inputs = lax.psum_scatter(grad_rows.astype(BF16), "head", scatter_dimension=1, tiled=True)
-    key_width = key_heads * DK
-    value_width = heads * DV
-
-    def pair(start, size):
-        return jnp.stack([term[:, start : start + size], term[:, start + size : start + 2 * size]])
-
+    mixed, grad_inputs, grad_query_key, grad_value_gate, grad_decay_beta = finish(
+        inputs, delta, weights, hidden, out_weight, heads, key_heads
+    )
     return (
         mixed,
         grad_inputs,
-        pair(0, key_width),
-        pair(2 * key_width, value_width),
-        pair(2 * key_width + 2 * value_width, heads),
+        grad_query_key,
+        grad_value_gate,
+        grad_decay_beta,
         grad_out_weight,
     )
 

time: 367 us -> 253 us (0.69)
  waiting for transfers between devices: 149 us -> 0.02 us
  Pallas kernels: 109 us -> 172 us
  matrix products: 33.1 us -> 14.3 us
  local copies, waits for them, and re-layouts: 58.4 us -> 50.2 us
    unnamed x6 -> x2, waiting for transfers between devices: 81.1 us -> 0.02 us
    reduce_scatter x2 -> x0, waiting for transfers between devices: 67.7 us -> none  [the longest x1 35.4 us: body(): lax.psum_scatter(partial_out.astype(BF16), 'head', scatter_dimension=1, t...]
    pallas_call x0 -> x1, Pallas kernels: none -> 63.5 us  [finish(): pl.pallas_call(functools.partial(finish_kernel, parts, split_at), out_sha...]
    dot_general x3 -> x0, matrix products: 19.5 us -> none  [the longest x1 8.1 us: body(): jnp.einsum('tf,df->td', delta, weights, preferred_element_type=F32)]
    unnamed x68 -> x63, local copies, waits for them, and re-layouts: 38.1 us -> 32.1 us
  transfers between devices with their start and end apart: 4 -> 1, of which waited for: 3 -> 0; matrix products, arithmetic and copies ran while one was open for 10% -> 1% of each run, Pallas kernels for 11% -> 41%
where the time goes in v2:
time: 253 us; the launch traced here: 252 us
  Pallas kernels  172 us (68%)
  local copies, waits for them, and re-layouts  50.2 us (20%)
  matrix products  14.3 us (6%)
  between operations  14.2 us (6%)
    pallas_call x1, Pallas kernels, finish(): pl.pallas_call(functools.partial(finish_kernel, parts, split_at), out_sha...  63.5 us
    pallas_call x1, Pallas kernels, chain_forward(): pl.pallas_call(functools.partial(chain_forward_kernel, heads), out_shape=...  34.7 us
    unnamed x63, local copies, waits for them, and re-layouts  32.1 us
    pallas_call x1, Pallas kernels, chain_backward(): pl.pallas_call(functools.partial(chain_backward_kernel, heads), out_shape...  22.9 us
    pallas_call x1, Pallas kernels, body(): pl.pallas_call(functools.partial(terms_kernel, key_heads, repeat), grid=(...  20.1 us
    pallas_call x1, Pallas kernels, body(): pl.pallas_call(functools.partial(backward_kernel, key_heads, repeat), gri...  18 us
    pallas_call x1, Pallas kernels, body(): pl.pallas_call(functools.partial(forward_kernel, heads), grid=(blocks,),...  12.7 us
    concatenate x1, local copies, waits for them, and re-layouts, body(): jnp.concatenate([query_key_weight[0], query_key_weight[1], value_gate_wei...  11 us
  transfers between devices with their start and end apart: 1, of which 0 were waited for; matrix products, arithmetic and copies ran while one was open for 1% of the time, Pallas kernels for 41%

profile of v2, /device:TPU:0, one launch (start us, length us, event | category | flops | bytes accessed | tf_op | source)
XLA Modules:
  0.0 252.2 jit_solution(2705926057088076173)
XLA Ops:
  9.0 1.1 copy.36
  10.0 1.1 copy.35
  11.1 2.9 %slice_bitcast_fusion.2 = (bf16[2048,256]{1,0:T(8,128)(2,1)S(1)}, bf16[2048,256]{1,0:T(8,128)(2,1)}) fusion(bf16[2,2048,256]{2,1,0:T(8,128)(2,1)} %param.11), kind=kLoop, calls=%fused_computation.4 | loop fusion | bytes 4194304 | tf_op jit(solution)/shard_map/squeeze | solution.py:742
  14.0 2.4 slice_bitcast_fusion
  16.6 2.4 fusion.1.up_ref
  19.8 11.0 %concatenate.3.weight_ref = bf16[2048,1664]{1,0:T(8,128)(2,1)} concatenate(bf16[2048,256]{1,0:T(8,128)(2,1)} %get-tuple-element.77, bf16[2048,256]{1,0:T(8,128)(2,1)S(1)} %get-tuple-element.76, bf16[2048,512]{1,0:T(8,128)(2,1)} %get-tuple-element.75, bf16[2048,512]{1,0:T(8,128)(2,1)} %get-tuple-element.74, bf16[2048,4]{1,0:T(8,128)(2,1)} %bitcast.29, bf16[2048,4]{1,0:T(8,128)(2,1)} %bitcast.28, ...), dimensions={1} | concatenate | bytes 13631488 | tf_op jit(solution)/shard_map/concatenate | solution.py:739
  30.8 9.3 %convolution_bitcast_fusion.proj_ref.gate_ref = f32[512,1664]{1,0:T(8,128)} fusion(bf16[512,2048]{1,0:T(8,128)(2,1)} %x_ref.1, bf16[2048,1664]{1,0:T(8,128)(2,1)} %concatenate.3.weight_ref), kind=kOutput, calls=%fused_computation | convolution fusion | flops 3489660928 | bytes 12320768 | tf_op jit(solution)/shard_map/dot_general | solution.py:752
  40.2 20.1 %terms.1 = (f32[4,4,128,128]{3,2,1,0:T(8,128)S(1)}, f32[4,4,128,128]{3,2,1,0:T(8,128)S(1)}, f32[4,4,128,128]{3,2,1,0:T(8,128)S(1)}, f32[4,4,128,128]{3,2,1,0:T(8...) custom-call(f32[512,1664]{1,0:T(8,128)} %convolution_bitcast_fusion., ...), custom_call_target="tpu_custom_call" | custom-call | tf_op jit(solution)/shard_map/terms/pallas_call | solution.py:777
  60.3 1.0 copy-done.1
  61.3 0.9 copy-done.9
  62.2 1.0 copy-done.10
  63.2 1.0 copy-done.11
  64.2 34.7 %chain_forward.1 = (f32[4,128,128]{2,1,0:T(8,128)S(1)}, bf16[4,4,128,128]{3,2,1,0:T(8,128)(2,1)S(1)}, bf16[4,4,128,128]{3,2,1,0:T(8,128)(2,1)S(1)}) custom-call(f32[4,128,128]{2,1,0:T(8,128)S(1)} %get-tuple-element.31.a_ref, f32[4,128,128]{2,1,0:T(8,128)S(1)} %get-tuple-element.32.b_ref), custom_call_target="tpu_custom_call" | custom-call | tf_op jit(solution)/shard_map/chain_forward/pallas_call | solution.py:880
  100.5 12.7 %forward.1 = (bf16[512,512]{1,0:T(8,128)(2,1)S(1)}, bf16[512,512]{1,0:T(8,128)(2,1)S(1)}, f32[4,4,128,128]{3,2,1,0:T(8,128)S(1)}, f32[4,4,128,128]{3,2,1,0:T(8,1...) custom-call(f32[512,1664]{1,0:T(8,128)} %convolution_bitcast_fusion.proj_ref.gate_ref, ...), custom_call_target="tpu_custom_call" | custom-call | tf_op jit(solution)/shard_map/forward/pallas_call | solution.py:797
  113.2 1.0 copy-done.4
  114.2 1.0 copy-done.5
  115.2 1.0 copy-done.7
  118.5 2.6 %convolution_convert_fusion = bf16[512,2048]{1,0:T(8,128)(2,1)} fusion(bf16[512,512]{1,0:T(8,128)(2,1)S(1)} %get-tuple-element.50.hidden_ref, bf16[512,2048]{1,0:T(8,128)(2,1)S(1)} %copy-done), kind=kOutput, calls=%fused_computation.1 | convolution fusion | flops 1074790400 | bytes 4718592 | tf_op jit(solution)/shard_map/tf,td->fd/dot_general | solution.py:825
  121.1 3.9 %copy.33 = bf16[512,2048]{0,1:T(8,128)(2,1)} copy(bf16[512,2048]{1,0:T(8,128)(2,1)} %convolution_convert_fusion) | data formatting | bytes 4194304
  125.1 1.1 copy-done.16
  126.2 1.0 copy-done.18
  128.2 22.9 %chain_backward.1.grad_state_ref = f32[4,128,128]{2,1,0:T(8,128)S(1)} custom-call(f32[4,128,128]{2,1,0:T(8,128)S(1)} %copy-done.20, bf16[4,4,128,128]{3,2,1,0:T(8,128)(2,1)S(1)} %copy-done.16, bf16[4,4,128,128]{3,2,1,0:T(8,128)(2,1)S(1)} %copy-done.18), custom_call_target="tpu_custom_call" | custom-call | tf_op jit(solution)/shard_map/chain_backward/pallas_call | solution.py:896
  151.1 1.2 copy-done.6
  152.4 1.2 copy-done.8
  153.6 1.0 copy-done.14
  154.6 18.0 %backward.1.delta_ref = bf16[512,1664]{1,0:T(8,128)(2,1)} custom-call(f32[512,1664]{1,0:T(8,128)} %convolution_bitcast_fusion.proj_ref.gate_ref, f32[512,1]{1,0:T(8,128)S(1)} %copy.30.reset_ref, f32[1,128]{1,0:T(1,128)S(1)} %get-tuple-element.81.scale_ref, f32[1,128]{1,0:T(1,128)S(1)} %get-tuple-element.80.bias_ref, ...), custom_call_target="tpu_custom_call" | custom-call | tf_op jit(solution)/shard_map/backward/pallas_call | solution.py:833
  172.6 63.5 %finish.1 = (bf16[512,256]{1,0:T(8,128)(2,1)}, bf16[512,256]{1,0:T(8,128)(2,1)}, f32[2,128,256]{2,1,0:T(8,128)}, f32[2,128,512]{2,1,0:T(8,128)}, f32[2,128,4]{2,1,0:T(8,128)}) custom-call(bf16[512,2048]{1,0:T(8,128)(2,1)} %x_ref.1, bf16[512,1664]{1,0:T(8,128)(2,1)} %backward.1.delta_ref, bf16[2048,1664]{1,0:T(8,128)(2,1)} %concatenate.3.weight_ref, ...), custom_call_target="tpu_custom_call" | custom-call | tf_op jit(solution)/shard_map/finish/pallas_call | solution.py:686
  236.2 1.6 copy.31
  237.8 1.0 copy.34
  239.5 1.7 copy.41
  241.2 1.7 copy.42
  242.9 1.7 copy.43
  (52 shorter events, 9.3 us)
Async XLA Ops:
  7.2 9.3 %copy-start = (bf16[512,2048]{1,0:T(8,128)(2,1)S(1)}, bf16[512,2048]{1,0:T(8,128)(2,1)}, u32[]{:S(2)}) copy-start(bf16[512,2048]{1,0:T(8,128)(2,1)} %param.19) | copy-start | bytes 6291460
  7.2 230.6 %reduce-scatter.4.cloned.1.call-start = ((), (), s32[]{:S(2)}) async-start(), calls=%async_computation.1 | async-start | bytes 2228224
  11.1 2.9 %copy-start.22 = (bf16[2,2048,512]{2,1,0:T(8,128)(2,1)S(1)}, bf16[2,2048,512]{2,1,0:T(8,128)(2,1)}, u32[]{:S(2)}) copy-start(bf16[2,2048,512]{2,1,0:T(8,128)(2,1)} %param.12) | copy-start | bytes 12582916
  14.0 2.4 copy-start.25
  14.0 2.4 copy-start.26
  14.0 2.5 %copy-start.23 = (bf16[512,2048]{1,0:T(8,128)(2,1)S(1)}, bf16[512,2048]{1,0:T(8,128)(2,1)}, u32[]{:S(2)}) copy-start(bf16[512,2048]{1,0:T(8,128)(2,1)} %out_weight_ref.1) | copy-start | bytes 6291460
  40.2 60.4 %copy-start.3 = (f32[512,512]{1,0:T(8,128)S(1)}, f32[512,512]{1,0:T(8,128)}, u32[]{:S(2)}) copy-start(f32[512,512]{1,0:T(8,128)} %fusion.1.up_ref) | copy-start | bytes 3145732
  40.2 60.4 %copy-start.21 = (f32[128]{0:T(128)S(1)}, f32[128]{0:T(128)}, u32[]{:S(2)}) copy-start(f32[128]{0:T(128)} %param.16) | copy-start | bytes 1540
  60.3 1.0 copy-start.1
  61.3 1.0 copy-start.9
  62.2 1.0 copy-start.10
  63.2 1.0 copy-start.11
  98.9 0.8 copy-start.15
  99.7 0.8 copy-start.17
  113.2 1.0 copy-start.4
  114.2 1.0 copy-start.5
  115.2 1.0 copy-start.7
  116.2 0.8 copy-start.13
  117.0 0.7 copy-start.19
  117.7 0.8 copy-start.12
  125.1 26.1 %copy-start.2 = (f32[4,4,128,128]{3,2,1,0:T(8,128)S(1)}, f32[4,4,128,128]{3,2,1,0:T(8,128)}, u32[]{:S(2)}) copy-start(f32[4,4,128,128]{3,2,1,0:T(8,128)} %copy-done.1) | copy-start | bytes 3145732
  125.1 1.1 copy-start.16
  126.2 1.0 copy-start.18
  127.3 0.9 copy-start.20
  151.1 1.2 copy-start.6
  152.4 1.2 copy-start.8
  153.6 1.0 copy-start.14
  236.1 8.4 %copy-start.24 = (f32[2,128,512]{2,1,0:T(8,128)S(1)}, f32[2,128,512]{2,1,0:T(8,128)}, u32[]{:S(2)}) copy-start(f32[2,128,512]{2,1,0:T(8,128)} %get-tuple-element.91) | copy-start | bytes 1572868
Sparse Core Ops, SparseCore 0:
  125.2 77.4 reduce-scatter.3

commit v3 on v2

v3 whole, which is shorter than its diff:
```python
import functools

import jax
import jax.numpy as jnp
from jax import lax
from jax.experimental import pallas as pl
from jax.experimental.pallas import tpu as pltpu
from jax.sharding import PartitionSpec as P

DK = 128
DV = 128
BLOCK = 128
EPS = 1e-06
LANES = 128
SIDE = 4
F32 = jnp.float32
BF16 = jnp.bfloat16
MESH = pl.DeviceIdType.MESH

NN = ((1,), (0,))
NT = ((1,), (1,))
TN = ((0,), (0,))


def dot(a, b, dims):
    return lax.dot_general(a, b, (dims, ((), ())), preferred_element_type=F32)


def split(a):
    high = a.astype(BF16)
    return high, (a - high.astype(F32)).astype(BF16)


def mm3(a, b, dims=NN):
    a_high, a_low = split(a)
    b_high, b_low = split(b)
    return dot(a_high, b_high, dims) + (dot(a_high, b_low, dims) + dot(a_low, b_high, dims))


def mm1(a, b, dims=NN):
    return dot(a.astype(BF16), b.astype(BF16), dims)


def exact(a, b, dims=NN):
    return lax.dot_general(
        a, b, (dims, ((), ())), precision=lax.Precision.HIGHEST, preferred_element_type=F32
    )


def rows_cols():
    rows = lax.broadcasted_iota(jnp.int32, (BLOCK, BLOCK), 0)
    cols = lax.broadcasted_iota(jnp.int32, (BLOCK, BLOCK), 1)
    return rows, cols


def softplus(x):
    return jnp.maximum(x, 0.0) + jnp.log1p(jnp.exp(-jnp.abs(x)))


def unit(raw):
    scale = lax.rsqrt(jnp.sum(raw * raw, axis=-1, keepdims=True) + EPS)
    return raw * scale, scale


def invert(systems):
    rows, cols = rows_cols()
    eye = (rows == cols).astype(F32)
    first = ((rows >> 1) == (cols >> 1)) & (rows > cols)
    inverses = [eye - jnp.where(first, n, 0.0) for n in systems]
    for level in range(1, 7):
        pick = ((rows >> (level + 1)) == (cols >> (level + 1))) & (
            (rows >> level) > (cols >> level)
        )
        halves = [mm3(jnp.where(pick, n, 0.0), x) for n, x in zip(systems, inverses)]
        inverses = [x - mm3(x, h) for x, h in zip(inverses, halves)]
    return inverses


def gates(side, reset, scale_row, bias_row, heads):
    rows, cols = rows_cols()
    beta = jax.nn.sigmoid(side + bias_row)
    decay = -scale_row * softplus(side)
    lower = (rows >= cols).astype(F32)
    summed = exact(lower, jnp.where(cols == 2 * heads, reset, decay))
    flipped = summed.T
    doc = summed[:, 2 * heads : 2 * heads + 1]
    doc_row = flipped[2 * heads : 2 * heads + 1, :]
    same = (doc == doc_row) & (rows >= cols)
    start = jnp.where(doc == 0.0, jnp.exp(summed), 0.0)
    last = summed[BLOCK - 1 : BLOCK, :]
    end = jnp.where(
        doc == doc[BLOCK - 1 : BLOCK, :], jnp.exp(jnp.minimum(last - summed, 0.0)), 0.0
    )
    return beta, summed, flipped, same, start, end


def pair_decay(summed, flipped, same, head):
    gap = jnp.minimum(summed[:, head : head + 1] - flipped[head : head + 1, :], 0.0)
    return jnp.where(same, jnp.exp(gap), 0.0)


def mm_wide(a, s, dims=NN):
    s_high, s_low = split(s)
    return dot(a, s_high, dims) + dot(a, s_low, dims)


def greet(peers):
    barrier = pltpu.get_barrier_semaphore()
    for peer in peers:
        pl.semaphore_signal(barrier, inc=1, device_id={"ctx": peer}, device_id_type=MESH)
    pl.semaphore_wait(barrier, len(peers))


def ring_peers():
    me = lax.axis_index("ctx")
    x, y = me // SIDE, lax.rem(me, SIDE)
    row = [x * SIDE + lax.rem(y + d, SIDE) for d in range(1, SIDE)]
    col = [lax.rem(x + d, SIDE) * SIDE + y for d in range(1, SIDE)]
    return x, y, row, col


def each(count, body):
    def step(i, carry):
        body(i)
        return carry

    lax.fori_loop(0, count, step, 0)


def mixer_kernel(
    key_heads,
    repeat,
    x_hbm,
    side_hbm,
    qk_hbm,
    vg_hbm,
    cotangent_hbm,
    out_hbm,
    reset_ref,
    scale_ref,
    bias_ref,
    gain_ref,
    hidden_ref,
    delta_ref,
    x_in,
    side_in,
    qk_in,
    vg_in,
    cotangent_in,
    out_in,
    proj,
    gate,
    up,
    betas,
    starts,
    ends,
    decays,
    inverses,
    scores,
    base,
    weight,
    start_map,
    local_out,
    step_map,
    step_add,
    prefix,
    before,
    grad_out,
    map_total,
    add_total,
    state,
    row_buf,
    col_buf,
    row_grad,
    col_grad,
    load_sem,
    send_sem,
    recv_sem,
):
    heads = key_heads * repeat
    blocks = x_in.shape[0] // BLOCK
    key_width, value_width = key_heads * DK, heads * DV
    value_at = 2 * key_width
    gate_at = value_at + value_width
    side_at = gate_at + value_width
    rows, cols = rows_cols()
    eye = (rows == cols).astype(F32)

    loads = [
        pltpu.make_async_copy(src, dst, load_sem.at[i])
        for i, (src, dst) in enumerate(
            [
                (x_hbm, x_in),
                (side_hbm, side_in),
                (qk_hbm, qk_in),
                (vg_hbm.at[0], vg_in.at[0]),
                (vg_hbm.at[1], vg_in.at[1]),
                (cotangent_hbm, cotangent_in),
                (out_hbm, out_in),
            ]
        )
    ]
    for load in loads:
        load.start()
    x, y, row, col = ring_peers()
    greet(row + col)

    def span(b):
        return pl.ds(pl.multiple_of(b * BLOCK, BLOCK), BLOCK)

    def head_cols(h, base_at=0):
        return slice(base_at + h * DV, base_at + (h + 1) * DV)

    for h in range(heads):
        map_total[h] = eye
        add_total[h] = jnp.zeros_like(eye)
    for load in loads[:4]:
        load.wait()

    def make_terms(b):
        at = span(b)
        left = x_in[at, :]
        proj[at, :key_width] = dot(left, qk_in[0], NN)
        proj[at, key_width:value_at] = dot(left, qk_in[1], NN)
        proj[at, value_at:gate_at] = dot(left, vg_in[0], NN)
        side = dot(left, side_in[...], NN)
        proj[at, gate_at:] = side
        beta, summed, flipped, same, start, end = gates(
            side, reset_ref[at, :], scale_ref[...], bias_ref[...], heads
        )
        betas[b] = beta
        starts[b] = start
        ends[b] = end
        systems, keys = [], []
        for kh in range(key_heads):
            q, _ = unit(proj[at, kh * DK : (kh + 1) * DK])
            q = q * DK ** (-0.5)
            k, _ = unit(proj[at, key_width + kh * DK : key_width + (kh + 1) * DK])
            gram = mm3(k, k, NT)
            cross = mm3(q, k, NT)
            for h in range(kh * repeat, (kh + 1) * repeat):
                decay = pair_decay(summed, flipped, same, h)
                strength = beta[:, heads + h : heads + h + 1]
                systems.append(jnp.where(rows > cols, strength * decay * gram, 0.0))
                decays[b, h] = decay
                scores[b, h] = decay * cross
                start_map[b, h] = start[:, h : h + 1] * q
                keys.append(k)
        solved_by = invert(systems)
        for h in range(heads):
            strength = beta[:, heads + h : heads + h + 1]
            begin = start[:, h : h + 1]
            v = proj[at, head_cols(h, value_at)]
            right = jnp.concatenate([strength * v, (strength * begin) * keys[h]], axis=1)
            solved = mm3(solved_by[h], right)
            state_map = mm3(end[:, h : h + 1] * keys[h], solved, TN)
            a = begin[BLOCK - 1 : BLOCK, :] * eye - state_map[:, DV:]
            add = state_map[:, :DV]
            inverses[b, h] = solved_by[h]
            base[b, h] = solved[:, :DV]
            weight[b, h] = solved[:, DV:]
            step_map[b, h] = a
            step_add[b, h] = add
            prefix[b, h] = map_total[h]
            both = mm3(a, jnp.concatenate([map_total[h], add_total[h]], axis=1))
            map_total[h] = both[:, :DK]
            add_total[h] = both[:, DK:] + add

    each(blocks, make_terms)

    def exchange(phase, h, buffer, slot, at, peers):
        copies = [
            pltpu.make_async_remote_copy(
                src_ref=buffer.at[(slot, *at)],
                dst_ref=buffer.at[(slot, *at)],
                send_sem=send_sem.at[phase, h, d],
                recv_sem=recv_sem.at[phase, h, d],
                device_id={"ctx": peer},
                device_id_type=MESH,
            )
            for d, peer in enumerate(peers)
        ]
        for copy in copies:
            copy.start()
        return copies

    sent = []
    row_copies, col_copies = [], []
    for h in range(heads):
        row_buf[y, h, 0] = map_total[h].astype(BF16)
        row_buf[y, h, 1] = add_total[h].astype(BF16)
        row_copies.append(exchange(0, h, row_buf, y, (h,), row))

    for load in loads[4:]:
        load.wait()

    def make_local(b):
        at = span(b)
        gate[at, :] = dot(x_in[at, :], vg_in[1], NN)
        up[at, :] = dot(cotangent_in[at, :], out_in[...], NT)
        for h in range(heads):
            local = mm3(
                scores[b, h], jnp.concatenate([base[b, h], weight[b, h]], axis=1)
            )
            local_out[b, h] = local[:, :DV]
            start_map[b, h] = start_map[b, h] - local[:, DV:]

    each(blocks, make_local)

    for h in range(heads):
        for copy in row_copies[h]:
            copy.wait_recv()
        a = row_buf[0, h, 0].astype(F32)
        add = row_buf[0, h, 1].astype(F32)
        for i in range(1, SIDE):
            both = mm_wide(row_buf[i, h, 0], jnp.concatenate([a, add], axis=1))
            a = both[:, :DK]
            add = both[:, DK:] + row_buf[i, h, 1].astype(F32)
        col_buf[x, h, 0] = a.astype(BF16)
        col_buf[x, h, 1] = add.astype(BF16)
        col_copies.append(exchange(1, h, col_buf, x, (h,), col))
    for h in range(heads):
        for copy in col_copies[h]:
            copy.wait_recv()
    for i in range(SIDE - 1):
        for h in range(heads):
            s = jnp.zeros((DK, DV), F32) if i == 0 else state[h]
            new = mm_wide(col_buf[i, h, 0], s) + col_buf[i, h, 1].astype(F32)
            state[h] = jnp.where(i < x, new, s)
    for i in range(SIDE - 1):
        for h in range(heads):
            s = state[h]
            new = mm_wide(row_buf[i, h, 0], s) + row_buf[i, h, 1].astype(F32)
            state[h] = jnp.where(i < y, new, s)

    gain = gain_ref[...]
    for h in range(heads):
        add_total[h] = jnp.zeros_like(eye)

    def go_forward(b):
        at = span(b)
        for h in range(heads):
            s = state[h]
            before[b, h] = s
            stacked = mm3(
                jnp.concatenate([step_map[b, h], start_map[b, h], weight[b, h]], axis=0), s
            )
            state[h] = stacked[:DK] + step_add[b, h]
            out = stacked[DK : DK + BLOCK] + local_out[b, h]
            base[b, h] = base[b, h] - stacked[DK + BLOCK :]
            scale = lax.rsqrt(jnp.mean(out * out, axis=-1, keepdims=True) + EPS)
            normed = out * scale
            g = gate[at, head_cols(h)]
            above = up[at, head_cols(h)]
            opened = jax.nn.sigmoid(g)
            swish = g * opened
            hidden_ref[at, head_cols(h)] = (normed * gain * swish).astype(BF16)
            delta_ref[at, head_cols(h, gate_at)] = (
                above * normed * gain * (opened * (1.0 + g * (1.0 - opened)))
            ).astype(BF16)
            d_normed = above * gain * swish
            d_out = scale * (
                d_normed - normed * jnp.mean(d_normed * normed, axis=-1, keepdims=True)
            )
            grad_out[b, h] = d_out
            local = mm3(start_map[b, h], d_out, TN)
            add_total[h] += mm3(prefix[b, h], local, TN)

    each(blocks, go_forward)

    row_copies, col_copies = [], []
    for h in range(heads):
        row_grad[y, h] = add_total[h].astype(BF16)
        row_copies.append(exchange(2, h, row_grad, y, (h,), row))

    value, early_dq, early_dk, early_value = base, step_map, step_add, local_out

    def go_early(b):
        at = span(b)
        for kh in range(key_heads):
            q, _ = unit(proj[at, kh * DK : (kh + 1) * DK])
            q = q * DK ** (-0.5)
            k, _ = unit(proj[at, key_width + kh * DK : key_width + (kh + 1) * DK])
            for h in range(kh * repeat, (kh + 1) * repeat):
                d_out = grad_out[b, h]
                d_scores = mm3(d_out, value[b, h], NT) * decays[b, h]
                early_dq[b, h] = mm3(d_scores, k) + starts[b][:, h : h + 1] * mm3(
                    d_out, before[b, h], NT
                )
                early_dk[b, h] = mm3(d_scores, q, TN)
                early_value[b, h] = mm3(scores[b, h], d_out, TN)

    each(blocks, go_early)

    for h in range(heads):
        for copy in row_copies[h]:
            copy.wait_recv()
        g = row_grad[SIDE - 1, h].astype(F32)
        for i in range(SIDE - 2, -1, -1):
            g = mm_wide(row_buf[i, h, 0], g, TN) + row_grad[i, h].astype(F32)
        col_grad[x, h] = g.astype(BF16)
        col_copies.append(exchange(3, h, col_grad, x, (h,), col))
    for h in range(heads):
        for copy in col_copies[h]:
            copy.wait_recv()
    for i in range(SIDE - 1, 0, -1):
        for h in range(heads):
            g = jnp.zeros((DK, DV), F32) if i == SIDE - 1 else state[h]
            new = mm_wide(col_buf[i, h, 0], g, TN) + col_grad[i, h].astype(F32)
            state[h] = jnp.where(i > x, new, g)
    for i in range(SIDE - 1, 0, -1):
        for h in range(heads):
            g = state[h]
            new = mm_wide(row_buf[i, h, 0], g, TN) + row_grad[i, h].astype(F32)
            state[h] = jnp.where(i > y, new, g)

    at_last = rows[:, :1] == BLOCK - 1
    lower = (rows >= cols).astype(F32)

    def go_backward(step):
        b = blocks - 1 - step
        at = span(b)
        beta, start, end = betas[b], starts[b], ends[b]
        d_summed = jnp.zeros((BLOCK, LANES), F32)
        d_strength = jnp.zeros((BLOCK, LANES), F32)
        for kh in range(key_heads):
            q_unit, q_scale = unit(proj[at, kh * DK : (kh + 1) * DK])
            q = q_unit * DK ** (-0.5)
            k, k_scale = unit(proj[at, key_width + kh * DK : key_width + (kh + 1) * DK])
            dq_sum = jnp.zeros((BLOCK, DK), F32)
            dk_sum = jnp.zeros((BLOCK, DK), F32)
            for h in range(kh * repeat, (kh + 1) * repeat):
                strength = beta[:, heads + h : heads + h + 1]
                begin = start[:, h : h + 1]
                finish_by = end[:, h : h + 1]
                v = proj[at, head_cols(h, value_at)]
                s = before[b, h]
                ds = state[h]
                total = begin[BLOCK - 1 : BLOCK, :]
                d_value = early_value[b, h] + finish_by * mm3(k, ds)
                d_right = mm3(inverses[b, h], d_value, TN)
                d_system = jnp.where(
                    rows > cols, -mm3(d_right, value[b, h], NT) * decays[b, h], 0.0
                )
                row_part = mm3(d_system, k) - begin * mm3(d_right, s, NT)
                last_part = finish_by * mm3(value[b, h], ds, NT)
                dk_col = early_dk[b, h] + mm3(strength * d_system, k, TN) + last_part
                dk_row = strength * row_part
                dq = early_dq[b, h]
                state[h] = total * ds + mm3(
                    jnp.concatenate([begin * q, (strength * begin) * k], axis=0),
                    jnp.concatenate([grad_out[b, h], -d_right], axis=0),
                    TN,
                )
                dq_sum += dq
                dk_sum += dk_row + dk_col
                d_beta = jnp.sum(k * row_part + v * d_right, axis=-1, keepdims=True)
                d_cum = jnp.sum(q * dq + k * (dk_row - dk_col), axis=-1, keepdims=True)
                d_last = jnp.sum(k * last_part) + jnp.sum(s * ds * total)
                d_cum = d_cum + jnp.where(at_last, d_last, 0.0)
                d_summed = d_summed + jnp.where(cols == h, d_cum, 0.0)
                d_strength = d_strength + jnp.where(cols == heads + h, d_beta, 0.0)
                delta_ref[at, head_cols(h, value_at)] = (strength * d_right).astype(BF16)
            dq_raw = (q_scale * DK ** (-0.5)) * (
                dq_sum - q_unit * jnp.sum(q_unit * dq_sum, axis=-1, keepdims=True)
            )
            dk_raw = k_scale * (dk_sum - k * jnp.sum(k * dk_sum, axis=-1, keepdims=True))
            delta_ref[at, kh * DK : (kh + 1) * DK] = dq_raw.astype(BF16)
            delta_ref[at, key_width + kh * DK : key_width + (kh + 1) * DK] = dk_raw.astype(BF16)
        d_decay = exact(lower, d_summed, TN)
        side = proj[at, gate_at:]
        d_side = (
            d_decay * (-scale_ref[...]) * jax.nn.sigmoid(side)
            + d_strength * beta * (1.0 - beta)
        )
        delta_ref[at, side_at:] = d_side.astype(BF16)

    each(blocks, go_backward)
    for phase, (buffer, at, peers) in enumerate(
        ((row_buf, y, row), (col_buf, x, col), (row_grad, y, row), (col_grad, x, col))
    ):
        for h in range(heads):
            for d, peer in enumerate(peers):
                pltpu.make_async_remote_copy(
                    src_ref=buffer.at[at, h],
                    dst_ref=buffer.at[at, h],
                    send_sem=send_sem.at[phase, h, d],
                    recv_sem=recv_sem.at[phase, h, d],
                    device_id={"ctx": peer},
                    device_id_type=MESH,
                ).wait_send()


def mix(inputs, side, qk, vg, cotangent, out_weight, resets, scale, bias, gain):
    tokens, width = inputs.shape
    key_width, value_width = qk.shape[2], vg.shape[2]
    heads, key_heads = value_width // DV, key_width // DK
    blocks = tokens // BLOCK
    columns = 2 * (key_width + value_width) + LANES
    hbm, vmem = pl.BlockSpec(memory_space=pl.ANY), pl.BlockSpec(memory_space=pltpu.VMEM)
    square = pltpu.VMEM((blocks, heads, BLOCK, BLOCK), F32)
    lanes = pltpu.VMEM((blocks, BLOCK, LANES), F32)
    one = pltpu.VMEM((heads, DK, DV), F32)
    return pl.pallas_call(
        functools.partial(mixer_kernel, key_heads, heads // key_heads),
        out_shape=[
            jax.ShapeDtypeStruct((tokens, value_width), BF16),
            jax.ShapeDtypeStruct((tokens, columns), BF16),
        ],
        in_specs=[hbm] * 6 + [vmem] * 4,
        out_specs=[vmem] * 2,
        scratch_shapes=[
            pltpu.VMEM(inputs.shape, BF16),
            pltpu.VMEM(side.shape, BF16),
            pltpu.VMEM(qk.shape, BF16),
            pltpu.VMEM(vg.shape, BF16),
            pltpu.VMEM(cotangent.shape, BF16),
            pltpu.VMEM(out_weight.shape, BF16),
            pltpu.VMEM((tokens, 2 * key_width + value_width + LANES), F32),
            pltpu.VMEM((tokens, value_width), F32),
            pltpu.VMEM((tokens, value_width), F32),
            lanes,
            lanes,
            lanes,
            *[square] * 12,
            *[one] * 3,
            *[pltpu.VMEM((SIDE, heads, 2, DK, DV), BF16)] * 2,
            *[pltpu.VMEM((SIDE, heads, DK, DV), BF16)] * 2,
            pltpu.SemaphoreType.DMA((7,)),
            pltpu.SemaphoreType.DMA((4, heads, SIDE - 1)),
            pltpu.SemaphoreType.DMA((4, heads, SIDE - 1)),
        ],
        compiler_params=pltpu.CompilerParams(
            collective_id=0, has_side_effects=True, vmem_limit_bytes=VMEM_LIMIT
        ),
        name="mixer",
    )(inputs, side, qk, vg, cotangent, out_weight, resets, scale, bias, gain)


def add_into(target, index, *others):
    total = target[index].astype(F32)
    for ref, at in others:
        total += ref[at].astype(F32)
    target[index] = total.astype(BF16)


def around(position):
    return (
        lax.rem(position + 1, SIDE),
        lax.rem(position + SIDE - 1, SIDE),
        lax.rem(position + 2, SIDE),
    )


def finish_kernel(
    parts,
    split_at,
    x_ref,
    delta_ref,
    side_weight_ref,
    qk_weight_ref,
    vg_weight_ref,
    hidden_ref,
    out_weight_ref,
    cotangent_ref,
    mixed_ref,
    grad_ref,
    qk_ref,
    vg_ref,
    db_ref,
    out_ref,
    one,
    two,
    one_first,
    two_first,
    one_second,
    two_second,
    one_third,
    two_third,
    one_fourth,
    two_fourth,
    away,
    kept,
    core_in,
    z_first,
    z_second,
    send_sem,
    recv_sem,
):
    me = lax.axis_index("ctx")
    mine = lax.axis_index("head")
    x, y = me // SIDE, lax.rem(me, SIDE)
    z, core = mine // 2, lax.rem(mine, 2)
    x_up, x_down, x_far = around(x)
    y_up, y_down, y_far = around(y)
    z_up, z_down, z_far = around(z)
    peers = [
        {"ctx": x * SIDE + y_up},
        {"ctx": x * SIDE + y_down},
        {"ctx": x_up * SIDE + y},
        {"ctx": x_down * SIDE + y},
        {"head": z * 2 + 1 - core},
        {"head": z_up * 2 + core},
        {"head": z_down * 2 + core},
    ]
    barrier = pltpu.get_barrier_semaphore()
    for peer in peers:
        pl.semaphore_signal(barrier, inc=1, device_id=peer, device_id_type=MESH)
    pl.semaphore_wait(barrier, len(peers))
    y_next, y_prev, x_next, x_prev, pair, z_next, z_prev = peers
    used = []

    def send(src, dst, peer):
        slot = len(used)
        copy = pltpu.make_async_remote_copy(
            src_ref=src,
            dst_ref=dst,
            send_sem=send_sem.at[slot],
            recv_sem=recv_sem.at[slot],
            device_id=peer,
            device_id_type=MESH,
        )
        copy.start()
        used.append(copy)
        return copy

    width = grad_ref.shape[1]
    rows = qk_ref.shape[1]

    def mixed_block(z_to, core_to, target):
        at = pl.multiple_of((z_to * 2 + core_to) * width, width)
        target[0, z_to] = dot(
            hidden_ref[...], out_weight_ref[:, pl.ds(at, width)], NN
        ).astype(BF16)

    def grad_block(z_to, core_to, target):
        at = pl.multiple_of((z_to * 2 + core_to) * width, width)
        total = 0.0
        start = 0
        for ref in (qk_weight_ref, vg_weight_ref):
            size = ref.shape[2]
            for s in range(2):
                total += dot(
                    delta_ref[:, start : start + size], ref[s, pl.ds(at, width), :], NT
                )
                start += size
        total += dot(delta_ref[:, start:], side_weight_ref[pl.ds(at, width), :], NT)
        target[1, z_to] = total.astype(BF16)

    def term_block(x_to, y_to):
        at = pl.multiple_of((x_to * SIDE + y_to) * rows, rows)
        term = dot(x_ref[:, pl.ds(at, rows)], delta_ref[...], TN).astype(BF16)
        one[y_to, x_to] = term[:, :split_at]
        rest = term.shape[1] - split_at
        two[x_to, y_to, :, :rest] = term[:, split_at:]
        two[x_to, y_to, :, rest:] = dot(
            cotangent_ref[:, pl.ds(at, rows)], hidden_ref[...], TN
        ).astype(BF16)

    each(SIDE, lambda i: term_block(i, y_far))
    one_a = send(one.at[y_far, pl.ds(0, 2)], one_first.at[0], y_next)
    one_b = send(one.at[y_far, pl.ds(2, 2)], one_first.at[1], y_prev)
    each(SIDE - 1, lambda i: term_block(x_far, lax.rem(y_far + 1 + i, SIDE)))
    two_a = send(two.at[x_far, pl.ds(0, 2)], two_first.at[0], x_next)
    two_b = send(two.at[x_far, pl.ds(2, 2)], two_first.at[1], x_prev)
    each(SIDE, lambda i: mixed_block(i, 1 - core, away))
    mixed_pair = send(away.at[0], core_in.at[0], pair)
    each(
        (SIDE - 1) * (SIDE - 1),
        lambda i: term_block(
            lax.rem(x_far + 1 + i // (SIDE - 1), SIDE),
            lax.rem(y_far + 1 + lax.rem(i, SIDE - 1), SIDE),
        ),
    )
    each(SIDE, lambda i: mixed_block(i, core, kept))

    def second(store, first, second_in, ups, downs, up_peer, down_peer, a, b):
        a.wait_recv()
        each(2, lambda i: add_into(store, (ups, i), (first, (0, i))))
        up = send(store.at[ups], second_in.at[0], up_peer)
        b.wait_recv()
        each(2, lambda i: add_into(store, (downs, 2 + i), (first, (1, i))))
        down = send(store.at[downs], second_in.at[1], down_peer)
        return up, down

    one_c = second(one, one_first, one_second, y_up, y_down, y_next, y_prev, one_a, one_b)
    two_c = second(two, two_first, two_second, x_up, x_down, x_next, x_prev, two_a, two_b)

    half = grad_ref.shape[0] // 2

    def z_start(k, arrived):
        arrived.wait_recv()
        add_into(kept, (k, z_far), (core_in, (k, z_far)))
        a = send(kept.at[k, z_far, pl.ds(0, half)], z_first.at[k, 0], z_next)
        b = send(kept.at[k, z_far, pl.ds(half, half)], z_first.at[k, 1], z_prev)
        each(
            SIDE - 1,
            lambda i: add_into(
                kept,
                (k, lax.rem(z_far + 1 + i, SIDE)),
                (core_in, (k, lax.rem(z_far + 1 + i, SIDE))),
            ),
        )
        return a, b

    def z_middle(k, pending):
        a, b = pending
        a.wait_recv()
        add_into(kept, (k, z_up, pl.ds(0, half)), (z_first, (k, 0)))
        up = send(kept.at[k, z_up], z_second.at[k, 0], z_next)
        b.wait_recv()
        add_into(kept, (k, z_down, pl.ds(half, half)), (z_first, (k, 1)))
        down = send(kept.at[k, z_down], z_second.at[k, 1], z_prev)
        return up, down

    def z_end(k, pending, out_ref):
        for copy in pending:
            copy.wait_recv()
        out_ref[...] = (
            kept[k, z].astype(F32) + z_second[k, 0].astype(F32) + z_second[k, 1].astype(F32)
        ).astype(BF16)

    mixed_z = z_start(0, mixed_pair)
    each(SIDE, lambda i: grad_block(i, 1 - core, away))
    grad_pair = send(away.at[1], core_in.at[1], pair)
    mixed_z = z_middle(0, mixed_z)
    each(SIDE, lambda i: grad_block(i, core, kept))
    grad_z = z_start(1, grad_pair)
    z_end(0, mixed_z, mixed_ref)
    grad_z = z_middle(1, grad_z)

    def third(store, second_in, third_in, at, far, far_next, far_prev, pending):
        for copy in pending:
            copy.wait_recv()
        add_into(store, (at, far), (second_in, (0, far)), (second_in, (1, far)))
        n = rows // 2
        a = send(store.at[at, far, pl.ds(0, n)], third_in.at[0], far_next)
        b = send(store.at[at, far, pl.ds(n, n)], third_in.at[1], far_prev)
        for i in range(1, SIDE):
            other = lax.rem(far + i, SIDE)
            add_into(store, (at, other), (second_in, (0, other)), (second_in, (1, other)))
        return a, b

    def fourth(store, third_in, fourth_in, at, ups, downs, up_peer, down_peer, pending):
        a, b = pending
        n = rows // 2
        a.wait_recv()
        add_into(store, (at, ups, pl.ds(0, n)), (third_in, 0))
        up = send(store.at[at, ups], fourth_in.at[0], up_peer)
        b.wait_recv()
        add_into(store, (at, downs, pl.ds(n, n)), (third_in, 1))
        down = send(store.at[at, downs], fourth_in.at[1], down_peer)
        return up, down

    two_d = third(two, two_second, two_third, x, y_far, y_next, y_prev, two_c)
    one_d = third(one, one_second, one_third, y, x_far, x_next, x_prev, one_c)
    two_e = fourth(two, two_third, two_fourth, x, y_up, y_down, y_next, y_prev, two_d)
    one_e = fourth(one, one_third, one_fourth, y, x_up, x_down, x_next, x_prev, one_d)
    z_end(1, grad_z, grad_ref)

    def total(store, fourth_in, at, to, pending):
        for copy in pending:
            copy.wait_recv()
        return (
            store[at, to].astype(F32) + fourth_in[0].astype(F32) + fourth_in[1].astype(F32)
        )

    sums = (total(two, two_fourth, x, y, two_e), total(one, one_fourth, y, x, one_e))
    for ref, s, start, size in parts:
        if start < split_at:
            ref_value = sums[1][:, start : start + size]
        else:
            ref_value = sums[0][:, start - split_at : start - split_at + size]
        (qk_ref, vg_ref, db_ref)[ref][s] = ref_value
    out_ref[...] = sums[0][:, -out_ref.shape[0] :].T
    for copy in used:
        copy.wait_send()


def finish(inputs, delta, side, qk, vg, hidden, out_weight, cotangent):
    tokens, width = inputs.shape
    heads, key_heads = vg.shape[2] // DV, qk.shape[2] // DK
    columns = delta.shape[1] + hidden.shape[1]
    key_width, value_width = key_heads * DK, heads * DV
    side_at = 2 * (key_width + value_width)
    parts = [
        (0, 0, 0, key_width),
        (0, 1, key_width, key_width),
        (1, 0, 2 * key_width, value_width),
        (1, 1, 2 * key_width + value_width, value_width),
        (2, 0, side_at, heads),
        (2, 1, side_at + heads, heads),
    ]
    split_at = 2 * key_width + value_width
    rows = width // (SIDE * SIDE)
    block = width // (2 * SIDE)
    sizes = (split_at, columns - split_at)
    half = tokens // 2

    def both(*shape):
        return [pltpu.VMEM((*shape, n), BF16) for n in sizes]

    vmem = pl.BlockSpec(memory_space=pltpu.VMEM)
    return pl.pallas_call(
        functools.partial(finish_kernel, parts, split_at),
        out_shape=[
            jax.ShapeDtypeStruct((tokens, block), BF16),
            jax.ShapeDtypeStruct((tokens, block), BF16),
            jax.ShapeDtypeStruct((2, rows, key_width), F32),
            jax.ShapeDtypeStruct((2, rows, value_width), F32),
            jax.ShapeDtypeStruct((2, rows, heads), F32),
            jax.ShapeDtypeStruct((value_width, rows), F32),
        ],
        in_specs=[vmem] * 8,
        out_specs=[vmem] * 6,
        scratch_shapes=[
            *both(SIDE, SIDE, rows),
            *both(2, 2, rows),
            *both(2, SIDE, rows),
            *both(2, rows // 2),
            *both(2, rows),
            pltpu.VMEM((2, SIDE, tokens, block), BF16),
            pltpu.VMEM((2, SIDE, tokens, block), BF16),
            pltpu.VMEM((2, SIDE, tokens, block), BF16),
            pltpu.VMEM((2, 2, half, block), BF16),
            pltpu.VMEM((2, 2, tokens, block), BF16),
            pltpu.SemaphoreType.DMA((26,)),
            pltpu.SemaphoreType.DMA((26,)),
        ],
        compiler_params=pltpu.CompilerParams(
            collective_id=2, has_side_effects=True, vmem_limit_bytes=FINISH_LIMIT
        ),
        name="finish",
    )(inputs, delta, side, qk, vg, hidden, out_weight, cotangent)


FINISH_LIMIT = 56 * 2**20
VMEM_LIMIT = 48 * 2**20


def body(
    inputs,
    query_key_weight,
    value_gate_weight,
    decay_beta_weight,
    beta_bias,
    decay_scale,
    norm_gain,
    out_weight,
    boundaries,
    grad_mixed,
):
    heads = beta_bias.shape[0]
    side = jnp.pad(
        jnp.concatenate([decay_beta_weight[0], decay_beta_weight[1]], axis=1),
        ((0, 0), (0, LANES - 2 * heads)),
    )
    resets = boundaries.astype(F32)[:, None]
    scale_row = jnp.pad(decay_scale, (0, LANES - heads))[None]
    bias_row = jnp.pad(beta_bias, (heads, LANES - 2 * heads))[None]
    hidden, delta = mix(
        inputs,
        side,
        query_key_weight,
        value_gate_weight,
        grad_mixed,
        out_weight,
        resets,
        scale_row,
        bias_row,
        norm_gain[None],
    )
    mixed, grad_inputs, grad_query_key, grad_value_gate, grad_decay_beta, grad_out_weight = finish(
        inputs, delta, side, query_key_weight, value_gate_weight, hidden, out_weight, grad_mixed
    )
    return (
        mixed,
        grad_inputs,
        grad_query_key,
        grad_value_gate,
        grad_decay_beta,
        grad_out_weight,
    )


def solution(mesh):
    in_specs = (
        P("ctx", None),
        P(None, None, "head"),
        P(None, None, "head"),
        P(None, None, "head"),
        P("head"),
        P("head"),
        P(),
        P("head", None),
        P("ctx"),
        P("ctx", None),
    )
    out_specs = (
        P("ctx", "head"),
        P("ctx", "head"),
        P(None, "ctx", "head"),
        P(None, "ctx", "head"),
        P(None, "ctx", "head"),
        P("head", "ctx"),
    )
    return jax.shard_map(body, mesh=mesh, in_specs=in_specs, out_specs=out_specs, check_vma=False)
```

time: 253 us -> 173 us (0.68)
  local copies, waits for them, and re-layouts: 50.2 us -> 15.5 us
  Pallas kernels: 172 us -> 155 us
  matrix products: 14.3 us -> 0 us
  between operations: 14.2 us -> 0.72 us
    unnamed x63 -> x17, local copies, waits for them, and re-layouts: 32.1 us -> 11.9 us
    pallas_call x5 -> x1, Pallas kernels: 108 us -> 89.3 us  [mix(): pl.pallas_call(functools.partial(mixer_kernel, key_heads, heads // key_he...]
    dot_general x3 -> x0, matrix products: 14.3 us -> none  [the longest x1 9.34 us: body(): proj = jnp.dot(inputs, weights, preferred_element_type=F32)]
    concatenate x1, local copies, waits for them, and re-layouts: 11 us -> 0.28 us  [body(): jnp.concatenate([decay_beta_weight[0], decay_beta_weight[1]], axis=1)]
    squeeze x2 -> x1, local copies, waits for them, and re-layouts: 5.21 us -> 0.75 us  [body(): decay_beta_weight[0]]
  transfers between devices with their start and end apart: 1 -> 0, of which waited for: 0 -> 0; matrix products, arithmetic and copies ran while one was open for 1% -> 0% of each run, Pallas kernels for 41% -> 0%
where the time goes in v3:
time: 173 us; the launch traced here: 172 us
  Pallas kernels  155 us (90%)
  local copies, waits for them, and re-layouts  15.5 us (9%)
    pallas_call x1, Pallas kernels, mix(): pl.pallas_call(functools.partial(mixer_kernel, key_heads, heads // key_he...  89.3 us
    pallas_call x1, Pallas kernels, finish(): pl.pallas_call(functools.partial(finish_kernel, parts, split_at), out_sha...  65.8 us
    unnamed x17, local copies, waits for them, and re-layouts  11.9 us

profile of v3, /device:TPU:0, one launch (start us, length us, event | category | flops | bytes accessed | tf_op | source)
XLA Modules:
  0.0 172.0 jit_solution(16548694875117883255)
XLA Ops:
  0.6 0.7 pad_bitcast_fusion
  1.4 0.7 convert_element_type.9
  2.1 0.7 slice_bitcast_fusion.1
  2.8 0.1 copy.24.reset_ref
  3.0 0.3 copy.23
  3.3 0.1 pad.12.side_hbm.side_weight_ref
  3.4 0.0 copy-start
  3.4 1.6 copy-done
  5.0 0.0 copy-start.4
  5.0 0.7 copy-done.4
  5.6 0.0 copy-start.1
  5.6 89.3 %mixer.1 = (bf16[512,512]{1,0:T(8,128)(2,1)S(1)}, bf16[512,1664]{1,0:T(8,128)(2,1)S(1)}) custom-call(bf16[512,2048]{1,0:T(8,128)(2,1)S(1)} %copy-done, bf16[2048,128]{1,0:T(8,128)(2,1)S(1)} %pad.12.side_hbm.side_weight_ref, bf16[2,2048,256]{2,1,0:T(8,128)(2,1)} %qk_weight_ref.1, bf16[2,2048,512]{2,1,0:T(8,128)(2,1)} %vg_weight_ref.1, ...), custom_call_target="tpu_custom_call" | custom-call | tf_op jit(solution)/shard_map/mixer/pallas_call | solution.py:504
  95.0 0.0 copy-done.1
  95.0 0.0 copy-start.2
  95.0 1.2 copy-done.2
  96.2 0.0 copy-start.3
  96.2 0.8 copy-done.3
  97.0 65.8 %finish.1 = (bf16[512,256]{1,0:T(8,128)(2,1)}, bf16[512,256]{1,0:T(8,128)(2,1)}, f32[2,128,256]{2,1,0:T(8,128)}, f32[2,128,512]{2,1,0:T(8,128)}, f32[2,128,4]{2,1,0:T(8,128)}, /*index=5*/f32[512,128]{1,0:T(8,128)}) custom-call(bf16[512,2048]{1,0:T(8,128)(2,1)} %x_ref.1, bf16[512,1664]{1,0:T(8,128)(2,1)} %copy-done.2, bf16[2048,128]{1,0:T(8,128)(2,1)} %copy-done.1, ...), custom_call_target="tpu_custom_call" | custom-call | tf_op jit(solution)/shard_map/finish/pallas_call | solution.py:804
  162.8 0.0 copy-start.5
  162.8 1.6 copy.25
  164.5 1.7 copy.31
  166.1 1.7 copy.32
  167.8 1.7 copy.33
  169.5 1.9 %copy.34 = f32[2,128,512]{2,1,0:T(8,128)} copy(f32[2,128,512]{2,1,0:T(8,128)} %get-tuple-element.41) | data formatting | bytes 1048576
  171.3 0.0 copy-done.5
  171.3 0.7 copy.35
  (1 shorter events, 0.0 us)
Async XLA Ops:
  3.4 1.6 copy-start
  5.0 0.7 copy-start.4
  5.6 89.3 %copy-start.1 = (bf16[2048,128]{1,0:T(8,128)(2,1)}, bf16[2048,128]{1,0:T(8,128)(2,1)S(1)}, u32[]{:S(2)}) copy-start(bf16[2048,128]{1,0:T(8,128)(2,1)S(1)} %pad.12.side_hbm.side_weight_ref) | copy-start | bytes 1572868
  95.0 1.2 copy-start.2
  96.2 0.8 copy-start.3
  162.8 8.5 %copy-start.5 = (f32[512,128]{1,0:T(8,128)S(1)}, f32[512,128]{1,0:T(8,128)}, u32[]{:S(2)}) copy-start(f32[512,128]{1,0:T(8,128)} %get-tuple-element.43) | copy-start | bytes 786436

commit v4 on v3

--- a/solution.py
+++ b/solution.py
@@ -107,7 +107,7 @@
 def greet(peers):
     barrier = pltpu.get_barrier_semaphore()
     for peer in peers:
-        pl.semaphore_signal(barrier, inc=1, device_id={"ctx": peer}, device_id_type=MESH)
+        pl.semaphore_signal(barrier, inc=1, device_id=peer, device_id_type=MESH)
     pl.semaphore_wait(barrier, len(peers))
 
 
@@ -125,6 +125,160 @@
         return carry
 
     lax.fori_loop(0, count, step, 0)
+
+
+def add_into(target, index, *others):
+    total = target[index].astype(F32)
+    for ref, at in others:
+        total += ref[at].astype(F32)
+    target[index] = total.astype(BF16)
+
+
+def around(position):
+    return (
+        lax.rem(position + 1, SIDE),
+        lax.rem(position + SIDE - 1, SIDE),
+        lax.rem(position + 2, SIDE),
+    )
+
+
+class Links:
+    def __init__(self, send_sem, recv_sem):
+        self.send_sem, self.recv_sem, self.used = send_sem, recv_sem, []
+
+    def send(self, src, dst, peer):
+        slot = len(self.used)
+        copy = pltpu.make_async_remote_copy(
+            src_ref=src,
+            dst_ref=dst,
+            send_sem=self.send_sem.at[slot],
+            recv_sem=self.recv_sem.at[slot],
+            device_id=peer,
+            device_id_type=MESH,
+        )
+        copy.start()
+        self.used.append(copy)
+        return copy
+
+
+class AxesSum:
+    def __init__(self, links, store, buffers, first, second):
+        self.links, self.store = links, store
+        self.arrive, self.merge, self.third_in, self.fourth_in = buffers
+        self.at, self.up_peer, self.down_peer = first
+        self.to, self.next_peer, self.prev_peer = second
+
+    def start(self):
+        _, _, far = around(self.at)
+        self.wait = (
+            self.links.send(self.store.at[far, pl.ds(0, 2)], self.arrive.at[0], self.up_peer),
+            self.links.send(self.store.at[far, pl.ds(2, 2)], self.arrive.at[1], self.down_peer),
+        )
+
+    def second(self):
+        up, down, _ = around(self.at)
+        store, arrive = self.store, self.arrive
+        a, b = self.wait
+        a.wait_recv()
+        each(2, lambda i: add_into(store, (up, i), (arrive, (0, i))))
+        a = self.links.send(store.at[up], self.merge.at[0], self.up_peer)
+        b.wait_recv()
+        each(2, lambda i: add_into(store, (down, 2 + i), (arrive, (1, i))))
+        b = self.links.send(store.at[down], self.merge.at[1], self.down_peer)
+        self.wait = (a, b)
+
+    def third(self):
+        _, _, far = around(self.to)
+        store, merge, at = self.store, self.merge, self.at
+        for copy in self.wait:
+            copy.wait_recv()
+        half = store.shape[2] // 2
+        add_into(store, (at, far), (merge, (0, far)), (merge, (1, far)))
+        a = self.links.send(
+            store.at[at, far, pl.ds(0, half)], self.third_in.at[0], self.next_peer
+        )
+        b = self.links.send(
+            store.at[at, far, pl.ds(half, half)], self.third_in.at[1], self.prev_peer
+        )
+        for i in range(1, SIDE):
+            other = lax.rem(far + i, SIDE)
+            add_into(store, (at, other), (merge, (0, other)), (merge, (1, other)))
+        self.wait = (a, b)
+
+    def fourth(self):
+        up, down, _ = around(self.to)
+        store, at = self.store, self.at
+        half = store.shape[2] // 2
+        a, b = self.wait
+        a.wait_recv()
+        add_into(store, (at, up, pl.ds(0, half)), (self.third_in, 0))
+        a = self.links.send(store.at[at, up], self.fourth_in.at[0], self.next_peer)
+        b.wait_recv()
+        add_into(store, (at, down, pl.ds(half, half)), (self.third_in, 1))
+        b = self.links.send(store.at[at, down], self.fourth_in.at[1], self.prev_peer)
+        self.wait = (a, b)
+
+    def total(self):
+        for copy in self.wait:
+            copy.wait_recv()
+        return (
+            self.store[self.at, self.to].astype(F32)
+            + self.fourth_in[0].astype(F32)
+            + self.fourth_in[1].astype(F32)
+        )
+
+
+class HeadSum:
+    def __init__(self, links, give, keep, buffers, at, pair, next_peer, prev_peer):
+        self.links, self.give, self.keep, self.at = links, give, keep, at
+        self.core_in, self.first_in, self.second_in = buffers
+        self.pair, self.next_peer, self.prev_peer = pair, next_peer, prev_peer
+        self.half = self.core_in.shape[1] // 2
+
+    def order(self):
+        up, down, far = around(self.at)
+        return (far, up, down, self.at)
+
+    def swap(self):
+        self.wait = []
+        for z in self.order():
+            ref, index = self.give(z)
+            self.wait.append(self.links.send(ref.at[index], self.core_in.at[z], self.pair))
+
+    def rows_of(self, z, start):
+        ref, index = self.keep(z)
+        return ref, (*index[:-2], pl.ds(start, self.half), index[-1])
+
+    def start(self):
+        for copy, z in zip(self.wait, self.order()):
+            copy.wait_recv()
+            ref, index = self.keep(z)
+            add_into(ref, index, (self.core_in, z))
+            if copy is self.wait[0]:
+                sent = []
+                for i, peer in enumerate((self.next_peer, self.prev_peer)):
+                    ref, index = self.rows_of(z, i * self.half)
+                    sent.append(self.links.send(ref.at[index], self.first_in.at[i], peer))
+        self.wait = sent
+
+    def middle(self):
+        up, down, _ = around(self.at)
+        sent = []
+        for i, (z, peer) in enumerate(((up, self.next_peer), (down, self.prev_peer))):
+            self.wait[i].wait_recv()
+            ref, index = self.rows_of(z, i * self.half)
+            add_into(ref, index, (self.first_in, i))
+            ref, index = self.keep(z)
+            sent.append(self.links.send(ref.at[index], self.second_in.at[i], peer))
+        self.wait = sent
+
+    def total(self):
+        for copy in self.wait:
+            copy.wait_recv()
+        ref, index = self.keep(self.at)
+        return (
+            ref[index].astype(F32) + self.second_in[0].astype(F32) + self.second_in[1].astype(F32)
+        )
 
 
 def mixer_kernel(
@@ -140,6 +294,9 @@
     scale_ref,
     bias_ref,
     gain_ref,
+    mixed_ref,
+    grad_ref,
+    sum_refs,
     hidden_ref,
     delta_ref,
     x_in,
@@ -173,9 +330,16 @@
     col_buf,
     row_grad,
     col_grad,
+    stores,
+    buffers,
+    away,
+    kept,
+    head_buffers,
     load_sem,
     send_sem,
     recv_sem,
+    link_send_sem,
+    link_recv_sem,
 ):
     heads = key_heads * repeat
     blocks = x_in.shape[0] // BLOCK
@@ -203,7 +367,88 @@
     for load in loads:
         load.start()
     x, y, row, col = ring_peers()
-    greet(row + col)
+    mine = lax.axis_index("head")
+    z, core = mine // 2, lax.rem(mine, 2)
+    z_up, z_down, _ = around(z)
+    pair, z_next, z_prev = z * 2 + 1 - core, z_up * 2 + core, z_down * 2 + core
+    greet([{"ctx": peer} for peer in row + col] + [{"head": p} for p in (pair, z_next, z_prev)])
+
+    links = Links(link_send_sem, link_recv_sem)
+    on_y = (y, {"ctx": row[0]}, {"ctx": row[SIDE - 2]})
+    on_x = (x, {"ctx": col[0]}, {"ctx": col[SIDE - 2]})
+    early = [
+        AxesSum(links, stores[0], buffers[0], on_y, on_x),
+        AxesSum(links, stores[1], buffers[1], on_x, on_y),
+    ]
+    late = [
+        AxesSum(links, stores[2], buffers[2], on_y, on_x),
+        AxesSum(links, stores[3], buffers[3], on_x, on_y),
+    ]
+    block = mixed_ref.shape[1]
+    part = stores[0].shape[2]
+
+    def head_block(z_to, core_to):
+        return pl.ds(pl.multiple_of((z_to * 2 + core_to) * block, block), block)
+
+    def grad_at(core_to):
+        return lambda z_to: (cotangent_in, (slice(None), head_block(z_to, core_to)))
+
+    whole = (slice(None), slice(None))
+    head_peers = (z, {"head": pair}, {"head": z_next}, {"head": z_prev})
+    mixed_sum = HeadSum(
+        links,
+        lambda z_to: (away, (z_to, *whole)),
+        lambda z_to: (kept, (z_to, *whole)),
+        head_buffers[0],
+        *head_peers,
+    )
+    grad_sum = HeadSum(links, grad_at(1 - core), grad_at(core), head_buffers[1], *head_peers)
+
+    def mixed_block(z_to, core_to, target):
+        target[z_to] = dot(
+            hidden_ref[...], out_in[:, head_block(z_to, core_to)], NN
+        ).astype(BF16)
+
+    def grad_block(z_to, core_to):
+        at = head_block(z_to, core_to)
+        total = dot(delta_ref[:, :key_width], qk_in[0, at, :], NT)
+        total += dot(delta_ref[:, key_width:value_at], qk_in[1, at, :], NT)
+        total += dot(delta_ref[:, value_at:gate_at], vg_in[0, at, :], NT)
+        total += dot(delta_ref[:, gate_at:side_at], vg_in[1, at, :], NT)
+        total += dot(delta_ref[:, side_at:], side_in[at, :], NT)
+        cotangent_in[:, at] = total.astype(BF16)
+
+    def early_block(x_to, y_to):
+        at = pl.ds(pl.multiple_of((x_to * SIDE + y_to) * part, part), part)
+        stores[0][y_to, x_to] = dot(x_in[:, at], delta_ref[:, gate_at:side_at], TN).astype(BF16)
+        stores[1][x_to, y_to] = dot(cotangent_in[:, at], hidden_ref[...], TN).astype(BF16)
+
+    def late_block(x_to, y_to):
+        at = pl.ds(pl.multiple_of((x_to * SIDE + y_to) * part, part), part)
+        cut = stores[2].shape[3]
+        term = dot(x_in[:, at], delta_ref[:, :gate_at], TN).astype(BF16)
+        stores[2][y_to, x_to] = term[:, :cut]
+        stores[3][x_to, y_to, :, : gate_at - cut] = term[:, cut:]
+        stores[3][x_to, y_to, :, gate_at - cut :] = dot(
+            x_in[:, at], delta_ref[:, side_at:], TN
+        ).astype(BF16)
+
+    def far_blocks(make):
+        _, _, x_far = around(x)
+        _, _, y_far = around(y)
+        each(SIDE, lambda i: make(i, y_far))
+        each(SIDE - 1, lambda i: make(x_far, lax.rem(y_far + 1 + i, SIDE)))
+
+    def near_blocks(make):
+        _, _, x_far = around(x)
+        _, _, y_far = around(y)
+        each(
+            (SIDE - 1) * (SIDE - 1),
+            lambda i: make(
+                lax.rem(x_far + 1 + i // (SIDE - 1), SIDE),
+                lax.rem(y_far + 1 + lax.rem(i, SIDE - 1), SIDE),
+            ),
+        )
 
     def span(b):
         return pl.ds(pl.multiple_of(b * BLOCK, BLOCK), BLOCK)
@@ -373,6 +618,10 @@
         row_grad[y, h] = add_total[h].astype(BF16)
         row_copies.append(exchange(2, h, row_grad, y, (h,), row))
 
+    far_blocks(early_block)
+    for reduction in early:
+        reduction.start()
+
     value, early_dq, early_dk, early_value = base, step_map, step_add, local_out
 
     def go_early(b):
@@ -391,6 +640,7 @@
                 early_value[b, h] = mm3(scores[b, h], d_out, TN)
 
     each(blocks, go_early)
+    near_blocks(early_block)
 
     for h in range(heads):
         for copy in row_copies[h]:
@@ -400,6 +650,9 @@
             g = mm_wide(row_buf[i, h, 0], g, TN) + row_grad[i, h].astype(F32)
         col_grad[x, h] = g.astype(BF16)
         col_copies.append(exchange(3, h, col_grad, x, (h,), col))
+    each(SIDE, lambda i: mixed_block(i, 1 - core, away))
+    mixed_sum.swap()
+    each(SIDE, lambda i: mixed_block(i, core, kept))
     for h in range(heads):
         for copy in col_copies[h]:
             copy.wait_recv()
@@ -413,6 +666,9 @@
             g = state[h]
             new = mm_wide(row_buf[i, h, 0], g, TN) + row_grad[i, h].astype(F32)
             state[h] = jnp.where(i > y, new, g)
+    for reduction in early:
+        reduction.second()
+    mixed_sum.start()
 
     at_last = rows[:, :1] == BLOCK - 1
     lower = (rows >= cols).astype(F32)
@@ -476,6 +732,35 @@
         delta_ref[at, side_at:] = d_side.astype(BF16)
 
     each(blocks, go_backward)
+
+    for reduction in early:
+        reduction.third()
+    far_blocks(late_block)
+    for reduction in late:
+        reduction.start()
+    mixed_sum.middle()
+    near_blocks(late_block)
+    each(SIDE, lambda i: grad_block(i, 1 - core))
+    grad_sum.swap()
+    for reduction in early:
+        reduction.fourth()
+    for reduction in late:
+        reduction.second()
+    each(SIDE, lambda i: grad_block(i, core))
+    grad_sum.start()
+    mixed_ref[...] = mixed_sum.total().astype(BF16)
+    for reduction, ref in zip(early, sum_refs[:2]):
+        ref[...] = reduction.total()
+    grad_sum.middle()
+    for reduction in late[::-1]:
+        reduction.third()
+    for reduction in late[::-1]:
+        reduction.fourth()
+    grad_ref[...] = grad_sum.total().astype(BF16)
+    for reduction, ref in zip(late[::-1], sum_refs[:1:-1]):
+        ref[...] = reduction.total()
+    for copy in links.used:
+        copy.wait_send()
     for phase, (buffer, at, peers) in enumerate(
         ((row_buf, y, row), (col_buf, x, col), (row_grad, y, row), (col_grad, x, col))
     ):
@@ -491,45 +776,92 @@
                 ).wait_send()
 
 
+VMEM_LIMIT = 63 * 2**20
+LINKS = 48
+
+
 def mix(inputs, side, qk, vg, cotangent, out_weight, resets, scale, bias, gain):
     tokens, width = inputs.shape
     key_width, value_width = qk.shape[2], vg.shape[2]
     heads, key_heads = value_width // DV, key_width // DK
     blocks = tokens // BLOCK
     columns = 2 * (key_width + value_width) + LANES
+    rows = width // (SIDE * SIDE)
+    cut = 2 * key_width + LANES
+    sizes = (value_width, value_width, cut, 2 * key_width + value_width + LANES - cut)
+    head_size = width // (2 * SIDE)
     hbm, vmem = pl.BlockSpec(memory_space=pl.ANY), pl.BlockSpec(memory_space=pltpu.VMEM)
     square = pltpu.VMEM((blocks, heads, BLOCK, BLOCK), F32)
     lanes = pltpu.VMEM((blocks, BLOCK, LANES), F32)
     one = pltpu.VMEM((heads, DK, DV), F32)
+    head_store = pltpu.VMEM((SIDE, tokens, head_size), BF16)
+    buffers = [
+        [
+            pltpu.VMEM((2, 2, rows, n), BF16),
+            pltpu.VMEM((2, SIDE, rows, n), BF16),
+            pltpu.VMEM((2, rows // 2, n), BF16),
+            pltpu.VMEM((2, rows, n), BF16),
+        ]
+        for n in sizes
+    ]
+    head_buffers = [
+        [
+            head_store,
+            pltpu.VMEM((2, tokens // 2, head_size), BF16),
+            pltpu.VMEM((2, tokens, head_size), BF16),
+        ]
+        for _ in range(2)
+    ]
+    scratch = [
+        pltpu.VMEM((tokens, value_width), BF16),
+        pltpu.VMEM((tokens, columns), BF16),
+        pltpu.VMEM(inputs.shape, BF16),
+        pltpu.VMEM(side.shape, BF16),
+        pltpu.VMEM(qk.shape, BF16),
+        pltpu.VMEM(vg.shape, BF16),
+        pltpu.VMEM(cotangent.shape, BF16),
+        pltpu.VMEM(out_weight.shape, BF16),
+        pltpu.VMEM((tokens, 2 * key_width + value_width + LANES), F32),
+        pltpu.VMEM((tokens, value_width), F32),
+        pltpu.VMEM((tokens, value_width), F32),
+        lanes,
+        lanes,
+        lanes,
+        *[square] * 12,
+        *[one] * 3,
+        *[pltpu.VMEM((SIDE, heads, 2, DK, DV), BF16)] * 2,
+        *[pltpu.VMEM((SIDE, heads, DK, DV), BF16)] * 2,
+        [pltpu.VMEM((SIDE, SIDE, rows, n), BF16) for n in sizes],
+        buffers,
+        head_store,
+        head_store,
+        head_buffers,
+        pltpu.SemaphoreType.DMA((7,)),
+        *[pltpu.SemaphoreType.DMA((4, heads, SIDE - 1))] * 2,
+        *[pltpu.SemaphoreType.DMA((LINKS,))] * 2,
+    ]
+    flat, tree = jax.tree.flatten(scratch)
+
+    def kernel(*refs):
+        fixed, rest = refs[:16], refs[16:]
+        mixer_kernel(
+            key_heads,
+            heads // key_heads,
+            *fixed[:12],
+            fixed[12:16],
+            *jax.tree.unflatten(tree, rest),
+        )
+
     return pl.pallas_call(
-        functools.partial(mixer_kernel, key_heads, heads // key_heads),
+        kernel,
         out_shape=[
-            jax.ShapeDtypeStruct((tokens, value_width), BF16),
-            jax.ShapeDtypeStruct((tokens, columns), BF16),
+            jax.ShapeDtypeStruct((tokens, head_size), BF16),
+            jax.ShapeDtypeStruct((tokens, head_size), BF16),
+            *[jax.ShapeDtypeStruct((rows, n), F32) for n in sizes],
         ],
         in_specs=[hbm] * 6 + [vmem] * 4,
-        out_specs=[vmem] * 2,
-        scratch_shapes=[
-            pltpu.VMEM(inputs.shape, BF16),
-            pltpu.VMEM(side.shape, BF16),
-            pltpu.VMEM(qk.shape, BF16),
-            pltpu.VMEM(vg.shape, BF16),
-            pltpu.VMEM(cotangent.shape, BF16),
-            pltpu.VMEM(out_weight.shape, BF16),
-            pltpu.VMEM((tokens, 2 * key_width + value_width + LANES), F32),
-            pltpu.VMEM((tokens, value_width), F32),
-            pltpu.VMEM((tokens, value_width), F32),
-            lanes,
-            lanes,
-            lanes,
-            *[square] * 12,
-            *[one] * 3,
-            *[pltpu.VMEM((SIDE, heads, 2, DK, DV), BF16)] * 2,
-            *[pltpu.VMEM((SIDE, heads, DK, DV), BF16)] * 2,
-            pltpu.SemaphoreType.DMA((7,)),
-            pltpu.SemaphoreType.DMA((4, heads, SIDE - 1)),
-            pltpu.SemaphoreType.DMA((4, heads, SIDE - 1)),
-        ],
+        out_specs=[vmem] * 6,
+        scratch_shapes=flat,
         compiler_params=pltpu.CompilerParams(
             collective_id=0, has_side_effects=True, vmem_limit_bytes=VMEM_LIMIT
         ),
@@ -537,305 +869,41 @@
     )(inputs, side, qk, vg, cotangent, out_weight, resets, scale, bias, gain)
 
 
-def add_into(target, index, *others):
-    total = target[index].astype(F32)
-    for ref, at in others:
-        total += ref[at].astype(F32)
-    target[index] = total.astype(BF16)
-
-
-def around(position):
-    return (
-        lax.rem(position + 1, SIDE),
-        lax.rem(position + SIDE - 1, SIDE),
-        lax.rem(position + 2, SIDE),
-    )
-
-
-def finish_kernel(
-    parts,
-    split_at,
-    x_ref,
-    delta_ref,
-    side_weight_ref,
-    qk_weight_ref,
-    vg_weight_ref,
-    hidden_ref,
-    out_weight_ref,
-    cotangent_ref,
-    mixed_ref,
-    grad_ref,
-    qk_ref,
-    vg_ref,
-    db_ref,
-    out_ref,
-    one,
-    two,
-    one_first,
-    two_first,
-    one_second,
-    two_second,
-    one_third,
-    two_third,
-    one_fourth,
-    two_fourth,
-    away,
-    kept,
-    core_in,
-    z_first,
-    z_second,
-    send_sem,
-    recv_sem,
-):
-    me = lax.axis_index("ctx")
-    mine = lax.axis_index("head")
-    x, y = me // SIDE, lax.rem(me, SIDE)
-    z, core = mine // 2, lax.rem(mine, 2)
-    x_up, x_down, x_far = around(x)
-    y_up, y_down, y_far = around(y)
-    z_up, z_down, z_far = around(z)
-    peers = [
-        {"ctx": x * SIDE + y_up},
-        {"ctx": x * SIDE + y_down},
-        {"ctx": x_up * SIDE + y},
-        {"ctx": x_down * SIDE + y},
-        {"head": z * 2 + 1 - core},
-        {"head": z_up * 2 + core},
-        {"head": z_down * 2 + core},
-    ]
-    barrier = pltpu.get_barrier_semaphore()
-    for peer in peers:
-        pl.semaphore_signal(barrier, inc=1, device_id=peer, device_id_type=MESH)
-    pl.semaphore_wait(barrier, len(peers))
-    y_next, y_prev, x_next, x_prev, pair, z_next, z_prev = peers
-    used = []
-
-    def send(src, dst, peer):
-        slot = len(used)
-        copy = pltpu.make_async_remote_copy(
-            src_ref=src,
-            dst_ref=dst,
-            send_sem=send_sem.at[slot],
-            recv_sem=recv_sem.at[slot],
-            device_id=peer,
-            device_id_type=MESH,
-        )
-        copy.start()
-        used.append(copy)
-        return copy
-
-    width = grad_ref.shape[1]
-    rows = qk_ref.shape[1]
-
-    def mixed_block(z_to, core_to, target):
-        at = pl.multiple_of((z_to * 2 + core_to) * width, width)
-        target[0, z_to] = dot(
-            hidden_ref[...], out_weight_ref[:, pl.ds(at, width)], NN
-        ).astype(BF16)
-
-    def grad_block(z_to, core_to, target):
-        at = pl.multiple_of((z_to * 2 + core_to) * width, width)
-        total = 0.0
-        start = 0
-        for ref in (qk_weight_ref, vg_weight_ref):
-            size = ref.shape[2]
-            for s in range(2):
-                total += dot(
-                    delta_ref[:, start : start + size], ref[s, pl.ds(at, width), :], NT
-                )
-                start += size
-        total += dot(delta_ref[:, start:], side_weight_ref[pl.ds(at, width), :], NT)
-        target[1, z_to] = total.astype(BF16)
-
-    def term_block(x_to, y_to):
-        at = pl.multiple_of((x_to * SIDE + y_to) * rows, rows)
-        term = dot(x_ref[:, pl.ds(at, rows)], delta_ref[...], TN).astype(BF16)
-        one[y_to, x_to] = term[:, :split_at]
-        rest = term.shape[1] - split_at
-        two[x_to, y_to, :, :rest] = term[:, split_at:]
-        two[x_to, y_to, :, rest:] = dot(
-            cotangent_ref[:, pl.ds(at, rows)], hidden_ref[...], TN
-        ).astype(BF16)
-
-    each(SIDE, lambda i: term_block(i, y_far))
-    one_a = send(one.at[y_far, pl.ds(0, 2)], one_first.at[0], y_next)
-    one_b = send(one.at[y_far, pl.ds(2, 2)], one_first.at[1], y_prev)
-    each(SIDE - 1, lambda i: term_block(x_far, lax.rem(y_far + 1 + i, SIDE)))
-    two_a = send(two.at[x_far, pl.ds(0, 2)], two_first.at[0], x_next)
-    two_b = send(two.at[x_far, pl.ds(2, 2)], two_first.at[1], x_prev)
-    each(SIDE, lambda i: mixed_block(i, 1 - core, away))
-    mixed_pair = send(away.at[0], core_in.at[0], pair)
-    each(
-        (SIDE - 1) * (SIDE - 1),
-        lambda i: term_block(
-            lax.rem(x_far + 1 + i // (SIDE - 1), SIDE),
-            lax.rem(y_far + 1 + lax.rem(i, SIDE - 1), SIDE),
-        ),
-    )
-    each(SIDE, lambda i: mixed_block(i, core, kept))
-
-    def second(store, first, second_in, ups, downs, up_peer, down_peer, a, b):
-        a.wait_recv()
-        each(2, lambda i: add_into(store, (ups, i), (first, (0, i))))
-        up = send(store.at[ups], second_in.at[0], up_peer)
-        b.wait_recv()
-        each(2, lambda i: add_into(store, (downs, 2 + i), (first, (1, i))))
-        down = send(store.at[downs], second_in.at[1], down_peer)
-        return up, down
-
-    one_c = second(one, one_first, one_second, y_up, y_down, y_next, y_prev, one_a, one_b)
-    two_c = second(two, two_first, two_second, x_up, x_down, x_next, x_prev, two_a, two_b)
-
-    half = grad_ref.shape[0] // 2
-
-    def z_start(k, arrived):
-        arrived.wait_recv()
-        add_into(kept, (k, z_far), (core_in, (k, z_far)))
-        a = send(kept.at[k, z_far, pl.ds(0, half)], z_first.at[k, 0], z_next)
-        b = send(kept.at[k, z_far, pl.ds(half, half)], z_first.at[k, 1], z_prev)
-        each(
-            SIDE - 1,
-            lambda i: add_into(
-                kept,
-                (k, lax.rem(z_far + 1 + i, SIDE)),
-                (core_in, (k, lax.rem(z_far + 1 + i, SIDE))),
-            ),
-        )
-        return a, b
-
-    def z_middle(k, pending):
-        a, b = pending
-        a.wait_recv()
-        add_into(kept, (k, z_up, pl.ds(0, half)), (z_first, (k, 0)))
-        up = send(kept.at[k, z_up], z_second.at[k, 0], z_next)
-        b.wait_recv()
-        add_into(kept, (k, z_down, pl.ds(half, half)), (z_first, (k, 1)))
-        down = send(kept.at[k, z_down], z_second.at[k, 1], z_prev)
-        return up, down
-
-    def z_end(k, pending, out_ref):
-        for copy in pending:
-            copy.wait_recv()
-        out_ref[...] = (
-            kept[k, z].astype(F32) + z_second[k, 0].astype(F32) + z_second[k, 1].astype(F32)
-        ).astype(BF16)
-
-    mixed_z = z_start(0, mixed_pair)
-    each(SIDE, lambda i: grad_block(i, 1 - core, away))
-    grad_pair = send(away.at[1], core_in.at[1], pair)
-    mixed_z = z_middle(0, mixed_z)
-    each(SIDE, lambda i: grad_block(i, core, kept))
-    grad_z = z_start(1, grad_pair)
-    z_end(0, mixed_z, mixed_ref)
-    grad_z = z_middle(1, grad_z)
-
-    def third(store, second_in, third_in, at, far, far_next, far_prev, pending):
-        for copy in pending:
-            copy.wait_recv()
-        add_into(store, (at, far), (second_in, (0, far)), (second_in, (1, far)))
-        n = rows // 2
-        a = send(store.at[at, far, pl.ds(0, n)], third_in.at[0], far_next)
-        b = send(store.at[at, far, pl.ds(n, n)], third_in.at[1], far_prev)
-        for i in range(1, SIDE):
-            other = lax.rem(far + i, SIDE)
-            add_into(store, (at, other), (second_in, (0, other)), (second_in, (1, other)))
-        return a, b
-
-    def fourth(store, third_in, fourth_in, at, ups, downs, up_peer, down_peer, pending):
-        a, b = pending
-        n = rows // 2
-        a.wait_recv()
-        add_into(store, (at, ups, pl.ds(0, n)), (third_in, 0))
-        up = send(store.at[at, ups], fourth_in.at[0], up_peer)
-        b.wait_recv()
-        add_into(store, (at, downs, pl.ds(n, n)), (third_in, 1))
-        down = send(store.at[at, downs], fourth_in.at[1], down_peer)
-        return up, down
-
-    two_d = third(two, two_second, two_third, x, y_far, y_next, y_prev, two_c)
-    one_d = third(one, one_second, one_third, y, x_far, x_next, x_prev, one_c)
-    two_e = fourth(two, two_third, two_fourth, x, y_up, y_down, y_next, y_prev, two_d)
-    one_e = fourth(one, one_third, one_fourth, y, x_up, x_down, x_next, x_prev, one_d)
-    z_end(1, grad_z, grad_ref)
-
-    def total(store, fourth_in, at, to, pending):
-        for copy in pending:
-            copy.wait_recv()
-        return (
-            store[at, to].astype(F32) + fourth_in[0].astype(F32) + fourth_in[1].astype(F32)
-        )
-
-    sums = (total(two, two_fourth, x, y, two_e), total(one, one_fourth, y, x, one_e))
-    for ref, s, start, size in parts:
-        if start < split_at:
-            ref_value = sums[1][:, start : start + size]
-        else:
-            ref_value = sums[0][:, start - split_at : start - split_at + size]
-        (qk_ref, vg_ref, db_ref)[ref][s] = ref_value
-    out_ref[...] = sums[0][:, -out_ref.shape[0] :].T
-    for copy in used:
-        copy.wait_send()
-
-
-def finish(inputs, delta, side, qk, vg, hidden, out_weight, cotangent):
-    tokens, width = inputs.shape
-    heads, key_heads = vg.shape[2] // DV, qk.shape[2] // DK
-    columns = delta.shape[1] + hidden.shape[1]
-    key_width, value_width = key_heads * DK, heads * DV
-    side_at = 2 * (key_width + value_width)
-    parts = [
-        (0, 0, 0, key_width),
-        (0, 1, key_width, key_width),
-        (1, 0, 2 * key_width, value_width),
-        (1, 1, 2 * key_width + value_width, value_width),
-        (2, 0, side_at, heads),
-        (2, 1, side_at + heads, heads),
-    ]
-    split_at = 2 * key_width + value_width
-    rows = width // (SIDE * SIDE)
-    block = width // (2 * SIDE)
-    sizes = (split_at, columns - split_at)
-    half = tokens // 2
-
-    def both(*shape):
-        return [pltpu.VMEM((*shape, n), BF16) for n in sizes]
-
+def place_kernel(mixed_in, grad_in, gate_in, out_in, one_in, two_in, *outs):
+    mixed, grad, qk, vg, db, out = outs
+    mixed[...] = mixed_in[...]
+    grad[...] = grad_in[...]
+    key_width, value_width, heads = qk.shape[2], vg.shape[2], db.shape[2]
+    extra = one_in.shape[1] - 2 * key_width
+    qk[0] = one_in[:, :key_width]
+    qk[1] = one_in[:, key_width : 2 * key_width]
+    vg[0, :, :extra] = one_in[:, 2 * key_width :]
+    vg[0, :, extra:] = two_in[:, : value_width - extra]
+    vg[1] = gate_in[...]
+    side_at = value_width - extra
+    db[0] = two_in[:, side_at : side_at + heads]
+    db[1] = two_in[:, side_at + heads : side_at + 2 * heads]
+    out[...] = out_in[...].T
+
+
+def place(results, qk, vg, db):
+    mixed, grad = results[:2]
+    rows = results[2].shape[0]
     vmem = pl.BlockSpec(memory_space=pltpu.VMEM)
     return pl.pallas_call(
-        functools.partial(finish_kernel, parts, split_at),
+        place_kernel,
         out_shape=[
-            jax.ShapeDtypeStruct((tokens, block), BF16),
-            jax.ShapeDtypeStruct((tokens, block), BF16),
-            jax.ShapeDtypeStruct((2, rows, key_width), F32),
-            jax.ShapeDtypeStruct((2, rows, value_width), F32),
-            jax.ShapeDtypeStruct((2, rows, heads), F32),
-            jax.ShapeDtypeStruct((value_width, rows), F32),
+            jax.ShapeDtypeStruct(mixed.shape, BF16),
+            jax.ShapeDtypeStruct(grad.shape, BF16),
+            jax.ShapeDtypeStruct((2, rows, qk.shape[2]), F32),
+            jax.ShapeDtypeStruct((2, rows, vg.shape[2]), F32),
+            jax.ShapeDtypeStruct((2, rows, db.shape[2]), F32),
+            jax.ShapeDtypeStruct((vg.shape[2], rows), F32),
         ],
-        in_specs=[vmem] * 8,
+        in_specs=[vmem] * 6,
         out_specs=[vmem] * 6,
-        scratch_shapes=[
-            *both(SIDE, SIDE, rows),
-            *both(2, 2, rows),
-            *both(2, SIDE, rows),
-            *both(2, rows // 2),
-            *both(2, rows),
-            pltpu.VMEM((2, SIDE, tokens, block), BF16),
-            pltpu.VMEM((2, SIDE, tokens, block), BF16),
-            pltpu.VMEM((2, SIDE, tokens, block), BF16),
-            pltpu.VMEM((2, 2, half, block), BF16),
-            pltpu.VMEM((2, 2, tokens, block), BF16),
-            pltpu.SemaphoreType.DMA((26,)),
-            pltpu.SemaphoreType.DMA((26,)),
-        ],
-        compiler_params=pltpu.CompilerParams(
-            collective_id=2, has_side_effects=True, vmem_limit_bytes=FINISH_LIMIT
-        ),
-        name="finish",
-    )(inputs, delta, side, qk, vg, hidden, out_weight, cotangent)
-
-
-FINISH_LIMIT = 56 * 2**20
-VMEM_LIMIT = 48 * 2**20
+        name="place",
+    )(*results)
 
 
 def body(
@@ -858,7 +926,7 @@
     resets = boundaries.astype(F32)[:, None]
     scale_row = jnp.pad(decay_scale, (0, LANES - heads))[None]
     bias_row = jnp.pad(beta_bias, (heads, LANES - 2 * heads))[None]
-    hidden, delta = mix(
+    results = mix(
         inputs,
         side,
         query_key_weight,
@@ -870,17 +938,7 @@
         bias_row,
         norm_gain[None],
     )
-    mixed, grad_inputs, grad_query_key, grad_value_gate, grad_decay_beta, grad_out_weight = finish(
-        inputs, delta, side, query_key_weight, value_gate_weight, hidden, out_weight, grad_mixed
-    )
-    return (
-        mixed,
-        grad_inputs,
-        grad_query_key,
-        grad_value_gate,
-        grad_decay_beta,
-        grad_out_weight,
-    )
+    return tuple(place(results, query_key_weight, value_gate_weight, decay_beta_weight))
 
 
 def solution(mesh):

time: 173 us -> 148 us (0.86)
  Pallas kernels: 155 us -> 141 us
  local copies, waits for them, and re-layouts: 15.5 us -> 5.61 us
    pallas_call x2, Pallas kernels: 155 us -> 141 us  [the longest x1 138 us: mix(): pl.pallas_call(kernel, out_shape=[jax.ShapeDtypeStruct((tokens, head_size...]
    unnamed x17 -> x0, local copies, waits for them, and re-layouts: 11.9 us -> none
where the time goes in v4:
time: 148 us
  Pallas kernels  141 us (95%)
  local copies, waits for them, and re-layouts  5.61 us (4%)
    pallas_call x1, Pallas kernels, mix(): pl.pallas_call(kernel, out_shape=[jax.ShapeDtypeStruct((tokens, head_size...  138 us

profile of v4, /device:TPU:0, one launch (start us, length us, event | category | flops | bytes accessed | tf_op | source)
XLA Modules:
  0.0 147.6 jit_solution(8216589914362415018)
XLA Ops:
  0.6 1.3 pad_bitcast_fusion
  1.9 0.7 convert_element_type.9
  2.6 0.7 slice_bitcast_fusion.1
  3.4 0.9 copy.24.refs_6_
  4.2 0.3 copy.23
  4.5 0.9 pad.12.refs_1_
  5.4 137.9 %mixer.1 = (bf16[512,256]{1,0:T(8,128)(2,1)}, bf16[512,256]{1,0:T(8,128)(2,1)}, f32[128,512]{1,0:T(8,128)}, f32[128,512]{1,0:T(8,128)}, f32[128,640]{1,0:T(8,128)}, /*index=5*/f32[128,512]{1,0:T(8,128)}) custom-call(bf16[512,2048]{1,0:T(8,128)(2,1)} %refs_0_.1, bf16[2048,128]{1,0:T(8,128)(2,1)} %pad.12.refs_1_, bf16[2,2048,256]{2,1,0:T(8,128)(2,1)} %refs_2_.1, ...), custom_call_target="tpu_custom_call" | custom-call | tf_op jit(solution)/shard_map/mixer/pallas_call | solution.py:855
  143.3 2.7 %place.1 = (bf16[512,256]{1,0:T(8,128)(2,1)}, bf16[512,256]{1,0:T(8,128)(2,1)}, f32[2,128,256]{2,1,0:T(8,128)}, f32[2,128,512]{2,1,0:T(8,128)}, f32[2,128,4]{2,1,0:T(8,128)}, /*index=5*/f32[512,128]{1,0:T(8,128)}) custom-call(bf16[512,256]{1,0:T(8,128)(2,1)} %get-tuple-element.12.mixed_in, bf16[512,256]{1,0:T(8,128)(2,1)} %get-tuple-element.13.grad_in, ...), custom_call_target="tpu_custom_call" | custom-call | tf_op jit(solution)/shard_map/place/pallas_call | solution.py:893
  146.0 1.6 %copy.25 = f32[2,128,4]{1,2,0:T(4,128)} copy(f32[2,128,4]{2,1,0:T(8,128)} %get-tuple-element.34) | data formatting | bytes 8192 | tf_op jit(solution)/shard_map/place/pallas_call | solution.py:893
  (1 shorter events, 0.0 us)

commit v5 on v4

--- a/solution.py
+++ b/solution.py
@@ -285,7 +285,7 @@
     key_heads,
     repeat,
     x_hbm,
-    side_hbm,
+    side_ref,
     qk_hbm,
     vg_hbm,
     cotangent_hbm,
@@ -355,7 +355,6 @@
         for i, (src, dst) in enumerate(
             [
                 (x_hbm, x_in),
-                (side_hbm, side_in),
                 (qk_hbm, qk_in),
                 (vg_hbm.at[0], vg_in.at[0]),
                 (vg_hbm.at[1], vg_in.at[1]),
@@ -364,7 +363,7 @@
             ]
         )
     ]
-    for load in loads:
+    for load in loads[:3]:
         load.start()
     x, y, row, col = ring_peers()
     mine = lax.axis_index("head")
@@ -381,8 +380,11 @@
         AxesSum(links, stores[1], buffers[1], on_x, on_y),
     ]
     late = [
-        AxesSum(links, stores[2], buffers[2], on_y, on_x),
-        AxesSum(links, stores[3], buffers[3], on_x, on_y),
+        [
+            AxesSum(links, stores[i], buffers[i], on_y, on_x),
+            AxesSum(links, stores[i + 1], buffers[i + 1], on_x, on_y),
+        ]
+        for i in (2, 4)
     ]
     block = mixed_ref.shape[1]
     part = stores[0].shape[2]
@@ -415,7 +417,7 @@
         total += dot(delta_ref[:, key_width:value_at], qk_in[1, at, :], NT)
         total += dot(delta_ref[:, value_at:gate_at], vg_in[0, at, :], NT)
         total += dot(delta_ref[:, gate_at:side_at], vg_in[1, at, :], NT)
-        total += dot(delta_ref[:, side_at:], side_in[at, :], NT)
+        total += dot(delta_ref[:, side_at:], side_in[:, at], NN)
         cotangent_in[:, at] = total.astype(BF16)
 
     def early_block(x_to, y_to):
@@ -423,13 +425,19 @@
         stores[0][y_to, x_to] = dot(x_in[:, at], delta_ref[:, gate_at:side_at], TN).astype(BF16)
         stores[1][x_to, y_to] = dot(cotangent_in[:, at], hidden_ref[...], TN).astype(BF16)
 
-    def late_block(x_to, y_to):
+    def key_block(x_to, y_to):
         at = pl.ds(pl.multiple_of((x_to * SIDE + y_to) * part, part), part)
-        cut = stores[2].shape[3]
-        term = dot(x_in[:, at], delta_ref[:, :gate_at], TN).astype(BF16)
-        stores[2][y_to, x_to] = term[:, :cut]
-        stores[3][x_to, y_to, :, : gate_at - cut] = term[:, cut:]
-        stores[3][x_to, y_to, :, gate_at - cut :] = dot(
+        term = dot(x_in[:, at], delta_ref[:, :value_at], TN).astype(BF16)
+        stores[2][y_to, x_to] = term[:, :key_width]
+        stores[3][x_to, y_to] = term[:, key_width:]
+
+    def value_block(x_to, y_to):
+        at = pl.ds(pl.multiple_of((x_to * SIDE + y_to) * part, part), part)
+        cut = stores[4].shape[3]
+        term = dot(x_in[:, at], delta_ref[:, value_at:gate_at], TN).astype(BF16)
+        stores[4][y_to, x_to] = term[:, :cut]
+        stores[5][x_to, y_to, :, : value_width - cut] = term[:, cut:]
+        stores[5][x_to, y_to, :, value_width - cut :] = dot(
             x_in[:, at], delta_ref[:, side_at:], TN
         ).astype(BF16)
 
@@ -459,8 +467,17 @@
     for h in range(heads):
         map_total[h] = eye
         add_total[h] = jnp.zeros_like(eye)
-    for load in loads[:4]:
+    side_in[...] = jnp.zeros_like(side_in)
+    side_in[: side_ref.shape[0], :] = side_ref[...]
+    lane = lax.broadcasted_iota(jnp.int32, (1, LANES), 1)
+    scale_row, bias_row = jnp.zeros((1, LANES), F32), jnp.zeros((1, LANES), F32)
+    for h in range(heads):
+        scale_row = jnp.where(lane == h, scale_ref[h], scale_row)
+        bias_row = jnp.where(lane == heads + h, bias_ref[h], bias_row)
+    for load in loads[:3]:
         load.wait()
+    for load in loads[3:]:
+        load.start()
 
     def make_terms(b):
         at = span(b)
@@ -468,10 +485,11 @@
         proj[at, :key_width] = dot(left, qk_in[0], NN)
         proj[at, key_width:value_at] = dot(left, qk_in[1], NN)
         proj[at, value_at:gate_at] = dot(left, vg_in[0], NN)
-        side = dot(left, side_in[...], NN)
+        side = dot(left, side_in[...], NT)
+        reset = jnp.broadcast_to(reset_ref[pl.ds(b, 1), :].astype(F32), (BLOCK, BLOCK)).T
         proj[at, gate_at:] = side
         beta, summed, flipped, same, start, end = gates(
-            side, reset_ref[at, :], scale_ref[...], bias_ref[...], heads
+            side, reset, scale_row, bias_row, heads
         )
         betas[b] = beta
         starts[b] = start
@@ -536,7 +554,7 @@
         row_buf[y, h, 1] = add_total[h].astype(BF16)
         row_copies.append(exchange(0, h, row_buf, y, (h,), row))
 
-    for load in loads[4:]:
+    for load in loads[3:]:
         load.wait()
 
     def make_local(b):
@@ -632,12 +650,12 @@
             k, _ = unit(proj[at, key_width + kh * DK : key_width + (kh + 1) * DK])
             for h in range(kh * repeat, (kh + 1) * repeat):
                 d_out = grad_out[b, h]
-                d_scores = mm3(d_out, value[b, h], NT) * decays[b, h]
-                early_dq[b, h] = mm3(d_scores, k) + starts[b][:, h : h + 1] * mm3(
+                d_scores = mm1(d_out, value[b, h], NT) * decays[b, h]
+                early_dq[b, h] = mm1(d_scores, k) + starts[b][:, h : h + 1] * mm1(
                     d_out, before[b, h], NT
                 )
-                early_dk[b, h] = mm3(d_scores, q, TN)
-                early_value[b, h] = mm3(scores[b, h], d_out, TN)
+                early_dk[b, h] = mm1(d_scores, q, TN)
+                early_value[b, h] = mm1(scores[b, h], d_out, TN)
 
     each(blocks, go_early)
     near_blocks(early_block)
@@ -693,17 +711,17 @@
                 s = before[b, h]
                 ds = state[h]
                 total = begin[BLOCK - 1 : BLOCK, :]
-                d_value = early_value[b, h] + finish_by * mm3(k, ds)
-                d_right = mm3(inverses[b, h], d_value, TN)
+                d_value = early_value[b, h] + finish_by * mm1(k, ds)
+                d_right = mm1(inverses[b, h], d_value, TN)
                 d_system = jnp.where(
-                    rows > cols, -mm3(d_right, value[b, h], NT) * decays[b, h], 0.0
+                    rows > cols, -mm1(d_right, value[b, h], NT) * decays[b, h], 0.0
                 )
-                row_part = mm3(d_system, k) - begin * mm3(d_right, s, NT)
-                last_part = finish_by * mm3(value[b, h], ds, NT)
-                dk_col = early_dk[b, h] + mm3(strength * d_system, k, TN) + last_part
+                row_part = mm1(d_system, k) - begin * mm1(d_right, s, NT)
+                last_part = finish_by * mm1(value[b, h], ds, NT)
+                dk_col = early_dk[b, h] + mm1(strength * d_system, k, TN) + last_part
                 dk_row = strength * row_part
                 dq = early_dq[b, h]
-                state[h] = total * ds + mm3(
+                state[h] = total * ds + mm1(
                     jnp.concatenate([begin * q, (strength * begin) * k], axis=0),
                     jnp.concatenate([grad_out[b, h], -d_right], axis=0),
                     TN,
@@ -726,7 +744,7 @@
         d_decay = exact(lower, d_summed, TN)
         side = proj[at, gate_at:]
         d_side = (
-            d_decay * (-scale_ref[...]) * jax.nn.sigmoid(side)
+            d_decay * (-scale_row) * jax.nn.sigmoid(side)
             + d_strength * beta * (1.0 - beta)
         )
         delta_ref[at, side_at:] = d_side.astype(BF16)
@@ -735,29 +753,37 @@
 
     for reduction in early:
         reduction.third()
-    far_blocks(late_block)
-    for reduction in late:
-        reduction.start()
+    for make, pieces in zip((key_block, value_block), late):
+        far_blocks(make)
+        for reduction in pieces:
+            reduction.start()
     mixed_sum.middle()
-    near_blocks(late_block)
+    near_blocks(key_block)
+    for reduction in early:
+        reduction.fourth()
+    for reduction in late[0]:
+        reduction.second()
+    near_blocks(value_block)
     each(SIDE, lambda i: grad_block(i, 1 - core))
     grad_sum.swap()
-    for reduction in early:
-        reduction.fourth()
-    for reduction in late:
+    for reduction in late[1]:
         reduction.second()
     each(SIDE, lambda i: grad_block(i, core))
     grad_sum.start()
+    for reduction in late[0]:
+        reduction.third()
     mixed_ref[...] = mixed_sum.total().astype(BF16)
     for reduction, ref in zip(early, sum_refs[:2]):
         ref[...] = reduction.total()
     grad_sum.middle()
-    for reduction in late[::-1]:
+    for reduction in late[0]:
+        reduction.fourth()
+    for reduction in late[1][::-1]:
         reduction.third()
-    for reduction in late[::-1]:
+    grad_ref[...] = grad_sum.total().astype(BF16)
+    for reduction in late[1][::-1]:
         reduction.fourth()
-    grad_ref[...] = grad_sum.total().astype(BF16)
-    for reduction, ref in zip(late[::-1], sum_refs[:1:-1]):
+    for reduction, ref in zip(late[0] + late[1], sum_refs[2:]):
         ref[...] = reduction.total()
     for copy in links.used:
         copy.wait_send()
@@ -777,7 +803,7 @@
 
 
 VMEM_LIMIT = 63 * 2**20
-LINKS = 48
+LINKS = 64
 
 
 def mix(inputs, side, qk, vg, cotangent, out_weight, resets, scale, bias, gain):
@@ -787,10 +813,11 @@
     blocks = tokens // BLOCK
     columns = 2 * (key_width + value_width) + LANES
     rows = width // (SIDE * SIDE)
-    cut = 2 * key_width + LANES
-    sizes = (value_width, value_width, cut, 2 * key_width + value_width + LANES - cut)
+    cut = value_width - LANES
+    sizes = (value_width, value_width, key_width, key_width, cut, 2 * LANES)
     head_size = width // (2 * SIDE)
     hbm, vmem = pl.BlockSpec(memory_space=pl.ANY), pl.BlockSpec(memory_space=pltpu.VMEM)
+    smem = pl.BlockSpec(memory_space=pltpu.SMEM)
     square = pltpu.VMEM((blocks, heads, BLOCK, BLOCK), F32)
     lanes = pltpu.VMEM((blocks, BLOCK, LANES), F32)
     one = pltpu.VMEM((heads, DK, DV), F32)
@@ -816,7 +843,7 @@
         pltpu.VMEM((tokens, value_width), BF16),
         pltpu.VMEM((tokens, columns), BF16),
         pltpu.VMEM(inputs.shape, BF16),
-        pltpu.VMEM(side.shape, BF16),
+        pltpu.VMEM((LANES, width), BF16),
         pltpu.VMEM(qk.shape, BF16),
         pltpu.VMEM(vg.shape, BF16),
         pltpu.VMEM(cotangent.shape, BF16),
@@ -836,19 +863,19 @@
         head_store,
         head_store,
         head_buffers,
-        pltpu.SemaphoreType.DMA((7,)),
+        pltpu.SemaphoreType.DMA((6,)),
         *[pltpu.SemaphoreType.DMA((4, heads, SIDE - 1))] * 2,
         *[pltpu.SemaphoreType.DMA((LINKS,))] * 2,
     ]
     flat, tree = jax.tree.flatten(scratch)
 
     def kernel(*refs):
-        fixed, rest = refs[:16], refs[16:]
+        fixed, rest = refs[:18], refs[18:]
         mixer_kernel(
             key_heads,
             heads // key_heads,
             *fixed[:12],
-            fixed[12:16],
+            fixed[12:18],
             *jax.tree.unflatten(tree, rest),
         )
 
@@ -859,8 +886,8 @@
             jax.ShapeDtypeStruct((tokens, head_size), BF16),
             *[jax.ShapeDtypeStruct((rows, n), F32) for n in sizes],
         ],
-        in_specs=[hbm] * 6 + [vmem] * 4,
-        out_specs=[vmem] * 6,
+        in_specs=[hbm, vmem] + [hbm] * 4 + [vmem, smem, smem, vmem],
+        out_specs=[vmem] * 8,
         scratch_shapes=flat,
         compiler_params=pltpu.CompilerParams(
             collective_id=0, has_side_effects=True, vmem_limit_bytes=VMEM_LIMIT
@@ -869,20 +896,21 @@
     )(inputs, side, qk, vg, cotangent, out_weight, resets, scale, bias, gain)
 
 
-def place_kernel(mixed_in, grad_in, gate_in, out_in, one_in, two_in, *outs):
+def place_kernel(
+    mixed_in, grad_in, gate_in, out_in, query_in, key_in, value_in, rest_in, *outs
+):
     mixed, grad, qk, vg, db, out = outs
     mixed[...] = mixed_in[...]
     grad[...] = grad_in[...]
-    key_width, value_width, heads = qk.shape[2], vg.shape[2], db.shape[2]
-    extra = one_in.shape[1] - 2 * key_width
-    qk[0] = one_in[:, :key_width]
-    qk[1] = one_in[:, key_width : 2 * key_width]
-    vg[0, :, :extra] = one_in[:, 2 * key_width :]
-    vg[0, :, extra:] = two_in[:, : value_width - extra]
+    heads, cut = db.shape[1], value_in.shape[1]
+    qk[0] = query_in[...]
+    qk[1] = key_in[...]
+    vg[0, :, :cut] = value_in[...]
+    vg[0, :, cut:] = rest_in[:, :LANES]
     vg[1] = gate_in[...]
-    side_at = value_width - extra
-    db[0] = two_in[:, side_at : side_at + heads]
-    db[1] = two_in[:, side_at + heads : side_at + 2 * heads]
+    side = rest_in[:, LANES:].T
+    db[0] = side[:heads]
+    db[1] = side[heads : 2 * heads]
     out[...] = out_in[...].T
 
 
@@ -897,10 +925,10 @@
             jax.ShapeDtypeStruct(grad.shape, BF16),
             jax.ShapeDtypeStruct((2, rows, qk.shape[2]), F32),
             jax.ShapeDtypeStruct((2, rows, vg.shape[2]), F32),
-            jax.ShapeDtypeStruct((2, rows, db.shape[2]), F32),
+            jax.ShapeDtypeStruct((2, db.shape[2], rows), F32),
             jax.ShapeDtypeStruct((vg.shape[2], rows), F32),
         ],
-        in_specs=[vmem] * 6,
+        in_specs=[vmem] * 8,
         out_specs=[vmem] * 6,
         name="place",
     )(*results)
@@ -919,26 +947,30 @@
     grad_mixed,
 ):
     heads = beta_bias.shape[0]
-    side = jnp.pad(
-        jnp.concatenate([decay_beta_weight[0], decay_beta_weight[1]], axis=1),
-        ((0, 0), (0, LANES - 2 * heads)),
-    )
-    resets = boundaries.astype(F32)[:, None]
-    scale_row = jnp.pad(decay_scale, (0, LANES - heads))[None]
-    bias_row = jnp.pad(beta_bias, (heads, LANES - 2 * heads))[None]
+    side = jnp.swapaxes(decay_beta_weight, 1, 2).reshape(2 * heads, -1)
     results = mix(
         inputs,
-        side,
+        jnp.pad(side, ((0, 2 * heads), (0, 0))),
         query_key_weight,
         value_gate_weight,
         grad_mixed,
         out_weight,
-        resets,
-        scale_row,
-        bias_row,
+        boundaries.reshape(-1, BLOCK),
+        decay_scale,
+        beta_bias,
         norm_gain[None],
     )
-    return tuple(place(results, query_key_weight, value_gate_weight, decay_beta_weight))
+    mixed, grad_inputs, grad_query_key, grad_value_gate, grad_decay_beta, grad_out_weight = place(
+        results, query_key_weight, value_gate_weight, decay_beta_weight
+    )
+    return (
+        mixed,
+        grad_inputs,
+        grad_query_key,
+        grad_value_gate,
+        jnp.swapaxes(grad_decay_beta, 1, 2),
+        grad_out_weight,
+    )
 
 
 def solution(mesh):

time: 148 us -> 136 us (0.919)
  Pallas kernels: 141 us -> 133 us
  local copies, waits for them, and re-layouts: 5.61 us -> 1.41 us
    pallas_call x1, Pallas kernels: 138 us -> 131 us  [mix(): pl.pallas_call(kernel, out_shape=[jax.ShapeDtypeStruct((tokens, head_size...]
    broadcast_in_dim x2 -> x0, local copies, waits for them, and re-layouts: 2.12 us -> none  [the longest x1 1.26 us: body(): bias_row = jnp.pad(beta_bias, (heads, LANES - 2 * heads))[None]]
    pallas_call x1 -> x0, local copies, waits for them, and re-layouts: 1.58 us -> none  [place(): pl.pallas_call(place_kernel, out_shape=[jax.ShapeDtypeStruct(mixed.shape,...]
where the time goes in v5:
time: 136 us; the launch traced here: 135 us
  Pallas kernels  133 us (98%)
  local copies, waits for them, and re-layouts  1.41 us (1%)
    pallas_call x1, Pallas kernels, mix(): pl.pallas_call(kernel, out_shape=[jax.ShapeDtypeStruct((tokens, head_size...  131 us

profile of v5, /device:TPU:0, one launch (start us, length us, event | category | flops | bytes accessed | tf_op | source)
XLA Modules:
  0.0 135.4 jit_solution(16975929286742711235)
XLA Ops:
  0.6 0.8 reshape.18
  1.4 0.6 pad.4.refs_1_
  2.0 130.7 %mixer.1 = (bf16[512,256]{1,0:T(8,128)(2,1)}, bf16[512,256]{1,0:T(8,128)(2,1)}, f32[128,512]{1,0:T(8,128)}, f32[128,512]{1,0:T(8,128)}, f32[128,256]{1,0:T(8,128...) custom-call(bf16[512,2048]{1,0:T(8,128)(2,1)} %refs_0_.1, bf16[16,2048]{1,0:T(8,128)(2,1)} %pad.4.refs_1_, ...), custom_call_target="tpu_custom_call" | custom-call | tf_op jit(solution)/shard_map/mixer/pallas_call | solution.py:882
  132.8 2.6 %place.1 = (bf16[512,256]{1,0:T(8,128)(2,1)}, bf16[512,256]{1,0:T(8,128)(2,1)}, f32[2,128,256]{2,1,0:T(8,128)}, f32[2,128,512]{2,1,0:T(8,128)}, f32[2,4,128]{2,1,0:T(4,128)}, /*index=5*/f32[512,128]{1,0:T(8,128)}) custom-call(bf16[512,256]{1,0:T(8,128)(2,1)} %get-tuple-element.20.mixed_in, bf16[512,256]{1,0:T(8,128)(2,1)} %get-tuple-element.21.grad_in, ...), custom_call_target="tpu_custom_call" | custom-call | tf_op jit(solution)/shard_map/place/pallas_call | solution.py:921

commit v6 on v5

--- a/solution.py
+++ b/solution.py
@@ -108,7 +108,10 @@
     barrier = pltpu.get_barrier_semaphore()
     for peer in peers:
         pl.semaphore_signal(barrier, inc=1, device_id=peer, device_id_type=MESH)
-    pl.semaphore_wait(barrier, len(peers))
+
+
+def met(count):
+    pl.semaphore_wait(pltpu.get_barrier_semaphore(), count)
 
 
 def ring_peers():
@@ -311,6 +314,8 @@
     betas,
     starts,
     ends,
+    sums,
+    flips,
     decays,
     inverses,
     scores,
@@ -370,7 +375,8 @@
     z, core = mine // 2, lax.rem(mine, 2)
     z_up, z_down, _ = around(z)
     pair, z_next, z_prev = z * 2 + 1 - core, z_up * 2 + core, z_down * 2 + core
-    greet([{"ctx": peer} for peer in row + col] + [{"head": p} for p in (pair, z_next, z_prev)])
+    peers = [{"ctx": peer} for peer in row + col] + [{"head": p} for p in (pair, z_next, z_prev)]
+    greet(peers)
 
     links = Links(link_send_sem, link_recv_sem)
     on_y = (y, {"ctx": row[0]}, {"ctx": row[SIDE - 2]})
@@ -479,58 +485,6 @@
     for load in loads[3:]:
         load.start()
 
-    def make_terms(b):
-        at = span(b)
-        left = x_in[at, :]
-        proj[at, :key_width] = dot(left, qk_in[0], NN)
-        proj[at, key_width:value_at] = dot(left, qk_in[1], NN)
-        proj[at, value_at:gate_at] = dot(left, vg_in[0], NN)
-        side = dot(left, side_in[...], NT)
-        reset = jnp.broadcast_to(reset_ref[pl.ds(b, 1), :].astype(F32), (BLOCK, BLOCK)).T
-        proj[at, gate_at:] = side
-        beta, summed, flipped, same, start, end = gates(
-            side, reset, scale_row, bias_row, heads
-        )
-        betas[b] = beta
-        starts[b] = start
-        ends[b] = end
-        systems, keys = [], []
-        for kh in range(key_heads):
-            q, _ = unit(proj[at, kh * DK : (kh + 1) * DK])
-            q = q * DK ** (-0.5)
-            k, _ = unit(proj[at, key_width + kh * DK : key_width + (kh + 1) * DK])
-            gram = mm3(k, k, NT)
-            cross = mm3(q, k, NT)
-            for h in range(kh * repeat, (kh + 1) * repeat):
-                decay = pair_decay(summed, flipped, same, h)
-                strength = beta[:, heads + h : heads + h + 1]
-                systems.append(jnp.where(rows > cols, strength * decay * gram, 0.0))
-                decays[b, h] = decay
-                scores[b, h] = decay * cross
-                start_map[b, h] = start[:, h : h + 1] * q
-                keys.append(k)
-        solved_by = invert(systems)
-        for h in range(heads):
-            strength = beta[:, heads + h : heads + h + 1]
-            begin = start[:, h : h + 1]
-            v = proj[at, head_cols(h, value_at)]
-            right = jnp.concatenate([strength * v, (strength * begin) * keys[h]], axis=1)
-            solved = mm3(solved_by[h], right)
-            state_map = mm3(end[:, h : h + 1] * keys[h], solved, TN)
-            a = begin[BLOCK - 1 : BLOCK, :] * eye - state_map[:, DV:]
-            add = state_map[:, :DV]
-            inverses[b, h] = solved_by[h]
-            base[b, h] = solved[:, :DV]
-            weight[b, h] = solved[:, DV:]
-            step_map[b, h] = a
-            step_add[b, h] = add
-            prefix[b, h] = map_total[h]
-            both = mm3(a, jnp.concatenate([map_total[h], add_total[h]], axis=1))
-            map_total[h] = both[:, :DK]
-            add_total[h] = both[:, DK:] + add
-
-    each(blocks, make_terms)
-
     def exchange(phase, h, buffer, slot, at, peers):
         copies = [
             pltpu.make_async_remote_copy(
@@ -547,12 +501,69 @@
             copy.start()
         return copies
 
-    sent = []
+    def prepare(b):
+        at = span(b)
+        left = x_in[at, :]
+        proj[at, :key_width] = dot(left, qk_in[0], NN)
+        proj[at, key_width:value_at] = dot(left, qk_in[1], NN)
+        proj[at, value_at:gate_at] = dot(left, vg_in[0], NN)
+        side = dot(left, side_in[...], NT)
+        reset = jnp.broadcast_to(reset_ref[pl.ds(b, 1), :].astype(F32), (BLOCK, BLOCK)).T
+        proj[at, gate_at:] = side
+        betas[b], sums[b], flips[b], _, starts[b], ends[b] = gates(
+            side, reset, scale_row, bias_row, heads
+        )
+
+    each(blocks, prepare)
+
+    def make_terms(kh, group):
+        systems, items = [], []
+        for b in group:
+            at = span(b)
+            beta, summed, flipped, start = betas[b], sums[b], flips[b], starts[b]
+            doc, doc_row = summed[:, 2 * heads : 2 * heads + 1], flipped[2 * heads : 2 * heads + 1]
+            same = (doc == doc_row) & (rows >= cols)
+            q, _ = unit(proj[at, kh * DK : (kh + 1) * DK])
+            q = q * DK ** (-0.5)
+            k, _ = unit(proj[at, key_width + kh * DK : key_width + (kh + 1) * DK])
+            gram = mm3(k, k, NT)
+            cross = mm3(q, k, NT)
+            for h in range(kh * repeat, (kh + 1) * repeat):
+                decay = pair_decay(summed, flipped, same, h)
+                strength = beta[:, heads + h : heads + h + 1]
+                systems.append(jnp.where(rows > cols, strength * decay * gram, 0.0))
+                decays[b, h] = decay
+                scores[b, h] = decay * cross
+                start_map[b, h] = start[:, h : h + 1] * q
+                items.append((b, h, k))
+        for (b, h, k), solve in zip(items, invert(systems)):
+            strength = betas[b][:, heads + h : heads + h + 1]
+            begin = starts[b][:, h : h + 1]
+            v = proj[span(b), head_cols(h, value_at)]
+            right = jnp.concatenate([strength * v, (strength * begin) * k], axis=1)
+            solved = mm3(solve, right)
+            state_map = mm3(ends[b][:, h : h + 1] * k, solved, TN)
+            a = begin[BLOCK - 1 : BLOCK, :] * eye - state_map[:, DV:]
+            add = state_map[:, :DV]
+            inverses[b, h] = solve
+            base[b, h] = solved[:, :DV]
+            weight[b, h] = solved[:, DV:]
+            step_map[b, h] = a
+            step_add[b, h] = add
+            prefix[b, h] = map_total[h]
+            both = mm3(a, jnp.concatenate([map_total[h], add_total[h]], axis=1))
+            map_total[h] = both[:, :DK]
+            add_total[h] = both[:, DK:] + add
+
     row_copies, col_copies = [], []
-    for h in range(heads):
-        row_buf[y, h, 0] = map_total[h].astype(BF16)
-        row_buf[y, h, 1] = add_total[h].astype(BF16)
-        row_copies.append(exchange(0, h, row_buf, y, (h,), row))
+    for kh in range(key_heads):
+        each(blocks // 2, lambda i, kh=kh: make_terms(kh, (2 * i, 2 * i + 1)))
+        if kh == 0:
+            met(len(peers))
+        for h in range(kh * repeat, (kh + 1) * repeat):
+            row_buf[y, h, 0] = map_total[h].astype(BF16)
+            row_buf[y, h, 1] = add_total[h].astype(BF16)
+            row_copies.append(exchange(0, h, row_buf, y, (h,), row))
 
     for load in loads[3:]:
         load.wait()
@@ -562,7 +573,7 @@
         gate[at, :] = dot(x_in[at, :], vg_in[1], NN)
         up[at, :] = dot(cotangent_in[at, :], out_in[...], NT)
         for h in range(heads):
-            local = mm3(
+            local = mm1(
                 scores[b, h], jnp.concatenate([base[b, h], weight[b, h]], axis=1)
             )
             local_out[b, h] = local[:, :DV]
@@ -626,8 +637,8 @@
                 d_normed - normed * jnp.mean(d_normed * normed, axis=-1, keepdims=True)
             )
             grad_out[b, h] = d_out
-            local = mm3(start_map[b, h], d_out, TN)
-            add_total[h] += mm3(prefix[b, h], local, TN)
+            local = mm1(start_map[b, h], d_out, TN)
+            add_total[h] += mm1(prefix[b, h], local, TN)
 
     each(blocks, go_forward)
 
@@ -851,9 +862,7 @@
         pltpu.VMEM((tokens, 2 * key_width + value_width + LANES), F32),
         pltpu.VMEM((tokens, value_width), F32),
         pltpu.VMEM((tokens, value_width), F32),
-        lanes,
-        lanes,
-        lanes,
+        *[lanes] * 5,
         *[square] * 12,
         *[one] * 3,
         *[pltpu.VMEM((SIDE, heads, 2, DK, DV), BF16)] * 2,

time: 136 us -> 135 us (level)
  no operation moved by 1% of the time
where the time goes in v6:
time: 135 us; the launch traced here: 134 us
  Pallas kernels  132 us (98%)
  local copies, waits for them, and re-layouts  1.41 us (1%)
    pallas_call x1, Pallas kernels, mix(): pl.pallas_call(kernel, out_shape=[jax.ShapeDtypeStruct((tokens, head_size...  130 us

profile of v6, /device:TPU:0, one launch (start us, length us, event | category | flops | bytes accessed | tf_op | source)
XLA Modules:
  0.0 134.4 jit_solution(7705104791579168713)
XLA Ops:
  0.6 0.8 reshape.18
  1.4 0.6 pad.4.refs_1_
  2.0 129.7 %mixer.1 = (bf16[512,256]{1,0:T(8,128)(2,1)}, bf16[512,256]{1,0:T(8,128)(2,1)}, f32[128,512]{1,0:T(8,128)}, f32[128,512]{1,0:T(8,128)}, f32[128,256]{1,0:T(8,128...) custom-call(bf16[512,2048]{1,0:T(8,128)(2,1)} %refs_0_.1, bf16[16,2048]{1,0:T(8,128)(2,1)} %pad.4.refs_1_, ...), custom_call_target="tpu_custom_call" | custom-call | tf_op jit(solution)/shard_map/mixer/pallas_call | solution.py:891
  131.8 2.6 %place.1 = (bf16[512,256]{1,0:T(8,128)(2,1)}, bf16[512,256]{1,0:T(8,128)(2,1)}, f32[2,128,256]{2,1,0:T(8,128)}, f32[2,128,512]{2,1,0:T(8,128)}, f32[2,4,128]{2,1,0:T(4,128)}, /*index=5*/f32[512,128]{1,0:T(8,128)}) custom-call(bf16[512,256]{1,0:T(8,128)(2,1)} %get-tuple-element.20.mixed_in, bf16[512,256]{1,0:T(8,128)(2,1)} %get-tuple-element.21.grad_in, ...), custom_call_target="tpu_custom_call" | custom-call | tf_op jit(solution)/shard_map/place/pallas_call | solution.py:930
